TPU v7x, 128 devices: a whole 4x4x4 slice. The times are simulated.
128 devices in a mesh: layer: 4 (over y_hi, core), tensor: 32 (over z, x, y_lo).
Axes of the slice: x: 4, y: 4 (y_hi: 2, y_lo: 2; y = y_hi * 2 + y_lo), z: 4, core: 2. Of those that a mesh axis runs over, the one named last changes fastest.
Arguments:
- weight_slab: bfloat16 [32768, 8192], P(('layer', 'tensor')), parts along dimension 0, may hold values from -0.0625 to 0.0625
- token_rows: bfloat16 [4096, 8192], P(('layer', 'tensor')), parts along dimension 0, may hold values from -6 to 6
- skew_params: float32 [24, 64, 128, 128], P('layer', 'tensor'), parts along dimension 0, may hold values from -0.2 to 0.2
- pairing: int32 [24, 128], P('layer'), parts along dimension 0, may hold values from 0 to 127, each once within a row
Outputs:
- projected: bfloat16 [4096, 8192], P(('layer', 'tensor')), parts along dimension 0
There are 4 independent parts, one for each index of `layer`. A program takes and returns all parts, laid end to end along the dimension named above; each array names one. Nothing has to cross between parts.
Inputs may be any that keep to these rules, and one draw needn't show every extreme that they name: Each row of pairing is a permutation of 0 to 127.
All inputs are finite; a program needn't handle non-finite values.
Results may differ from a plain program's by a relative error of at most 0.025.
Values may be sent and summed in bfloat16 or wider, within the bound.
A program may use at most 128 MiB of HBM per device.

v0:
```python
import jax
import jax.numpy as jnp
import numpy as np
from jax import lax
from jax.sharding import PartitionSpec as P

section_bits = (0, 2, 3, 4, 5, 6)


def from_partner(block, axis, distance):
    count = lax.axis_size(axis)
    route = []
    for low in range(count):
        high = low | 1 << distance
        if high != low and high < count:
            route += [(low, high), (high, low)]
    return lax.ppermute(block, axis, route)


def pair_table(distance, count):
    stride = 1 << distance
    groups = count // (2 * stride)
    lookup = np.zeros((groups, stride), np.int32)
    for group_idx in range(groups):
        lower_half = group_idx * 2 * stride
        member = lower_half if lower_half >> 1 & 1 == 0 else lower_half + stride
        lookup[group_idx, 0] = (member >> 2) * 2 + (member & 1)
    return lookup


def chol_solve(factor, target):
    first = lax.linalg.triangular_solve(factor, target, left_side=True, lower=True)
    return lax.linalg.triangular_solve(factor, first, left_side=True, lower=True, transpose_a=True)


def cayley_blocks(skew_part, order_row):
    block_len = skew_part.shape[-1]
    identity = jnp.eye(block_len, dtype=jnp.float32)
    chosen = (order_row[:, None] == jnp.arange(block_len, dtype=jnp.int32)[None, :]).astype(
        jnp.float32
    )

    def one_block(params):
        skewed = params - params.T
        square = jnp.dot(skewed, skewed, precision=lax.Precision.HIGHEST)
        factor = jnp.linalg.cholesky(identity - square)
        raised = identity + skewed
        rotation = chol_solve(factor, jnp.dot(raised, raised, precision=lax.Precision.HIGHEST))
        inner = jnp.dot(rotation, chosen, precision=lax.Precision.HIGHEST)
        return jnp.dot(chosen.T, inner, precision=lax.Precision.HIGHEST)

    return lax.map(one_block, skew_part).astype(jnp.bfloat16)


def shards(weight_slab, token_rows, skew_params, pairing):
    block_len = skew_params.shape[-1]
    half_len = block_len // 2
    cols_total = weight_slab.shape[1]
    count = weight_slab.shape[0] // half_len
    local_bits = count.bit_length() - 1
    my_index = lax.axis_index("tensor")
    features = lax.all_to_all(token_rows, "tensor", split_axis=1, concat_axis=0, tiled=True)
    current = weight_slab
    for section_idx in range(len(section_bits)):
        distance = section_bits[section_idx]
        rotations = cayley_blocks(skew_params[section_idx], pairing[section_idx])
        if distance < local_bits:
            lookup = pair_table(distance, count)
            picked = rotations[lookup.reshape(-1)]
            groups = count >> distance + 1
            stride = 1 << distance
            grouped = current.reshape(groups, 2, stride, half_len, cols_total)
            joined = jnp.concatenate([grouped[:, 0], grouped[:, 1]], axis=2).reshape(
                groups * stride, block_len, cols_total
            )
            rotated = jnp.einsum(
                "kij,kjn->kin", picked, joined, preferred_element_type=jnp.float32
            ).astype(jnp.bfloat16)
            rotated = rotated.reshape(groups, stride, 2, half_len, cols_total)
            current = jnp.stack([rotated[:, :, 0], rotated[:, :, 1]], axis=1).reshape(
                -1, cols_total
            )
        else:
            partner_bit = distance - local_bits
            is_upper = my_index >> partner_bit & 1
            split_rows = current.reshape(count // 4, 2, 2, half_len, cols_total)
            kept = lax.dynamic_index_in_dim(split_rows, is_upper, 1, keepdims=False)
            outgoing = lax.dynamic_index_in_dim(split_rows, 1 - is_upper, 1, keepdims=False)
            received = from_partner(outgoing, "tensor", partner_bit)
            owned_rot = rotations.reshape(count // 4, 2, block_len, block_len)
            coef_kept = lax.dynamic_slice_in_dim(owned_rot, is_upper * half_len, half_len, 3)
            coef_recv = lax.dynamic_slice_in_dim(owned_rot, (1 - is_upper) * half_len, half_len, 3)
            summed = jnp.einsum(
                "qrab,qrbn->qran", coef_kept, kept, preferred_element_type=jnp.float32
            )
            summed = summed + jnp.einsum(
                "qrab,qrbn->qran", coef_recv, received, preferred_element_type=jnp.float32
            )
            rotated = summed.astype(jnp.bfloat16)
            mine_new = lax.dynamic_slice_in_dim(rotated, is_upper * half_len, half_len, 2)
            give_back = lax.dynamic_slice_in_dim(rotated, (1 - is_upper) * half_len, half_len, 2)
            returned = from_partner(give_back, "tensor", partner_bit)
            first_slot = jnp.where(is_upper == 0, mine_new, returned)
            second_slot = jnp.where(is_upper == 0, returned, mine_new)
            current = jnp.stack([first_slot, second_slot], axis=1).reshape(-1, cols_total)
    return lax.psum_scatter(
        jnp.dot(features, current, preferred_element_type=jnp.float32).astype(jnp.bfloat16),
        "tensor",
        scatter_dimension=0,
        tiled=True,
    )


def solution(mesh):
    in_specs = (
        P(("layer", "tensor"), None),
        P(("layer", "tensor"), None),
        P("layer", "tensor", None, None),
        P("layer", None),
    )
    out_specs = P(("layer", "tensor"), None)
    return jax.shard_map(shards, mesh=mesh, in_specs=in_specs, out_specs=out_specs, check_vma=False)
```

profile of v0, /device:TPU:16, one launch (start us, length us, event | category | flops | bytes accessed | tf_op | source)
XLA Modules:
  0.0 1025.6 jit_solution(17080041249334460365)
XLA Ops:
  8.7 49.5 %while.77 = (s32[]{:T(128)}, bf16[2,128,128]{1,2,0:T(8,128)(2,1)S(1)}, f32[2,128,128]{2,1,0:T(8,128)S(1)}, s32[128]{0:T(128)S(1)}, s32[]{:T(128)}) while((s32[]{:T(128)}, bf16[2,128,128]{1,2,0:T(8,128)(2,1)S(1)}, f32[2,128,128]{2,1,0:T(8,128)S(1)}, s32[128]{0:T(128)S(1)}, s32[]{:T(128)}) %tuple.139), condition=%wide.region_13.17_spmd.clone.clone, body=%wide.region_12.16_spmd.clone.clone.sunk | while | flops 151339136 | bytes 1837143 | solution.py:52
  9.5 11.7 %cholesky.401 = f32[128,128]{1,0:T(8,128)S(1)} custom-call(f32[128,128]{1,0:T(8,128)S(1)} %fusion.394), custom_call_target="Cholesky" | custom-call | tf_op jit(solution)/shard_map/while/body/eval_jaxpr/jit(cholesky)/cholesky | solution.py:46
  22.6 9.8 custom-call.43
  34.3 11.7 %cholesky.401 = f32[128,128]{1,0:T(8,128)S(1)} custom-call(f32[128,128]{1,0:T(8,128)S(1)} %fusion.394), custom_call_target="Cholesky" | custom-call | tf_op jit(solution)/shard_map/while/body/eval_jaxpr/jit(cholesky)/cholesky | solution.py:46
  47.3 9.8 custom-call.43
  71.8 49.6 %while.76 = (s32[]{:T(128)}, bf16[2,128,128]{1,2,0:T(8,128)(2,1)S(1)}, f32[2,128,128]{2,1,0:T(8,128)S(1)}, s32[128]{0:T(128)S(1)}, s32[]{:T(128)}) while((s32[]{:T(128)}, bf16[2,128,128]{1,2,0:T(8,128)(2,1)S(1)}, f32[2,128,128]{2,1,0:T(8,128)S(1)}, s32[128]{0:T(128)S(1)}, s32[]{:T(128)}) %tuple.142), condition=%wide.region_11.15_spmd.clone.clone, body=%wide.region_10.14_spmd.clone.clone.sunk | while | flops 151339136 | bytes 1837143 | solution.py:52
  72.6 11.7 %cholesky.389 = f32[128,128]{1,0:T(8,128)S(1)} custom-call(f32[128,128]{1,0:T(8,128)S(1)} %fusion.379), custom_call_target="Cholesky" | custom-call | tf_op jit(solution)/shard_map/while/body/eval_jaxpr/jit(cholesky)/cholesky | solution.py:46
  85.7 9.8 custom-call.42
  97.4 11.7 %cholesky.389 = f32[128,128]{1,0:T(8,128)S(1)} custom-call(f32[128,128]{1,0:T(8,128)S(1)} %fusion.379), custom_call_target="Cholesky" | custom-call | tf_op jit(solution)/shard_map/while/body/eval_jaxpr/jit(cholesky)/cholesky | solution.py:46
  110.5 9.8 custom-call.42
  129.6 46.5 %collective-permute-done.1 = bf16[1,2,64,8192]{3,2,1,0:T(8,128)(2,1)} collective-permute-done((bf16[1,2,64,8192]{3,2,1,0:T(8,128)(2,1)S(1)}, bf16[1,2,64,8192]{3,2,1,0:T(8,128)(2,1)}, u32[]{:S(2)}, u32[]{:S(2)}) %collective-permute-start.1) | collective-permute-done | bytes 2097184 | tf_op jit(solution)/shard_map/ppermute | solution.py:17
  182.7 49.6 %while.75 = (s32[]{:T(128)}, bf16[2,128,128]{1,2,0:T(8,128)(2,1)S(1)}, f32[2,128,128]{2,1,0:T(8,128)S(1)}, s32[128]{0:T(128)S(1)}, s32[]{:T(128)}) while((s32[]{:T(128)}, bf16[2,128,128]{1,2,0:T(8,128)(2,1)S(1)}, f32[2,128,128]{2,1,0:T(8,128)S(1)}, s32[128]{0:T(128)S(1)}, s32[]{:T(128)}) %tuple.145), condition=%wide.region_9.13_spmd.clone.clone, body=%wide.region_8.12_spmd.clone.clone.sunk | while | flops 151339136 | bytes 1837143 | solution.py:52
  183.5 11.7 %cholesky.377 = f32[128,128]{1,0:T(8,128)S(1)} custom-call(f32[128,128]{1,0:T(8,128)S(1)} %fusion.364), custom_call_target="Cholesky" | custom-call | tf_op jit(solution)/shard_map/while/body/eval_jaxpr/jit(cholesky)/cholesky | solution.py:46
  196.6 9.8 custom-call.41
  208.3 11.7 %cholesky.377 = f32[128,128]{1,0:T(8,128)S(1)} custom-call(f32[128,128]{1,0:T(8,128)S(1)} %fusion.364), custom_call_target="Cholesky" | custom-call | tf_op jit(solution)/shard_map/while/body/eval_jaxpr/jit(cholesky)/cholesky | solution.py:46
  240.2 46.1 %collective-permute-done.3 = bf16[1,2,64,8192]{3,2,1,0:T(8,128)(2,1)} collective-permute-done((bf16[1,2,64,8192]{3,2,1,0:T(8,128)(2,1)S(1)}, bf16[1,2,64,8192]{3,2,1,0:T(8,128)(2,1)}, u32[]{:S(2)}, u32[]{:S(2)}) %collective-permute-start.3) | collective-permute-done | bytes 2097184 | tf_op jit(solution)/shard_map/ppermute | solution.py:17
  294.2 49.6 %while.74 = (s32[]{:T(128)}, bf16[2,128,128]{1,2,0:T(8,128)(2,1)S(1)}, f32[2,128,128]{2,1,0:T(8,128)S(1)}, s32[128]{0:T(128)S(1)}, s32[]{:T(128)}) while((s32[]{:T(128)}, bf16[2,128,128]{1,2,0:T(8,128)(2,1)S(1)}, f32[2,128,128]{2,1,0:T(8,128)S(1)}, s32[128]{0:T(128)S(1)}, s32[]{:T(128)}) %tuple.148), condition=%wide.region_7.11_spmd.clone.clone, body=%wide.region_6.10_spmd.clone.clone.sunk | while | flops 151339136 | bytes 1837143 | solution.py:52
  295.0 11.7 %cholesky.365 = f32[128,128]{1,0:T(8,128)S(1)} custom-call(f32[128,128]{1,0:T(8,128)S(1)} %fusion.349), custom_call_target="Cholesky" | custom-call | tf_op jit(solution)/shard_map/while/body/eval_jaxpr/jit(cholesky)/cholesky | solution.py:46
  319.8 11.7 %cholesky.365 = f32[128,128]{1,0:T(8,128)S(1)} custom-call(f32[128,128]{1,0:T(8,128)S(1)} %fusion.349), custom_call_target="Cholesky" | custom-call | tf_op jit(solution)/shard_map/while/body/eval_jaxpr/jit(cholesky)/cholesky | solution.py:46
  351.7 46.4 %collective-permute-done.5 = bf16[1,2,64,8192]{3,2,1,0:T(8,128)(2,1)} collective-permute-done((bf16[1,2,64,8192]{3,2,1,0:T(8,128)(2,1)S(1)}, bf16[1,2,64,8192]{3,2,1,0:T(8,128)(2,1)}, u32[]{:S(2)}, u32[]{:S(2)}) %collective-permute-start.5) | collective-permute-done | bytes 2097184 | tf_op jit(solution)/shard_map/ppermute | solution.py:17
  405.4 49.6 %while.73 = (s32[]{:T(128)}, bf16[2,128,128]{1,2,0:T(8,128)(2,1)S(1)}, f32[2,128,128]{2,1,0:T(8,128)S(1)}, s32[128]{0:T(128)S(1)}, s32[]{:T(128)}) while((s32[]{:T(128)}, bf16[2,128,128]{1,2,0:T(8,128)(2,1)S(1)}, f32[2,128,128]{2,1,0:T(8,128)S(1)}, s32[128]{0:T(128)S(1)}, s32[]{:T(128)}) %tuple.151), condition=%wide.region_5.9_spmd.clone.clone, body=%wide.region_4.8_spmd.clone.clone.sunk | while | flops 151339136 | bytes 1837143 | solution.py:52
  406.2 11.7 %cholesky.353 = f32[128,128]{1,0:T(8,128)S(1)} custom-call(f32[128,128]{1,0:T(8,128)S(1)} %fusion.334), custom_call_target="Cholesky" | custom-call | tf_op jit(solution)/shard_map/while/body/eval_jaxpr/jit(cholesky)/cholesky | solution.py:46
  431.0 11.7 %cholesky.353 = f32[128,128]{1,0:T(8,128)S(1)} custom-call(f32[128,128]{1,0:T(8,128)S(1)} %fusion.334), custom_call_target="Cholesky" | custom-call | tf_op jit(solution)/shard_map/while/body/eval_jaxpr/jit(cholesky)/cholesky | solution.py:46
  462.8 43.8 %collective-permute-done.7 = bf16[1,2,64,8192]{3,2,1,0:T(8,128)(2,1)} collective-permute-done((bf16[1,2,64,8192]{3,2,1,0:T(8,128)(2,1)S(1)}, bf16[1,2,64,8192]{3,2,1,0:T(8,128)(2,1)}, u32[]{:S(2)}, u32[]{:S(2)}) %collective-permute-start.7) | collective-permute-done | bytes 2097184 | tf_op jit(solution)/shard_map/ppermute | solution.py:17
  515.4 49.6 %while.72 = (s32[]{:T(128)}, bf16[2,128,128]{1,2,0:T(8,128)(2,1)S(1)}, f32[2,128,128]{2,1,0:T(8,128)S(1)}, s32[128]{0:T(128)S(1)}, s32[]{:T(128)}) while((s32[]{:T(128)}, bf16[2,128,128]{1,2,0:T(8,128)(2,1)S(1)}, f32[2,128,128]{2,1,0:T(8,128)S(1)}, s32[128]{0:T(128)S(1)}, s32[]{:T(128)}) %tuple.154), condition=%wide.region_3.0_spmd.clone.clone, body=%wide.region_0.6_spmd.clone.clone.sunk | while | flops 151339136 | bytes 1837143 | solution.py:52
  516.1 11.7 %cholesky.341 = f32[128,128]{1,0:T(8,128)S(1)} custom-call(f32[128,128]{1,0:T(8,128)S(1)} %fusion.319), custom_call_target="Cholesky" | custom-call | tf_op jit(solution)/shard_map/while/body/eval_jaxpr/jit(cholesky)/cholesky | solution.py:46
  529.3 9.8 custom-call.38
  541.0 11.7 %cholesky.341 = f32[128,128]{1,0:T(8,128)S(1)} custom-call(f32[128,128]{1,0:T(8,128)S(1)} %fusion.319), custom_call_target="Cholesky" | custom-call | tf_op jit(solution)/shard_map/while/body/eval_jaxpr/jit(cholesky)/cholesky | solution.py:46
  580.0 43.1 %collective-permute-done.9 = bf16[1,2,64,8192]{3,2,1,0:T(8,128)(2,1)S(1)} collective-permute-done((bf16[1,2,64,8192]{3,2,1,0:T(8,128)(2,1)}, bf16[1,2,64,8192]{3,2,1,0:T(8,128)(2,1)S(1)}, u32[]{:S(2)}, u32[]{:S(2)}) %collective-permute-start.9) | collective-permute-done | bytes 2097184 | tf_op jit(solution)/shard_map/ppermute | solution.py:17
  627.9 10.5 %convert_bitcast_fusion = bf16[1024,8192]{0,1:T(8,128)(2,1)} fusion(bf16[256,8192]{1,0:T(8,128)(2,1)} %bitcast.492, bf16[1024,256]{1,0:T(8,128)(2,1)S(1)} %bitcast.495), kind=kOutput, calls=%fused_computation.181 | convolution fusion | flops 4303355904 | bytes 21495808 | tf_op jit(solution)/shard_map/dot_general | solution.py:107
  638.4 21.4 %copy.102 = bf16[1024,8192]{1,0:T(8,128)(2,1)} copy(bf16[1024,8192]{0,1:T(8,128)(2,1)} %convert_bitcast_fusion) | data formatting | bytes 33554432
  659.8 358.7 %reduce-scatter.4.cloned.1.call-done = bf16[32,8192]{1,0:T(8,128)(2,1)} async-done(((bf16[1024,8192]{1,0:T(8,128)(2,1)}), bf16[32,8192]{1,0:T(8,128)(2,1)}) %reduce-scatter.4.cloned.1.call-update) | async-done | bytes 524304 | tf_op jit(solution)/shard_map/reduce_scatter | solution.py:106
  (242 shorter events, 194.6 us)
Async XLA Ops:
  70.0 54.0 %collective-permute-start = (bf16[1,2,64,8192]{3,2,1,0:T(8,128)(2,1)}, bf16[1,2,64,8192]{3,2,1,0:T(8,128)(2,1)}, u32[]{:S(2)}, u32[]{:S(2)}) collective-permute-start(bf16[1,2,64,8192]{3,2,1,0:T(8,128)(2,1)} %fusion.146), channel_id=1, source_target_pairs={{0,1},{1,0},{2,3},{3,2},{4,5},{5,4},{6,7},{7,6},{8,9},{9,8},{10,11... | collective-permute-start | bytes 6291464 | tf_op jit(solution)/shard_map/ppermute | solution.py:17
  127.0 1.9 copy-start.5
  128.9 47.2 %collective-permute-start.1 = (bf16[1,2,64,8192]{3,2,1,0:T(8,128)(2,1)S(1)}, bf16[1,2,64,8192]{3,2,1,0:T(8,128)(2,1)}, u32[]{:S(2)}, u32[]{:S(2)}) collective-permute-start(bf16[1,2,64,8192]{3,2,1,0:T(8,128)(2,1)S(1)} %dynamic-slice_bitcast_fusion.10), channel_id=1, source_target_pairs={{0,1},{1,0},{2,3},{3,2},{4,5},{5,4},{6,7},{7,6},{8,9},{9,8},{10,11... | collective-permute-start | bytes 6291464 | tf_op jit(solution)/shard_map/ppermute | solution.py:17
  179.0 2.1 copy-start.1
  181.1 54.2 %collective-permute-start.2 = (bf16[1,2,64,8192]{3,2,1,0:T(8,128)(2,1)}, bf16[1,2,64,8192]{3,2,1,0:T(8,128)(2,1)}, u32[]{:S(2)}, u32[]{:S(2)}) collective-permute-start(bf16[1,2,64,8192]{3,2,1,0:T(8,128)(2,1)} %fusion.140), channel_id=1, source_target_pairs={{0,2},{2,0},{1,3},{3,1},{4,6},{6,4},{5,7},{7,5},{8,10},{10,8},{9,1... | collective-permute-start | bytes 6291464 | tf_op jit(solution)/shard_map/ppermute | solution.py:17
  238.3 1.9 copy-start.6
  240.2 46.1 %collective-permute-start.3 = (bf16[1,2,64,8192]{3,2,1,0:T(8,128)(2,1)S(1)}, bf16[1,2,64,8192]{3,2,1,0:T(8,128)(2,1)}, u32[]{:S(2)}, u32[]{:S(2)}) collective-permute-start(bf16[1,2,64,8192]{3,2,1,0:T(8,128)(2,1)S(1)} %dynamic-slice_bitcast_fusion.9), channel_id=1, source_target_pairs={{0,2},{2,0},{1,3},{3,1},{4,6},{6,4},{5,7},{7,5},{8,10},{10,8},{9,1... | collective-permute-start | bytes 6291464 | tf_op jit(solution)/shard_map/ppermute | solution.py:17
  289.2 2.1 copy-start.2
  291.3 55.5 %collective-permute-start.4 = (bf16[1,2,64,8192]{3,2,1,0:T(8,128)(2,1)}, bf16[1,2,64,8192]{3,2,1,0:T(8,128)(2,1)}, u32[]{:S(2)}, u32[]{:S(2)}) collective-permute-start(bf16[1,2,64,8192]{3,2,1,0:T(8,128)(2,1)} %fusion.134), channel_id=1, source_target_pairs={{0,4},{4,0},{1,5},{5,1},{2,6},{6,2},{3,7},{7,3},{8,12},{12,8},{9,1... | collective-permute-start | bytes 6291464 | tf_op jit(solution)/shard_map/ppermute | solution.py:17
  349.7 1.9 copy-start.7
  351.7 46.4 %collective-permute-start.5 = (bf16[1,2,64,8192]{3,2,1,0:T(8,128)(2,1)S(1)}, bf16[1,2,64,8192]{3,2,1,0:T(8,128)(2,1)}, u32[]{:S(2)}, u32[]{:S(2)}) collective-permute-start(bf16[1,2,64,8192]{3,2,1,0:T(8,128)(2,1)S(1)} %dynamic-slice_bitcast_fusion.8), channel_id=1, source_target_pairs={{0,4},{4,0},{1,5},{5,1},{2,6},{6,2},{3,7},{7,3},{8,12},{12,8},{9,1... | collective-permute-start | bytes 6291464 | tf_op jit(solution)/shard_map/ppermute | solution.py:17
  401.0 2.1 copy-start.3
  403.1 54.8 %collective-permute-start.6 = (bf16[1,2,64,8192]{3,2,1,0:T(8,128)(2,1)}, bf16[1,2,64,8192]{3,2,1,0:T(8,128)(2,1)}, u32[]{:S(2)}, u32[]{:S(2)}) collective-permute-start(bf16[1,2,64,8192]{3,2,1,0:T(8,128)(2,1)} %fusion.128), channel_id=1, source_target_pairs={{0,8},{8,0},{1,9},{9,1},{2,10},{10,2},{3,11},{11,3},{4,12},{12,4},... | collective-permute-start | bytes 6291464 | tf_op jit(solution)/shard_map/ppermute | solution.py:17
  460.9 1.9 copy-start.4
  462.8 43.8 %collective-permute-start.7 = (bf16[1,2,64,8192]{3,2,1,0:T(8,128)(2,1)S(1)}, bf16[1,2,64,8192]{3,2,1,0:T(8,128)(2,1)}, u32[]{:S(2)}, u32[]{:S(2)}) collective-permute-start(bf16[1,2,64,8192]{3,2,1,0:T(8,128)(2,1)S(1)} %dynamic-slice_bitcast_fusion.7), channel_id=1, source_target_pairs={{0,8},{8,0},{1,9},{9,1},{2,10},{10,2},{3,11},{11,3},{4,12},{12,4},... | collective-permute-start | bytes 6291464 | tf_op jit(solution)/shard_map/ppermute | solution.py:17
  509.6 2.1 copy-start
  511.6 56.3 %collective-permute-start.8 = (bf16[1,2,64,8192]{3,2,1,0:T(8,128)(2,1)}, bf16[1,2,64,8192]{3,2,1,0:T(8,128)(2,1)}, u32[]{:S(2)}, u32[]{:S(2)}) collective-permute-start(bf16[1,2,64,8192]{3,2,1,0:T(8,128)(2,1)} %fusion.122), channel_id=1, source_target_pairs={{0,16},{16,0},{1,17},{17,1},{2,18},{18,2},{3,19},{19,3},{4,20},{20... | collective-permute-start | bytes 6291464 | tf_op jit(solution)/shard_map/ppermute | solution.py:17
  570.9 2.6 copy-start.8
  570.9 2.6 copy-start.9
  573.5 49.6 %collective-permute-start.9 = (bf16[1,2,64,8192]{3,2,1,0:T(8,128)(2,1)}, bf16[1,2,64,8192]{3,2,1,0:T(8,128)(2,1)S(1)}, u32[]{:S(2)}, u32[]{:S(2)}) collective-permute-start(bf16[1,2,64,8192]{3,2,1,0:T(8,128)(2,1)} %dynamic-slice_bitcast_fusion.6), channel_id=1, source_target_pairs={{0,16},{16,0},{1,17},{17,1},{2,18},{18,2},{3,19},{19,3},{4,20},{20... | collective-permute-start | bytes 6291464 | tf_op jit(solution)/shard_map/ppermute | solution.py:17
  574.3 53.5 %all-to-all-start = ((bf16[32,32,256]{2,0,1:T(8,128)(2,1)}), bf16[32,32,256]{2,0,1:T(8,128)(2,1)S(1)}, u32[]{:S(2)}, u32[]{:S(2)}) async-start(bf16[32,32,256]{2,0,1:T(8,128)(2,1)} %bitcast.347), calls=%async_computation | async-start | bytes 1048576 | tf_op jit(solution)/shard_map/all_to_all | solution.py:62
  579.7 438.8 %reduce-scatter.4.cloned.1.call-start = ((), (), s32[]{:S(2)}) async-start(), calls=%async_computation.2 | async-start | bytes 17301504 | tf_op jit(solution)/shard_map/reduce_scatter | solution.py:106
Sparse Core Ops, SparseCore 0:
  659.9 358.5 reduce-scatter.3
where the time goes:
time: 1030 us
  waiting for transfers between devices  584 us (57%)
  other arithmetic  302 us (29%)
  matrix products  61.6 us (6%)
  local copies, waits for them, and re-layouts  43.1 us (4%)
  starting transfers between devices  18.8 us (2%)
  between operations  14 us (1%)
    reduce_scatter x1, waiting for transfers between devices, shards(): lax.psum_scatter(jnp.dot(features, current, preferred_element_type=jnp.fl...  359 us
    ppermute x10, waiting for transfers between devices, from_partner(): return lax.ppermute(block, axis, route)  226 us
    another operation x36, other arithmetic, one_block(): factor = jnp.linalg.cholesky(identity - square)  149 us
    another operation x24, other arithmetic, chol_solve(): lax.linalg.triangular_solve(factor, first, left_side=True, lower=True, tr...  125 us
    unnamed x21, local copies, waits for them, and re-layouts  29.6 us
  transfers between devices with their start and end apart: 12, of which 6 were waited for; matrix products, arithmetic and copies ran while one was open for 26% of the time, Pallas kernels for 0%

commit v1 on v0

v1 whole, which is shorter than its diff:
```python
import jax
import jax.numpy as jnp
import numpy as np
from jax import lax
from jax.experimental import pallas as pl
from jax.experimental.pallas import tpu as pltpu
from jax.sharding import PartitionSpec as P

HALF = 64
BLK = 128


def pair_table(distance, count):
    stride = 1 << distance
    rows = []
    for group in range(count // (2 * stride)):
        for offset in range(stride):
            low = group * 2 * stride + offset
            member = low if low >> 1 & 1 == 0 else low + stride
            rows.append((low, low + stride, (member >> 2) * 2 + (member & 1)))
    return rows


def rotation_kernel(skew_ref, pairing_ref, out_ref, work):
    count = work.shape[0]
    for block in range(count):
        raw = skew_ref[block]
        work[block] = raw.T - raw
    lanes = lax.broadcasted_iota(jnp.int32, (BLK, BLK), 1)
    lane_row = lax.broadcasted_iota(jnp.int32, (1, BLK), 1)

    def eliminate(step, carry):
        is_pivot = lanes == step
        pick = jnp.full((BLK, BLK), step, jnp.int32)
        unit = (lane_row == step).astype(jnp.float32)
        for block in range(count):
            current = work[block]
            column = jnp.take_along_axis(current, pick, axis=1)
            row = work[block, pl.ds(step, 1), :]
            pivot = 1.0 + jnp.sum(row * unit, axis=1, keepdims=True)
            scaled = (row * (1.0 - unit) + unit) / pivot
            work[block] = jnp.where(is_pivot, 0.0, current) - column * scaled
        return carry

    lax.fori_loop(0, BLK, eliminate, 0)
    rows = lax.broadcasted_iota(jnp.int32, (BLK, BLK), 0)
    identity = (rows == lanes).astype(jnp.float32)
    for block in range(count):
        order = pairing_ref[pl.ds(block // 2, 1), :]
        chosen = (rows == order).astype(jnp.bfloat16)
        rotation = (identity + 2.0 * work[block]).astype(jnp.bfloat16)
        inner = jnp.dot(chosen, rotation, preferred_element_type=jnp.float32).astype(jnp.bfloat16)
        outer = lax.dot_general(inner, chosen, (((1,), (1,)), ((), ())), preferred_element_type=jnp.float32)
        out_ref[block] = outer.astype(jnp.bfloat16)


def cayley_blocks(skew_params, pairing):
    sections, owned = skew_params.shape[:2]
    count = sections * owned
    out = pl.pallas_call(
        rotation_kernel,
        out_shape=jax.ShapeDtypeStruct((count, BLK, BLK), jnp.bfloat16),
        in_specs=[pl.BlockSpec(memory_space=pltpu.VMEM)] * 2,
        out_specs=pl.BlockSpec(memory_space=pltpu.VMEM),
        scratch_shapes=[pltpu.VMEM((count, BLK, BLK), jnp.float32)],
        cost_estimate=pl.CostEstimate(flops=count * BLK**3 * 20, bytes_accessed=count * BLK * BLK * 6, transcendentals=0),
    )(skew_params.reshape(count, BLK, BLK), pairing)
    return out.reshape(sections, owned, BLK, BLK)


def rotate_rows(slab, rotations, distance):
    halves = slab.shape[0] // HALF
    parts = [None] * halves
    for low, high, owner in pair_table(distance, halves):
        joined = jnp.concatenate([slab[low * HALF:(low + 1) * HALF], slab[high * HALF:(high + 1) * HALF]], axis=0)
        turned = jnp.dot(rotations[owner], joined, preferred_element_type=jnp.float32).astype(jnp.bfloat16)
        parts[low], parts[high] = turned[:HALF], turned[HALF:]
    return jnp.concatenate(parts, axis=0)


def rotate_cols(rows, rotations, distance):
    halves = rows.shape[1] // HALF
    parts = [None] * halves
    for low, high, owner in pair_table(distance, halves):
        joined = jnp.concatenate([rows[:, low * HALF:(low + 1) * HALF], rows[:, high * HALF:(high + 1) * HALF]], axis=1)
        turned = jnp.dot(joined, rotations[owner], preferred_element_type=jnp.float32).astype(jnp.bfloat16)
        parts[low], parts[high] = turned[:, :HALF], turned[:, HALF:]
    return jnp.concatenate(parts, axis=1)


def shards(weight_slab, token_rows, skew_params, pairing):
    plane = [[z * 8 + c for c in range(8)] for z in range(4)]
    column = [[z * 8 + c for z in range(4)] for c in range(8)]
    rotations = cayley_blocks(skew_params, pairing)
    slab = lax.all_to_all(weight_slab, "tensor", split_axis=1, concat_axis=0, axis_index_groups=plane, tiled=True)
    local = token_rows.reshape(32, 4, 8, 256)
    spread = lax.all_to_all(local, "tensor", split_axis=2, concat_axis=0, axis_index_groups=plane, tiled=True)
    spread = spread.reshape(256, 1024)
    rot_z = lax.all_gather(rotations[4:], "tensor", axis_index_groups=column, axis=1, tiled=True)
    rot_xy = lax.all_gather(rotations[:4], "tensor", axis_index_groups=plane, axis=1, tiled=True)
    spread = rotate_cols(spread, rot_z[1], 3)
    spread = rotate_cols(spread, rot_z[0], 2)
    features = lax.all_to_all(spread, "tensor", split_axis=1, concat_axis=0, axis_index_groups=column, tiled=True)
    features = lax.all_gather(features, "tensor", axis_index_groups=plane, axis=0)
    for section, distance in enumerate((0, 2, 3, 4)):
        slab = rotate_rows(slab, rot_xy[section], distance)
    partial = jnp.einsum("ptf,pfn->tn", features, slab.reshape(8, 256, 1024), preferred_element_type=jnp.float32)
    partial = partial.astype(jnp.bfloat16)
    landed = lax.all_to_all(partial, "tensor", split_axis=0, concat_axis=0, tiled=True)
    landed = landed.reshape(4, 8, 32, 1024).astype(jnp.float32).sum(axis=0)
    return landed.transpose(1, 0, 2).reshape(32, 8192).astype(jnp.bfloat16)


def solution(mesh):
    in_specs = (
        P(("layer", "tensor"), None),
        P(("layer", "tensor"), None),
        P("layer", "tensor", None, None),
        P("layer", None),
    )
    out_specs = P(("layer", "tensor"), None)
    return jax.shard_map(shards, mesh=mesh, in_specs=in_specs, out_specs=out_specs, check_vma=False)
```

time: 1030 us -> 445 us (0.43)
  waiting for transfers between devices: 584 us -> 127 us
  other arithmetic: 302 us -> 0.43 us
  Pallas kernels: 0 us -> 153 us
  blocking collectives: 0 us -> 50.3 us
  matrix products: 61.6 us -> 31.7 us
    reduce_scatter x1 -> x0, waiting for transfers between devices: 359 us -> none  [shards(): lax.psum_scatter(jnp.dot(features, current, preferred_element_type=jnp.fl...]
    another operation x66 -> x0, other arithmetic: 291 us -> none  [the longest x36 149 us: one_block(): factor = jnp.linalg.cholesky(identity - square)]
    ppermute x10 -> x0, waiting for transfers between devices: 226 us -> none  [from_partner(): return lax.ppermute(block, axis, route)]
    pallas_call x0 -> x1, Pallas kernels: none -> 153 us  [cayley_blocks(): pl.pallas_call(rotation_kernel, out_shape=jax.ShapeDtypeStruct((count, BL...]
    all_to_all x1 -> x3, waiting for transfers between devices: 0.01 us -> 65.4 us  [the longest x1 64.6 us: shards(): lax.all_to_all(weight_slab, 'tensor', split_axis=1, concat_axis=0, axis_i...]
    all_gather x0 -> x2, waiting for transfers between devices: none -> 61.2 us  [the longest x1 49 us: shards(): lax.all_gather(features, 'tensor', axis_index_groups=plane, axis=0)]
    all_to_all x0 -> x1, blocking collectives: none -> 36.3 us  [shards(): lax.all_to_all(partial, 'tensor', split_axis=0, concat_axis=0, tiled=True)]
    dot_general x60 -> x81, matrix products: 55.7 us -> 31.7 us  [the longest x64 20 us: rotate_rows(): jnp.dot(rotations[owner], joined, preferred_element_type=jnp.float32)]
  transfers between devices with their start and end apart: 12 -> 5, of which waited for: 6 -> 4; matrix products, arithmetic and copies ran while one was open for 26% -> 13% of each run, Pallas kernels for 0% -> 35%
where the time goes in v1:
time: 445 us; the launch traced here: 443 us
  Pallas kernels  153 us (34%)
  waiting for transfers between devices  127 us (29%)
  local copies, waits for them, and re-layouts  50.9 us (11%)
  blocking collectives  50.3 us (11%)
  matrix products  31.7 us (7%)
  starting transfers between devices  15.1 us (3%)
  between operations  14.4 us (3%)
    pallas_call x1, Pallas kernels, cayley_blocks(): pl.pallas_call(rotation_kernel, out_shape=jax.ShapeDtypeStruct((count, BL...  153 us
    all_to_all x1, waiting for transfers between devices, shards(): lax.all_to_all(weight_slab, 'tensor', split_axis=1, concat_axis=0, axis_i...  64.6 us
    all_gather x1, waiting for transfers between devices, shards(): lax.all_gather(features, 'tensor', axis_index_groups=plane, axis=0)  49 us
    unnamed x55, local copies, waits for them, and re-layouts  37.5 us
    all_to_all x1, blocking collectives, shards(): lax.all_to_all(partial, 'tensor', split_axis=0, concat_axis=0, tiled=True)  36.3 us
    dot_general x64, matrix products, rotate_rows(): jnp.dot(rotations[owner], joined, preferred_element_type=jnp.float32)  20 us
    all_gather x1, blocking collectives, shards(): lax.all_gather(rotations[4:], 'tensor', axis_index_groups=column, axis=1,...  14 us
    all_gather x1, waiting for transfers between devices, shards(): lax.all_gather(rotations[:4], 'tensor', axis_index_groups=plane, axis=1,...  12.2 us
  transfers between devices with their start and end apart: 5, of which 4 were waited for; matrix products, arithmetic and copies ran while one was open for 13% of the time, Pallas kernels for 35%

profile of v1, /device:TPU:16, one launch (start us, length us, event | category | flops | bytes accessed | tf_op | source)
XLA Modules:
  0.0 442.6 jit_solution(8676832690451755885)
XLA Ops:
  6.5 1.2 copy.22
  7.7 1.0 copy.16
  8.7 5.0 %all-to-all-start = ((bf16[32,4,8,256]{3,1,0,2:T(4,128)(2,1)}), bf16[32,4,8,256]{3,1,0,2:T(4,128)(2,1)S(1)}, u32[]{:S(2)}, u32[]{:S(2)}) async-start(bf16[32,4,8,256]{3,1,0,2:T(4,128)(2,1)} %copy.16), calls=%async_computation | async-start | bytes 1048576 | tf_op jit(solution)/shard_map/all_to_all | solution.py:97
  13.7 153.2 %shard_map.46 = bf16[12,128,128]{2,1,0:T(8,128)(2,1)} custom-call(f32[12,128,128]{2,1,0:T(8,128)} %bitcast.297, s32[6,128]{1,0:T(8,128)} %pairing_ref.1), custom_call_target="tpu_custom_call" | custom-call | flops 503316480 | bytes 1179648 | tf_op jit(solution)/shard_map/pallas_call | solution.py:60
  166.9 0.9 slice.1256
  167.8 14.0 %all_gather.12 = bf16[2,8,128,128]{3,2,1,0:T(8,128)(2,1)S(1)} all-gather(bf16[2,2,128,128]{3,2,1,0:T(8,128)(2,1)S(1)} %bitcast.295), channel_id=1, replica_groups={{0,8,16,24},{1,9,17,25},{2,10,18,26},{3,11,19,27},{4,12,20,28},{5,13,21..., dimensions={1}, use_global_device_ids=true | all-gather | bytes 655360 | tf_op jit(solution)/shard_map/all_gather | solution.py:99
  196.0 4.6 %all-to-all-start.1 = ((bf16[256,4,256]{0,2,1:T(8,128)(2,1)}), bf16[256,4,256]{0,2,1:T(8,128)(2,1)S(1)}, u32[]{:S(2)}, u32[]{:S(2)}) async-start(bf16[256,4,256]{0,2,1:T(8,128)(2,1)} %bitcast.20), calls=%async_computation.1 | async-start | bytes 1048576 | tf_op jit(solution)/shard_map/all_to_all | solution.py:103
  200.6 0.7 slice.1319
  201.4 6.5 %copy.18 = bf16[256,8192]{0,1:T(8,128)(2,1)} copy(bf16[256,8192]{1,0:T(8,128)(2,1)} %param.4) | data formatting | bytes 8388608 | tf_op args[0]
  207.8 0.9 all-to-all-done.1
  208.7 5.4 %all-to-all-start.2 = ((bf16[256,8,1024]{0,2,1:T(8,128)(2,1)}), bf16[256,8,1024]{0,2,1:T(8,128)(2,1)}, u32[]{:S(2)}, u32[]{:S(2)}) async-start(bf16[256,8,1024]{0,2,1:T(8,128)(2,1)} %bitcast.285), calls=%async_computation.2 | async-start | bytes 8388608 | tf_op jit(solution)/shard_map/all_to_all | solution.py:95
  214.2 1.0 copy.17
  215.2 64.6 %all-to-all-done.2 = bf16[256,8,1024]{0,2,1:T(8,128)(2,1)} async-done(((bf16[256,8,1024]{0,2,1:T(8,128)(2,1)}), bf16[256,8,1024]{0,2,1:T(8,128)(2,1)}, u32[]{:S(2)}, u32[]{:S(2)}) %all-to-all-start.2) | async-done | bytes 4194336 | tf_op jit(solution)/shard_map/all_to_all | solution.py:95
  279.8 6.5 %copy.19 = bf16[8,256,1024]{2,1,0:T(8,128)(2,1)} copy(bf16[8,256,1024]{1,2,0:T(8,128)(2,1)} %bitcast.29) | data formatting | bytes 8388608 | tf_op jit(solution)/shard_map/all_to_all | solution.py:95
  286.2 12.2 %all-gather.5.cloned.1.call-done = bf16[4,16,128,128]{3,2,1,0:T(8,128)(2,1)} async-done(((bf16[4,2,128,128]{3,2,1,0:T(8,128)(2,1)}), bf16[4,16,128,128]{3,2,1,0:T(8,128)(2,1)}) %all-gather.5.cloned.1.call-update) | async-done | bytes 2097168 | tf_op jit(solution)/shard_map/all_gather | solution.py:100
  298.4 1.3 convolution_convert_fusion.40
  299.7 1.8 convolution_convert_fusion.41
  301.6 1.0 convolution_convert_fusion.26
  302.6 1.2 convolution_convert_fusion.37
  303.8 1.2 convolution_convert_fusion.38
  305.0 1.0 convolution_convert_fusion.25
  319.4 0.7 slice_dynamic-update-slice_fusion.28
  320.3 0.7 slice_dynamic-update-slice_fusion.27
  321.2 0.7 slice_dynamic-update-slice_fusion.26
  323.2 0.7 slice_dynamic-update-slice_fusion.24
  325.6 0.7 slice_dynamic-update-slice_fusion.21
  336.0 0.7 slice_dynamic-update-slice_fusion.7
  337.3 0.7 slice_dynamic-update-slice_fusion.5
  341.3 49.0 %all-gather.3.cloned.1.call-done = bf16[8,1024,256]{2,1,0:T(8,128)(2,1)} async-done(((bf16[1,1024,256]{2,1,0:T(8,128)(2,1)}), bf16[8,1024,256]{2,1,0:T(8,128)(2,1)}) %all-gather.3.cloned.1.call-update) | async-done | bytes 4194320 | tf_op jit(solution)/shard_map/all_gather | solution.py:104
  390.3 7.9 %bitcast_convert_fusion = bf16[1024,1024]{1,0:T(8,128)(2,1)S(1)} fusion(bf16[8,1024,256]{2,1,0:T(8,128)(2,1)} %all-gather.3.cloned.1.call-done, bf16[8,256,1024]{2,1,0:T(8,128)(2,1)} %bitcast.91), kind=kOutput, calls=%fused_computation | convolution fusion | flops 4296015872 | bytes 10485760 | tf_op jit(solution)/shard_map/ptf,pfn->tn/dot_general | solution.py:107
  398.3 36.3 %all_to_all.59 = bf16[32,32,1024]{2,1,0:T(8,128)(2,1)S(1)} all-to-all(bf16[32,32,1024]{2,1,0:T(8,128)(2,1)S(1)} %bitcast.288), channel_id=1, replica_groups=mesh['layer'=4,'tensor'=32] {'tensor'}, dimensions={0} | all-to-all | bytes 4194304 | tf_op jit(solution)/shard_map/all_to_all | solution.py:109
  435.0 0.8 copy.21
  (173 shorter events, 44.5 us)
Async XLA Ops:
  8.7 173.1 %all-to-all-start = ((bf16[32,4,8,256]{3,1,0,2:T(4,128)(2,1)}), bf16[32,4,8,256]{3,1,0,2:T(4,128)(2,1)S(1)}, u32[]{:S(2)}, u32[]{:S(2)}) async-start(bf16[32,4,8,256]{3,1,0,2:T(4,128)(2,1)} %copy.16), calls=%async_computation | async-start | bytes 1048576 | tf_op jit(solution)/shard_map/all_to_all | solution.py:97
  181.9 18.7 %copy-start.2 = (bf16[12,128,128]{2,1,0:T(8,128)(2,1)S(1)}, bf16[12,128,128]{2,1,0:T(8,128)(2,1)}, u32[]{:S(2)}) copy-start(bf16[12,128,128]{2,1,0:T(8,128)(2,1)} %shard_map.46) | copy-start | bytes 1179652
  196.0 12.7 %all-to-all-start.1 = ((bf16[256,4,256]{0,2,1:T(8,128)(2,1)}), bf16[256,4,256]{0,2,1:T(8,128)(2,1)S(1)}, u32[]{:S(2)}, u32[]{:S(2)}) async-start(bf16[256,4,256]{0,2,1:T(8,128)(2,1)} %bitcast.20), calls=%async_computation.1 | async-start | bytes 1048576 | tf_op jit(solution)/shard_map/all_to_all | solution.py:103
  200.6 97.8 %all-gather.5.cloned.1.call-start = ((), (), s32[]{:S(2)}) async-start(), calls=%async_computation.5 | async-start | bytes 2359296 | tf_op jit(solution)/shard_map/all_gather | solution.py:100
  208.7 71.1 %all-to-all-start.2 = ((bf16[256,8,1024]{0,2,1:T(8,128)(2,1)}), bf16[256,8,1024]{0,2,1:T(8,128)(2,1)}, u32[]{:S(2)}, u32[]{:S(2)}) async-start(bf16[256,8,1024]{0,2,1:T(8,128)(2,1)} %bitcast.285), calls=%async_computation.2 | async-start | bytes 8388608 | tf_op jit(solution)/shard_map/all_to_all | solution.py:95
  214.1 176.2 %all-gather.3.cloned.1.call-start = ((), (), s32[]{:S(2)}) async-start(), calls=%async_computation.4 | async-start | bytes 4718592 | tf_op jit(solution)/shard_map/all_gather | solution.py:104
  298.4 7.6 %copy-start.1 = (bf16[4,16,128,128]{3,2,1,0:T(8,128)(2,1)S(1)}, bf16[4,16,128,128]{3,2,1,0:T(8,128)(2,1)}, u32[]{:S(2)}) copy-start(bf16[4,16,128,128]{3,2,1,0:T(8,128)(2,1)} %all-gather.5.cloned.1.call-done) | copy-start | bytes 6291460
  298.4 7.9 %copy-start = (bf16[8,256,1024]{2,1,0:T(8,128)(2,1)S(1)}, bf16[8,256,1024]{2,1,0:T(8,128)(2,1)}, u32[]{:S(2)}) copy-start(bf16[8,256,1024]{2,1,0:T(8,128)(2,1)} %copy.19) | copy-start | bytes 12582916
Sparse Core Ops, SparseCore 0:
  203.1 95.2 all-gather.4
  300.0 90.2 all-gather.2

commit v2 on v1

--- a/solution.py
+++ b/solution.py
@@ -21,34 +21,60 @@
     return rows
 
 
-def rotation_kernel(skew_ref, pairing_ref, out_ref, work):
-    count = work.shape[0]
+def split_dot(left, right):
+    left_hi = left.astype(jnp.bfloat16)
+    left_lo = (left - left_hi.astype(jnp.float32)).astype(jnp.bfloat16)
+    right_hi = right.astype(jnp.bfloat16)
+    right_lo = (right - right_hi.astype(jnp.float32)).astype(jnp.bfloat16)
+    return jnp.dot(
+        jnp.concatenate([left_hi, left_hi, left_lo], axis=1),
+        jnp.concatenate([right_hi, right_lo, right_hi], axis=0),
+        preferred_element_type=jnp.float32,
+    )
+
+
+def full_dot(left, right):
+    return jnp.dot(left, right, precision=lax.Precision.HIGHEST, preferred_element_type=jnp.float32)
+
+
+def rotation_kernel(skew_ref, pairing_ref, out_ref, gram, guess):
+    count = gram.shape[0]
+    rows = lax.broadcasted_iota(jnp.int32, (BLK, BLK), 0)
+    lanes = lax.broadcasted_iota(jnp.int32, (BLK, BLK), 1)
+    identity = (rows == lanes).astype(jnp.float32)
+    largest = jnp.zeros((1, BLK), jnp.float32)
     for block in range(count):
         raw = skew_ref[block]
-        work[block] = raw.T - raw
-    lanes = lax.broadcasted_iota(jnp.int32, (BLK, BLK), 1)
-    lane_row = lax.broadcasted_iota(jnp.int32, (1, BLK), 1)
+        skewed = raw - raw.T
+        square = full_dot(skewed, skewed)
+        gram[block] = identity - square
+        largest = jnp.maximum(largest, jnp.sum(square * square, axis=0, keepdims=True).sum(axis=1, keepdims=True))
+    top = 1.0 + jnp.sqrt(0.5 * jnp.max(largest)) * 1.0001
+    start = 2.0 / (1.0 + top)
+    for block in range(count):
+        guess[block] = identity * start
 
-    def eliminate(step, carry):
-        is_pivot = lanes == step
-        pick = jnp.full((BLK, BLK), step, jnp.int32)
-        unit = (lane_row == step).astype(jnp.float32)
+    def more(state):
+        return state > 2e-2
+
+    def improve(spread):
+        shrunk = spread * spread / (2.0 - spread * spread)
+        scale = 2.0 / (2.0 - spread * spread)
         for block in range(count):
-            current = work[block]
-            column = jnp.take_along_axis(current, pick, axis=1)
-            row = work[block, pl.ds(step, 1), :]
-            pivot = 1.0 + jnp.sum(row * unit, axis=1, keepdims=True)
-            scaled = (row * (1.0 - unit) + unit) / pivot
-            work[block] = jnp.where(is_pivot, 0.0, current) - column * scaled
-        return carry
+            now = guess[block]
+            left = 2.0 * identity - split_dot(gram[block], now)
+            guess[block] = scale * split_dot(now, left)
+        return shrunk
 
-    lax.fori_loop(0, BLK, eliminate, 0)
-    rows = lax.broadcasted_iota(jnp.int32, (BLK, BLK), 0)
-    identity = (rows == lanes).astype(jnp.float32)
+    lax.while_loop(more, improve, (top - 1.0) / (top + 1.0))
     for block in range(count):
+        raw = skew_ref[block]
+        raised = identity + raw - raw.T
+        now = guess[block]
+        now = now + split_dot(now, identity - full_dot(gram[block], now))
+        rotation = (2.0 * full_dot(now, raised) - identity).astype(jnp.bfloat16)
         order = pairing_ref[pl.ds(block // 2, 1), :]
         chosen = (rows == order).astype(jnp.bfloat16)
-        rotation = (identity + 2.0 * work[block]).astype(jnp.bfloat16)
         inner = jnp.dot(chosen, rotation, preferred_element_type=jnp.float32).astype(jnp.bfloat16)
         outer = lax.dot_general(inner, chosen, (((1,), (1,)), ((), ())), preferred_element_type=jnp.float32)
         out_ref[block] = outer.astype(jnp.bfloat16)
@@ -62,7 +88,7 @@
         out_shape=jax.ShapeDtypeStruct((count, BLK, BLK), jnp.bfloat16),
         in_specs=[pl.BlockSpec(memory_space=pltpu.VMEM)] * 2,
         out_specs=pl.BlockSpec(memory_space=pltpu.VMEM),
-        scratch_shapes=[pltpu.VMEM((count, BLK, BLK), jnp.float32)],
+        scratch_shapes=[pltpu.VMEM((count, BLK, BLK), jnp.float32)] * 2,
         cost_estimate=pl.CostEstimate(flops=count * BLK**3 * 20, bytes_accessed=count * BLK * BLK * 6, transcendentals=0),
     )(skew_params.reshape(count, BLK, BLK), pairing)
     return out.reshape(sections, owned, BLK, BLK)

time: 445 us -> 312 us (0.70)
  Pallas kernels: 153 us -> 19.4 us
    pallas_call x1, Pallas kernels: 153 us -> 19.4 us  [cayley_blocks(): pl.pallas_call(rotation_kernel, out_shape=jax.ShapeDtypeStruct((count, BL...]
  transfers between devices with their start and end apart: 5 -> 5, of which waited for: 4 -> 4; matrix products, arithmetic and copies ran while one was open for 13% -> 19% of each run, Pallas kernels for 35% -> 6%
where the time goes in v2:
time: 312 us; the launch traced here: 309 us
  waiting for transfers between devices  127 us (41%)
  blocking collectives  51 us (16%)
  local copies, waits for them, and re-layouts  50.9 us (16%)
  matrix products  31.7 us (10%)
  Pallas kernels  19.4 us (6%)
  starting transfers between devices  14.9 us (5%)
  between operations  14.4 us (5%)
    all_to_all x1, waiting for transfers between devices, shards(): lax.all_to_all(weight_slab, 'tensor', split_axis=1, concat_axis=0, axis_i...  63.8 us
    all_gather x1, waiting for transfers between devices, shards(): lax.all_gather(features, 'tensor', axis_index_groups=plane, axis=0)  47.8 us
    unnamed x55, local copies, waits for them, and re-layouts  37.5 us
    all_to_all x1, blocking collectives, shards(): lax.all_to_all(partial, 'tensor', split_axis=0, concat_axis=0, tiled=True)  36.8 us
    dot_general x64, matrix products, rotate_rows(): jnp.dot(rotations[owner], joined, preferred_element_type=jnp.float32)  20 us
    pallas_call x1, Pallas kernels, cayley_blocks(): pl.pallas_call(rotation_kernel, out_shape=jax.ShapeDtypeStruct((count, BL...  19.4 us
    all_gather x1, waiting for transfers between devices, shards(): lax.all_gather(rotations[:4], 'tensor', axis_index_groups=plane, axis=1,...  14.2 us
    all_gather x1, blocking collectives, shards(): lax.all_gather(rotations[4:], 'tensor', axis_index_groups=column, axis=1,...  14.2 us
  transfers between devices with their start and end apart: 5, of which 4 were waited for; matrix products, arithmetic and copies ran while one was open for 19% of the time, Pallas kernels for 6%

profile of v2, /device:TPU:16, one launch (start us, length us, event | category | flops | bytes accessed | tf_op | source)
XLA Modules:
  0.0 309.5 jit_solution(13856570997544268497)
XLA Ops:
  6.5 1.2 copy.22
  7.7 1.0 copy.16
  8.7 5.0 %all-to-all-start = ((bf16[32,4,8,256]{3,1,0,2:T(4,128)(2,1)}), bf16[32,4,8,256]{3,1,0,2:T(4,128)(2,1)S(1)}, u32[]{:S(2)}, u32[]{:S(2)}) async-start(bf16[32,4,8,256]{3,1,0,2:T(4,128)(2,1)} %copy.16), calls=%async_computation | async-start | bytes 1048576 | tf_op jit(solution)/shard_map/all_to_all | solution.py:123
  13.7 19.4 %shard_map.46 = bf16[12,128,128]{2,1,0:T(8,128)(2,1)} custom-call(f32[12,128,128]{2,1,0:T(8,128)} %bitcast.297, s32[6,128]{1,0:T(8,128)} %pairing_ref.1), custom_call_target="tpu_custom_call" | custom-call | flops 503316480 | bytes 1179648 | tf_op jit(solution)/shard_map/pallas_call | solution.py:86
  33.1 0.9 slice.1256
  34.0 14.2 %all_gather.12 = bf16[2,8,128,128]{3,2,1,0:T(8,128)(2,1)S(1)} all-gather(bf16[2,2,128,128]{3,2,1,0:T(8,128)(2,1)S(1)} %bitcast.295), channel_id=1, replica_groups={{0,8,16,24},{1,9,17,25},{2,10,18,26},{3,11,19,27},{4,12,20,28},{5,13,21..., dimensions={1}, use_global_device_ids=true | all-gather | bytes 655360 | tf_op jit(solution)/shard_map/all_gather | solution.py:125
  62.4 4.4 %all-to-all-start.1 = ((bf16[256,4,256]{0,2,1:T(8,128)(2,1)}), bf16[256,4,256]{0,2,1:T(8,128)(2,1)S(1)}, u32[]{:S(2)}, u32[]{:S(2)}) async-start(bf16[256,4,256]{0,2,1:T(8,128)(2,1)} %bitcast.20), calls=%async_computation.1 | async-start | bytes 1048576 | tf_op jit(solution)/shard_map/all_to_all | solution.py:129
  66.8 0.7 slice.1319
  67.6 6.5 %copy.18 = bf16[256,8192]{0,1:T(8,128)(2,1)} copy(bf16[256,8192]{1,0:T(8,128)(2,1)} %param.4) | data formatting | bytes 8388608 | tf_op args[0]
  74.0 0.9 all-to-all-done.1
  74.9 5.4 %all-to-all-start.2 = ((bf16[256,8,1024]{0,2,1:T(8,128)(2,1)}), bf16[256,8,1024]{0,2,1:T(8,128)(2,1)}, u32[]{:S(2)}, u32[]{:S(2)}) async-start(bf16[256,8,1024]{0,2,1:T(8,128)(2,1)} %bitcast.285), calls=%async_computation.2 | async-start | bytes 8388608 | tf_op jit(solution)/shard_map/all_to_all | solution.py:121
  80.4 1.0 copy.17
  81.4 63.8 %all-to-all-done.2 = bf16[256,8,1024]{0,2,1:T(8,128)(2,1)} async-done(((bf16[256,8,1024]{0,2,1:T(8,128)(2,1)}), bf16[256,8,1024]{0,2,1:T(8,128)(2,1)}, u32[]{:S(2)}, u32[]{:S(2)}) %all-to-all-start.2) | async-done | bytes 4194336 | tf_op jit(solution)/shard_map/all_to_all | solution.py:121
  145.2 6.5 %copy.19 = bf16[8,256,1024]{2,1,0:T(8,128)(2,1)} copy(bf16[8,256,1024]{1,2,0:T(8,128)(2,1)} %bitcast.29) | data formatting | bytes 8388608 | tf_op jit(solution)/shard_map/all_to_all | solution.py:121
  151.7 14.2 %all-gather.5.cloned.1.call-done = bf16[4,16,128,128]{3,2,1,0:T(8,128)(2,1)} async-done(((bf16[4,2,128,128]{3,2,1,0:T(8,128)(2,1)}), bf16[4,16,128,128]{3,2,1,0:T(8,128)(2,1)}) %all-gather.5.cloned.1.call-update) | async-done | bytes 2097168 | tf_op jit(solution)/shard_map/all_gather | solution.py:126
  165.9 1.3 convolution_convert_fusion.40
  167.2 1.8 convolution_convert_fusion.41
  169.1 1.0 convolution_convert_fusion.26
  170.1 1.2 convolution_convert_fusion.37
  171.3 1.2 convolution_convert_fusion.38
  172.5 1.0 convolution_convert_fusion.25
  186.9 0.7 slice_dynamic-update-slice_fusion.28
  187.8 0.7 slice_dynamic-update-slice_fusion.27
  190.7 0.7 slice_dynamic-update-slice_fusion.24
  193.1 0.7 slice_dynamic-update-slice_fusion.21
  198.9 0.7 slice_dynamic-update-slice_fusion.14
  203.5 0.7 slice_dynamic-update-slice_fusion.7
  204.8 0.7 slice_dynamic-update-slice_fusion.5
  208.8 47.8 %all-gather.3.cloned.1.call-done = bf16[8,1024,256]{2,1,0:T(8,128)(2,1)} async-done(((bf16[1,1024,256]{2,1,0:T(8,128)(2,1)}), bf16[8,1024,256]{2,1,0:T(8,128)(2,1)}) %all-gather.3.cloned.1.call-update) | async-done | bytes 4194320 | tf_op jit(solution)/shard_map/all_gather | solution.py:130
  256.6 8.0 %bitcast_convert_fusion = bf16[1024,1024]{1,0:T(8,128)(2,1)S(1)} fusion(bf16[8,1024,256]{2,1,0:T(8,128)(2,1)} %all-gather.3.cloned.1.call-done, bf16[8,256,1024]{2,1,0:T(8,128)(2,1)} %bitcast.91), kind=kOutput, calls=%fused_computation | convolution fusion | flops 4296015872 | bytes 10485760 | tf_op jit(solution)/shard_map/ptf,pfn->tn/dot_general | solution.py:133
  264.6 36.8 %all_to_all.59 = bf16[32,32,1024]{2,1,0:T(8,128)(2,1)S(1)} all-to-all(bf16[32,32,1024]{2,1,0:T(8,128)(2,1)S(1)} %bitcast.288), channel_id=1, replica_groups=mesh['layer'=4,'tensor'=32] {'tensor'}, dimensions={0} | all-to-all | bytes 4194304 | tf_op jit(solution)/shard_map/all_to_all | solution.py:135
  301.8 0.8 copy.21
  (173 shorter events, 44.5 us)
Async XLA Ops:
  8.7 39.5 %all-to-all-start = ((bf16[32,4,8,256]{3,1,0,2:T(4,128)(2,1)}), bf16[32,4,8,256]{3,1,0,2:T(4,128)(2,1)S(1)}, u32[]{:S(2)}, u32[]{:S(2)}) async-start(bf16[32,4,8,256]{3,1,0,2:T(4,128)(2,1)} %copy.16), calls=%async_computation | async-start | bytes 1048576 | tf_op jit(solution)/shard_map/all_to_all | solution.py:123
  48.3 18.5 %copy-start.2 = (bf16[12,128,128]{2,1,0:T(8,128)(2,1)S(1)}, bf16[12,128,128]{2,1,0:T(8,128)(2,1)}, u32[]{:S(2)}) copy-start(bf16[12,128,128]{2,1,0:T(8,128)(2,1)} %shard_map.46) | copy-start | bytes 1179652
  62.4 12.5 %all-to-all-start.1 = ((bf16[256,4,256]{0,2,1:T(8,128)(2,1)}), bf16[256,4,256]{0,2,1:T(8,128)(2,1)S(1)}, u32[]{:S(2)}, u32[]{:S(2)}) async-start(bf16[256,4,256]{0,2,1:T(8,128)(2,1)} %bitcast.20), calls=%async_computation.1 | async-start | bytes 1048576 | tf_op jit(solution)/shard_map/all_to_all | solution.py:129
  66.8 99.1 %all-gather.5.cloned.1.call-start = ((), (), s32[]{:S(2)}) async-start(), calls=%async_computation.5 | async-start | bytes 2359296 | tf_op jit(solution)/shard_map/all_gather | solution.py:126
  74.9 70.3 %all-to-all-start.2 = ((bf16[256,8,1024]{0,2,1:T(8,128)(2,1)}), bf16[256,8,1024]{0,2,1:T(8,128)(2,1)}, u32[]{:S(2)}, u32[]{:S(2)}) async-start(bf16[256,8,1024]{0,2,1:T(8,128)(2,1)} %bitcast.285), calls=%async_computation.2 | async-start | bytes 8388608 | tf_op jit(solution)/shard_map/all_to_all | solution.py:121
  80.3 176.3 %all-gather.3.cloned.1.call-start = ((), (), s32[]{:S(2)}) async-start(), calls=%async_computation.4 | async-start | bytes 4718592 | tf_op jit(solution)/shard_map/all_gather | solution.py:130
  165.9 7.6 %copy-start.1 = (bf16[4,16,128,128]{3,2,1,0:T(8,128)(2,1)S(1)}, bf16[4,16,128,128]{3,2,1,0:T(8,128)(2,1)}, u32[]{:S(2)}) copy-start(bf16[4,16,128,128]{3,2,1,0:T(8,128)(2,1)} %all-gather.5.cloned.1.call-done) | copy-start | bytes 6291460
  165.9 7.9 %copy-start = (bf16[8,256,1024]{2,1,0:T(8,128)(2,1)S(1)}, bf16[8,256,1024]{2,1,0:T(8,128)(2,1)}, u32[]{:S(2)}) copy-start(bf16[8,256,1024]{2,1,0:T(8,128)(2,1)} %copy.19) | copy-start | bytes 12582916
Sparse Core Ops, SparseCore 0:
  69.2 96.5 all-gather.4
  167.5 89.0 all-gather.2

commit v3 on v2

--- a/solution.py
+++ b/solution.py
@@ -55,7 +55,7 @@
         guess[block] = identity * start
 
     def more(state):
-        return state > 2e-2
+        return state > 5e-3
 
     def improve(spread):
         shrunk = spread * spread / (2.0 - spread * spread)
@@ -94,47 +94,303 @@
     return out.reshape(sections, owned, BLK, BLK)
 
 
-def rotate_rows(slab, rotations, distance):
-    halves = slab.shape[0] // HALF
+def halves_dot(value, rotation_of, distance):
+    halves = value.shape[1] // HALF
     parts = [None] * halves
     for low, high, owner in pair_table(distance, halves):
-        joined = jnp.concatenate([slab[low * HALF:(low + 1) * HALF], slab[high * HALF:(high + 1) * HALF]], axis=0)
-        turned = jnp.dot(rotations[owner], joined, preferred_element_type=jnp.float32).astype(jnp.bfloat16)
-        parts[low], parts[high] = turned[:HALF], turned[HALF:]
-    return jnp.concatenate(parts, axis=0)
-
-
-def rotate_cols(rows, rotations, distance):
-    halves = rows.shape[1] // HALF
-    parts = [None] * halves
-    for low, high, owner in pair_table(distance, halves):
-        joined = jnp.concatenate([rows[:, low * HALF:(low + 1) * HALF], rows[:, high * HALF:(high + 1) * HALF]], axis=1)
-        turned = jnp.dot(joined, rotations[owner], preferred_element_type=jnp.float32).astype(jnp.bfloat16)
+        joined = jnp.concatenate([value[:, low * HALF:(low + 1) * HALF], value[:, high * HALF:(high + 1) * HALF]], axis=1)
+        turned = jnp.dot(joined, rotation_of(owner), preferred_element_type=jnp.float32).astype(jnp.bfloat16)
         parts[low], parts[high] = turned[:, :HALF], turned[:, HALF:]
     return jnp.concatenate(parts, axis=1)
 
 
+def place():
+    me = lax.axis_index("tensor")
+    return me, me // 8, (me // 2) % 4, me % 2
+
+
+def remote(src, dst, send, recv, peer):
+    return pltpu.make_async_remote_copy(
+        src_ref=src, dst_ref=dst, send_sem=send, recv_sem=recv,
+        device_id={"tensor": peer}, device_id_type=pl.DeviceIdType.MESH,
+    )
+
+
+def greet(peers):
+    barrier = pltpu.get_barrier_semaphore()
+    for peer in peers:
+        pl.semaphore_signal(barrier, inc=1, device_id={"tensor": peer}, device_id_type=pl.DeviceIdType.MESH)
+    pl.semaphore_wait(barrier, len(peers))
+
+
+def token_kernel(rows_ref, rot_ref, out_ref, rot_z, rot_x, rot_y, first, second, third, landed, send_e, recv_e, send_1, recv_1, send_2, recv_2):
+    me, z, x, y = place()
+    barrier = pltpu.get_barrier_semaphore()
+
+    def signal(step, carry):
+        pl.semaphore_signal(barrier, inc=1, device_id={"tensor": (me + step) % 32}, device_id_type=pl.DeviceIdType.MESH)
+        return carry
+
+    lax.fori_loop(1, 32, signal, 0)
+    pl.semaphore_wait(barrier, 31)
+
+    gathers = []
+    for step in range(1, 4):
+        gathers.append(remote(rot_ref.at[pl.ds(4, 2)], rot_z.at[:, z], send_e.at[step - 1], recv_e.at[step - 1], ((z + step) % 4) * 8 + x * 2 + y))
+    for step in range(1, 4):
+        gathers.append(remote(rot_ref.at[pl.ds(2, 2)], rot_x.at[:, x], send_e.at[2 + step], recv_e.at[2 + step], z * 8 + ((x + step) % 4) * 2 + y))
+    gathers.append(remote(rot_ref.at[pl.ds(0, 2)], rot_y.at[:, y], send_e.at[6], recv_e.at[6], z * 8 + x * 2 + 1 - y))
+    for gather in gathers:
+        gather.start()
+    rot_z[:, z] = rot_ref[4:6]
+    rot_x[:, x] = rot_ref[2:4]
+    rot_y[:, y] = rot_ref[0:2]
+
+    for gather in gathers[:3]:
+        gather.wait_recv()
+    value = rows_ref[...]
+    value = halves_dot(value, lambda k: rot_z[1, k // 2, k % 2], 3)
+    value = halves_dot(value, lambda k: rot_z[0, k // 2, k % 2], 2)
+    for piece in range(4):
+        first[piece] = value[:, piece * 256:(piece + 1) * 256]
+    moves = [remote(first.at[piece], second.at[x], send_1.at[piece], recv_1.at[x], piece * 8 + z * 2 + y) for piece in range(4)]
+    for piece in range(4):
+        @pl.when(jnp.logical_or(z != piece, x != z))
+        def _():
+            moves[piece].start()
+
+    @pl.when(x == z)
+    def _():
+        second[x] = first[z]
+
+    for piece in range(4):
+        @pl.when(jnp.logical_or(z != x, x != piece))
+        def _():
+            remote(first.at[0], second.at[piece], send_1.at[0], recv_1.at[piece], me).wait_recv()
+    for gather in gathers[3:6]:
+        gather.wait_recv()
+    value = jnp.concatenate([second[piece] for piece in range(4)], axis=1)
+    value = halves_dot(value, lambda k: rot_x[1, k // 2, k % 2], 3)
+    value = halves_dot(value, lambda k: rot_x[0, k // 2, k % 2], 2)
+    for piece in range(4):
+        third[piece] = value[:, piece * 256:(piece + 1) * 256]
+    spreads = []
+    for other in range(8):
+        to_x, to_y = other // 2, other % 2
+        spreads.append(remote(third.at[to_x], landed.at[x * 2 + y], send_2.at[other], recv_2.at[x * 2 + y], z * 8 + other))
+    for other in range(8):
+        @pl.when(other != x * 2 + y)
+        def _():
+            spreads[other].start()
+    landed[x * 2 + y] = third[x]
+    gathers[6].wait_recv()
+    for group in range(4):
+        for side in range(2):
+            other = group * 2 + side
+
+            @pl.when(other != x * 2 + y)
+            def _():
+                remote(third.at[0], landed.at[other], send_2.at[0], recv_2.at[other], me).wait_recv()
+        value = jnp.concatenate([landed[group * 2], landed[group * 2 + 1]], axis=1)
+        value = halves_dot(value, lambda k: rot_y[1, k // 2, k % 2], 2)
+        value = halves_dot(value, lambda k: rot_y[0, k // 2, k % 2], 0)
+        out_ref[group] = value
+    for gather in gathers:
+        gather.wait_send()
+    for piece in range(4):
+        @pl.when(jnp.logical_or(z != piece, x != z))
+        def _():
+            moves[piece].wait_send()
+    for other in range(8):
+        @pl.when(other != x * 2 + y)
+        def _():
+            spreads[other].wait_send()
+
+
+def turn_tokens(rows, rotations):
+    bf = jnp.bfloat16
+    return pl.pallas_call(
+        token_kernel,
+        out_shape=jax.ShapeDtypeStruct((4, 256, 512), bf),
+        in_specs=[pl.BlockSpec(memory_space=pltpu.VMEM)] * 2,
+        out_specs=pl.BlockSpec(memory_space=pltpu.VMEM),
+        scratch_shapes=[
+            pltpu.VMEM((2, 4, 2, BLK, BLK), bf),
+            pltpu.VMEM((2, 4, 2, BLK, BLK), bf),
+            pltpu.VMEM((2, 2, 2, BLK, BLK), bf),
+            pltpu.VMEM((4, 256, 256), bf),
+            pltpu.VMEM((4, 256, 256), bf),
+            pltpu.VMEM((4, 256, 256), bf),
+            pltpu.VMEM((8, 256, 256), bf),
+            pltpu.SemaphoreType.DMA((7,)),
+            pltpu.SemaphoreType.DMA((7,)),
+            pltpu.SemaphoreType.DMA((4,)),
+            pltpu.SemaphoreType.DMA((4,)),
+            pltpu.SemaphoreType.DMA((8,)),
+            pltpu.SemaphoreType.DMA((8,)),
+        ],
+        compiler_params=pltpu.CompilerParams(collective_id=1, has_side_effects=True),
+        cost_estimate=pl.CostEstimate(flops=20 * 10**9, bytes_accessed=40 * 2**20, transcendentals=0),
+    )(rows, rotations)
+
+
+def project_kernel(tok_ref, own_ref, other_ref, out_ref, slab, part, far, near, part2, far2, near2, last, swapped, send, recv, send_y, recv_y, load):
+    me, z, x, y = place()
+    coords = (z, x)
+
+    def peer(axis, step):
+        if axis == 0:
+            return ((z + step) % 4) * 8 + x * 2 + y
+        return z * 8 + ((x + step) % 4) * 2 + y
+
+    partner = z * 8 + x * 2 + 1 - y
+    loads = [
+        pltpu.make_async_copy(own_ref.at[:, pl.ds(pl.multiple_of(y * 4096, 4096), 4096)], slab.at[pl.ds(pl.multiple_of(y * 256, 256), 256)], load.at[0]),
+        pltpu.make_async_copy(other_ref, slab.at[pl.ds(pl.multiple_of((1 - y) * 256, 256), 256)], load.at[1]),
+    ]
+    for copy in loads:
+        copy.start()
+    greet([peer(0, 1), peer(0, 3), peer(1, 1), peer(1, 3), partner])
+    for copy in loads:
+        copy.wait()
+
+    def compute(color, role):
+        block = (coords[color] + role) % 4
+        if color == 0:
+            left = tok_ref[block]
+        else:
+            left = jnp.concatenate([tok_ref[group, pl.ds(pl.multiple_of(block * 64, 64), 64), :] for group in range(4)], axis=0)
+
+        def tile(step, carry):
+            at = pl.multiple_of(color * 2048 + step * 512, 512)
+            part[color, role, step] = jnp.dot(left, slab[:, pl.ds(at, 512)], preferred_element_type=jnp.float32).astype(jnp.bfloat16)
+            return carry
+
+        lax.fori_loop(0, 4, tile, 0)
+
+    pending = []
+
+    def ship(stage, color, slot, src, dst, step):
+        axis = color if stage == 0 else 1 - color
+        copy = remote(src, dst, send.at[stage, color, slot], recv.at[stage, color, slot], peer(axis, step))
+        copy.start()
+        pending.append(copy)
+        return copy
+
+    def start_far(stage, color, source, far_buf):
+        up = ship(stage, color, 0, source.at[color, 2, pl.ds(0, 2)], far_buf.at[color, 0], 1)
+        down = ship(stage, color, 1, source.at[color, 2, pl.ds(2, 2)], far_buf.at[color, 1], 3)
+        return up, down
+
+    def start_plain(stage, color, source, near_buf):
+        up = ship(stage, color, 2, source.at[color, 1, pl.ds(2, 2)], near_buf.at[color, 0, pl.ds(2, 2)], 1)
+        down = ship(stage, color, 3, source.at[color, 3, pl.ds(0, 2)], near_buf.at[color, 1, pl.ds(0, 2)], 3)
+        return up, down
+
+    def add(a, b):
+        return (a.astype(jnp.float32) + b.astype(jnp.float32)).astype(jnp.bfloat16)
+
+    def relay(stage, color, source, far_buf, near_buf, fars):
+        fars[0].wait_recv()
+        for tile in range(2):
+            source[color, 1, tile] = add(source[color, 1, tile], far_buf[color, 0, tile])
+        up = ship(stage, color, 4, source.at[color, 1, pl.ds(0, 2)], near_buf.at[color, 0, pl.ds(0, 2)], 1)
+        fars[1].wait_recv()
+        for tile in range(2):
+            source[color, 3, 2 + tile] = add(source[color, 3, 2 + tile], far_buf[color, 1, tile])
+        down = ship(stage, color, 5, source.at[color, 3, pl.ds(2, 2)], near_buf.at[color, 1, pl.ds(2, 2)], 3)
+        return up, down
+
+    fars, plains, relays = {}, {}, {}
+    for color in range(2):
+        compute(color, 2)
+        fars[color] = start_far(0, color, part, far)
+    for color in range(2):
+        for role in (1, 3):
+            compute(color, role)
+        plains[color] = start_plain(0, color, part, near)
+    for color in range(2):
+        compute(color, 0)
+    for color in range(2):
+        relays[color] = relay(0, color, part, far, near, fars[color])
+
+    fars2, plains2, relays2 = {}, {}, {}
+    for color in range(2):
+        for copy in plains[color] + relays[color]:
+            copy.wait_recv()
+        here = coords[1 - color]
+        for role in (2, 1, 3, 0):
+            at = pl.ds(pl.multiple_of((here + role) % 4 * 64, 64), 64)
+            for tile in range(4):
+                total = part[color, 0, tile, at, :].astype(jnp.float32)
+                total = total + near[color, 0, tile, at, :].astype(jnp.float32) + near[color, 1, tile, at, :].astype(jnp.float32)
+                part2[color, role, tile] = total.astype(jnp.bfloat16)
+        fars2[color] = start_far(1, color, part2, far2)
+        plains2[color] = start_plain(1, color, part2, near2)
+    for color in range(2):
+        relays2[color] = relay(1, color, part2, far2, near2, fars2[color])
+    for color in range(2):
+        for copy in plains2[color] + relays2[color]:
+            copy.wait_recv()
+        for tile in range(4):
+            total = part2[color, 0, tile].astype(jnp.float32)
+            total = total + near2[color, 0, tile].astype(jnp.float32) + near2[color, 1, tile].astype(jnp.float32)
+            at = color * 2048 + tile * 512
+            total = total.astype(jnp.bfloat16)
+            last[0, :, at:at + 512] = total[:32]
+            last[1, :, at:at + 512] = total[32:]
+    swap = remote(last.at[1 - y], swapped, send_y, recv_y, partner)
+    swap.start()
+    out_ref[:, pl.ds(pl.multiple_of(y * 4096, 4096), 4096)] = last[y]
+    swap.wait_recv()
+    out_ref[:, pl.ds(pl.multiple_of((1 - y) * 4096, 4096), 4096)] = swapped[...]
+    swap.wait_send()
+    for copy in pending:
+        copy.wait_send()
+
+
+def project(tokens, slab, received):
+    bf = jnp.bfloat16
+    return pl.pallas_call(
+        project_kernel,
+        out_shape=jax.ShapeDtypeStruct((32, 8192), bf),
+        in_specs=[
+            pl.BlockSpec(memory_space=pltpu.VMEM),
+            pl.BlockSpec(memory_space=pl.ANY),
+            pl.BlockSpec(memory_space=pl.ANY),
+        ],
+        out_specs=pl.BlockSpec(memory_space=pltpu.VMEM),
+        scratch_shapes=[
+            pltpu.VMEM((512, 4096), bf),
+            pltpu.VMEM((2, 4, 4, 256, 512), bf),
+            pltpu.VMEM((2, 2, 2, 256, 512), bf),
+            pltpu.VMEM((2, 2, 4, 256, 512), bf),
+            pltpu.VMEM((2, 4, 4, 64, 512), bf),
+            pltpu.VMEM((2, 2, 2, 64, 512), bf),
+            pltpu.VMEM((2, 2, 4, 64, 512), bf),
+            pltpu.VMEM((2, 32, 4096), bf),
+            pltpu.VMEM((32, 4096), bf),
+            pltpu.SemaphoreType.DMA((2, 2, 6)),
+            pltpu.SemaphoreType.DMA((2, 2, 6)),
+            pltpu.SemaphoreType.DMA,
+            pltpu.SemaphoreType.DMA,
+            pltpu.SemaphoreType.DMA((2,)),
+        ],
+        compiler_params=pltpu.CompilerParams(collective_id=2, has_side_effects=True, vmem_limit_bytes=48 * 2**20),
+        cost_estimate=pl.CostEstimate(flops=2 * 1024 * 512 * 4096, bytes_accessed=10 * 2**20, transcendentals=0),
+    )(tokens, slab, received)
+
+
 def shards(weight_slab, token_rows, skew_params, pairing):
+    side = lax.axis_index("tensor") % 2
     plane = [[z * 8 + c for c in range(8)] for z in range(4)]
-    column = [[z * 8 + c for z in range(4)] for c in range(8)]
-    rotations = cayley_blocks(skew_params, pairing)
-    slab = lax.all_to_all(weight_slab, "tensor", split_axis=1, concat_axis=0, axis_index_groups=plane, tiled=True)
+    outgoing = lax.dynamic_slice_in_dim(weight_slab, (1 - side) * 4096, 4096, 1)
+    received = lax.ppermute(outgoing, "tensor", [(d, d ^ 1) for d in range(32)])
     local = token_rows.reshape(32, 4, 8, 256)
     spread = lax.all_to_all(local, "tensor", split_axis=2, concat_axis=0, axis_index_groups=plane, tiled=True)
-    spread = spread.reshape(256, 1024)
-    rot_z = lax.all_gather(rotations[4:], "tensor", axis_index_groups=column, axis=1, tiled=True)
-    rot_xy = lax.all_gather(rotations[:4], "tensor", axis_index_groups=plane, axis=1, tiled=True)
-    spread = rotate_cols(spread, rot_z[1], 3)
-    spread = rotate_cols(spread, rot_z[0], 2)
-    features = lax.all_to_all(spread, "tensor", split_axis=1, concat_axis=0, axis_index_groups=column, tiled=True)
-    features = lax.all_gather(features, "tensor", axis_index_groups=plane, axis=0)
-    for section, distance in enumerate((0, 2, 3, 4)):
-        slab = rotate_rows(slab, rot_xy[section], distance)
-    partial = jnp.einsum("ptf,pfn->tn", features, slab.reshape(8, 256, 1024), preferred_element_type=jnp.float32)
-    partial = partial.astype(jnp.bfloat16)
-    landed = lax.all_to_all(partial, "tensor", split_axis=0, concat_axis=0, tiled=True)
-    landed = landed.reshape(4, 8, 32, 1024).astype(jnp.float32).sum(axis=0)
-    return landed.transpose(1, 0, 2).reshape(32, 8192).astype(jnp.bfloat16)
+    rotations = cayley_blocks(skew_params, pairing)
+    tokens = turn_tokens(spread.reshape(256, 1024), rotations)
+    return project(tokens, weight_slab, received)
 
 
 def solution(mesh):

time: 312 us -> 155 us (0.50)
  waiting for transfers between devices: 127 us -> 0.01 us
  Pallas kernels: 19.4 us -> 139 us
  blocking collectives: 51 us -> 0 us
  local copies, waits for them, and re-layouts: 50.9 us -> 8.19 us
  matrix products: 31.7 us -> 0 us
  between operations: 14.4 us -> 0.05 us
  starting transfers between devices: 14.9 us -> 7.04 us
    pallas_call x0 -> x2, Pallas kernels: none -> 119 us  [the longest x1 69 us: project(): pl.pallas_call(project_kernel, out_shape=jax.ShapeDtypeStruct((32, 8192),...]
    all_to_all x2 -> x0, waiting for transfers between devices: 64.7 us -> none  [the longest x1 63.8 us: shards(): lax.all_to_all(weight_slab, 'tensor', split_axis=1, concat_axis=0, axis_i...]
    all_gather x2 -> x0, waiting for transfers between devices: 62 us -> none  [the longest x1 47.8 us: shards(): lax.all_gather(features, 'tensor', axis_index_groups=plane, axis=0)]
    all_to_all x1 -> x0, blocking collectives: 36.8 us -> none  [shards(): lax.all_to_all(partial, 'tensor', split_axis=0, concat_axis=0, tiled=True)]
    unnamed x55 -> x5, local copies, waits for them, and re-layouts: 37.5 us -> 4.06 us
    dot_general x81 -> x0, matrix products: 31.7 us -> none  [the longest x64 20 us: rotate_rows(): jnp.dot(rotations[owner], joined, preferred_element_type=jnp.float32)]
    all_gather x1 -> x0, blocking collectives: 14.2 us -> none  [shards(): lax.all_gather(rotations[4:], 'tensor', axis_index_groups=column, axis=1,...]
    all_to_all x2 -> x0, starting transfers between devices: 9.87 us -> none  [the longest x1 5.43 us: shards(): lax.all_to_all(weight_slab, 'tensor', split_axis=1, concat_axis=0, axis_i...]
  transfers between devices with their start and end apart: 5 -> 2, of which waited for: 4 -> 0; matrix products, arithmetic and copies ran while one was open for 19% -> 3% of each run, Pallas kernels for 6% -> 45%
where the time goes in v3:
time: 155 us; the launch traced here: 154 us
  Pallas kernels  139 us (90%)
  local copies, waits for them, and re-layouts  8.19 us (5%)
  starting transfers between devices  7.04 us (5%)
    pallas_call x1, Pallas kernels, project(): pl.pallas_call(project_kernel, out_shape=jax.ShapeDtypeStruct((32, 8192),...  69 us
    pallas_call x1, Pallas kernels, turn_tokens(): pl.pallas_call(token_kernel, out_shape=jax.ShapeDtypeStruct((4, 256, 512)...  50.2 us
    pallas_call x1, Pallas kernels, cayley_blocks(): pl.pallas_call(rotation_kernel, out_shape=jax.ShapeDtypeStruct((count, BL...  19.4 us
    all_to_all x1, starting transfers between devices, shards(): lax.all_to_all(local, 'tensor', split_axis=2, concat_axis=0, axis_index_g...  5.02 us
    unnamed x5, local copies, waits for them, and re-layouts  4.06 us
    dynamic_slice x1, local copies, waits for them, and re-layouts, shards(): outgoing = lax.dynamic_slice_in_dim(weight_slab, (1 - side) * 4096, 4096, 1)  3.14 us
  transfers between devices with their start and end apart: 2, of which 0 were waited for; matrix products, arithmetic and copies ran while one was open for 3% of the time, Pallas kernels for 45%

profile of v3, /device:TPU:16, one launch (start us, length us, event | category | flops | bytes accessed | tf_op | source)
XLA Modules:
  0.0 153.8 jit_solution(10177662772085078360)
XLA Ops:
  0.0 1.2 copy.6
  1.2 1.0 copy.5
  2.2 5.0 %all-to-all-start = ((bf16[32,4,8,256]{3,1,0,2:T(4,128)(2,1)}), bf16[32,4,8,256]{3,1,0,2:T(4,128)(2,1)S(1)}, u32[]{:S(2)}, u32[]{:S(2)}) async-start(bf16[32,4,8,256]{3,1,0,2:T(4,128)(2,1)} %copy.5), calls=%async_computation | async-start | bytes 1048576 | tf_op jit(solution)/shard_map/all_to_all | solution.py:390
  7.2 3.1 %constant_dynamic-slice_fusion = bf16[256,4096]{1,0:T(8,128)(2,1)} fusion(bf16[256,8192]{1,0:T(8,128)(2,1)} %own_ref.1, s32[]{:T(128)S(6)} %select_n.11), kind=kLoop, calls=%fused_computation | loop fusion | bytes 4194308 | tf_op jit(solution)/shard_map/dynamic_slice | solution.py:387
  10.3 2.0 %collective-permute-start = (bf16[256,4096]{1,0:T(8,128)(2,1)}, bf16[256,4096]{1,0:T(8,128)(2,1)S(1)}, u32[]{:S(2)}, u32[]{:S(2)}) collective-permute-start(bf16[256,4096]{1,0:T(8,128)(2,1)} %constant_dynamic-slice_fusion), channel_id=1, source_target_pairs={{0,1},{1,0},{2,3},{3,2},{4,5},{5,4},{6,7},{7,6},{8,9},{9,8},{10,11... | collective-permute-start | bytes 6291464 | tf_op jit(solution)/shard_map/ppermute | solution.py:388
  12.3 19.4 %shard_map.46 = bf16[12,128,128]{2,1,0:T(8,128)(2,1)} custom-call(f32[12,128,128]{2,1,0:T(8,128)} %bitcast.16, s32[6,128]{1,0:T(8,128)} %pairing_ref.1), custom_call_target="tpu_custom_call" | custom-call | flops 503316480 | bytes 1179648 | tf_op jit(solution)/shard_map/pallas_call | solution.py:86
  31.7 0.0 all-to-all-done
  31.7 0.9 copy.7
  32.6 50.2 %shard_map.47.tok_ref = bf16[4,256,512]{2,1,0:T(8,128)(2,1)} custom-call(bf16[256,1024]{1,0:T(8,128)(2,1)} %bitcast.15, bf16[6,2,128,128]{3,2,1,0:T(8,128)(2,1)} %bitcast.17), custom_call_target="tpu_custom_call" | custom-call | flops 20000000000 | bytes 41943040 | tf_op jit(solution)/shard_map/pallas_call | solution.py:212
  82.8 0.0 collective-permute-done.other_ref
  82.8 0.0 copy-start
  82.8 1.2 copy-done
  84.0 69.0 %shard_map.48 = bf16[32,8192]{1,0:T(8,128)(2,1)S(1)} custom-call(bf16[4,256,512]{2,1,0:T(8,128)(2,1)S(1)} %copy-done, bf16[256,8192]{1,0:T(8,128)(2,1)} %own_ref.1, bf16[256,4096]{1,0:T(8,128)(2,1)S(1)} %collective-permute-done.other_ref), custom_call_target="tpu_custom_call" | custom-call | flops 4294967296 | bytes 10485760 | tf_op jit(solution)/shard_map/pallas_call | solution.py:354
  153.0 0.8 copy.9
Async XLA Ops:
  2.2 29.6 %all-to-all-start = ((bf16[32,4,8,256]{3,1,0,2:T(4,128)(2,1)}), bf16[32,4,8,256]{3,1,0,2:T(4,128)(2,1)S(1)}, u32[]{:S(2)}, u32[]{:S(2)}) async-start(bf16[32,4,8,256]{3,1,0,2:T(4,128)(2,1)} %copy.5), calls=%async_computation | async-start | bytes 1048576 | tf_op jit(solution)/shard_map/all_to_all | solution.py:390
  10.3 72.5 %collective-permute-start = (bf16[256,4096]{1,0:T(8,128)(2,1)}, bf16[256,4096]{1,0:T(8,128)(2,1)S(1)}, u32[]{:S(2)}, u32[]{:S(2)}) collective-permute-start(bf16[256,4096]{1,0:T(8,128)(2,1)} %constant_dynamic-slice_fusion), channel_id=1, source_target_pairs={{0,1},{1,0},{2,3},{3,2},{4,5},{5,4},{6,7},{7,6},{8,9},{9,8},{10,11... | collective-permute-start | bytes 6291464 | tf_op jit(solution)/shard_map/ppermute | solution.py:388
  82.8 1.2 copy-start

commit v4 on v3

--- a/solution.py
+++ b/solution.py
@@ -42,20 +42,22 @@
     rows = lax.broadcasted_iota(jnp.int32, (BLK, BLK), 0)
     lanes = lax.broadcasted_iota(jnp.int32, (BLK, BLK), 1)
     identity = (rows == lanes).astype(jnp.float32)
-    largest = jnp.zeros((1, BLK), jnp.float32)
+    largest = jnp.zeros((1, 1), jnp.float32)
     for block in range(count):
         raw = skew_ref[block]
         skewed = raw - raw.T
         square = full_dot(skewed, skewed)
         gram[block] = identity - square
-        largest = jnp.maximum(largest, jnp.sum(square * square, axis=0, keepdims=True).sum(axis=1, keepdims=True))
-    top = 1.0 + jnp.sqrt(0.5 * jnp.max(largest)) * 1.0001
+        rounded = square.astype(jnp.bfloat16)
+        fourth = jnp.dot(rounded, rounded, preferred_element_type=jnp.float32)
+        largest = jnp.maximum(largest, jnp.sum(jnp.sum(fourth * fourth, axis=0, keepdims=True), axis=1, keepdims=True))
+    top = 1.0 + 1.02 * jnp.sqrt(jnp.sqrt(0.5 * jnp.max(largest)))
     start = 2.0 / (1.0 + top)
     for block in range(count):
         guess[block] = identity * start
 
     def more(state):
-        return state > 5e-3
+        return state > 1e-2
 
     def improve(spread):
         shrunk = spread * spread / (2.0 - spread * spread)
@@ -72,7 +74,7 @@
         raised = identity + raw - raw.T
         now = guess[block]
         now = now + split_dot(now, identity - full_dot(gram[block], now))
-        rotation = (2.0 * full_dot(now, raised) - identity).astype(jnp.bfloat16)
+        rotation = (2.0 * split_dot(now, raised) - identity).astype(jnp.bfloat16)
         order = pairing_ref[pl.ds(block // 2, 1), :]
         chosen = (rows == order).astype(jnp.bfloat16)
         inner = jnp.dot(chosen, rotation, preferred_element_type=jnp.float32).astype(jnp.bfloat16)
@@ -123,8 +125,9 @@
     pl.semaphore_wait(barrier, len(peers))
 
 
-def token_kernel(rows_ref, rot_ref, out_ref, rot_z, rot_x, rot_y, first, second, third, landed, send_e, recv_e, send_1, recv_1, send_2, recv_2):
+def token_kernel(rows_ref, rot_ref, out_ref, rot_z, rot_x, rot_y, start, first, mid, second, third, landed, send_0, recv_0, send_e, recv_e, send_1, recv_1, send_2, recv_2, send_3, recv_3, send_4, recv_4):
     me, z, x, y = place()
+    spot = x * 2 + y
     barrier = pltpu.get_barrier_semaphore()
 
     def signal(step, carry):
@@ -134,77 +137,105 @@
     lax.fori_loop(1, 32, signal, 0)
     pl.semaphore_wait(barrier, 31)
 
-    gathers = []
-    for step in range(1, 4):
-        gathers.append(remote(rot_ref.at[pl.ds(4, 2)], rot_z.at[:, z], send_e.at[step - 1], recv_e.at[step - 1], ((z + step) % 4) * 8 + x * 2 + y))
-    for step in range(1, 4):
-        gathers.append(remote(rot_ref.at[pl.ds(2, 2)], rot_x.at[:, x], send_e.at[2 + step], recv_e.at[2 + step], z * 8 + ((x + step) % 4) * 2 + y))
-    gathers.append(remote(rot_ref.at[pl.ds(0, 2)], rot_y.at[:, y], send_e.at[6], recv_e.at[6], z * 8 + x * 2 + 1 - y))
-    for gather in gathers:
-        gather.start()
+    def gather(slot, source, target, peer):
+        return remote(source, target, send_e.at[slot], recv_e.at[slot], peer)
+
+    gathers_z = [gather(step - 1, rot_ref.at[pl.ds(4, 2)], rot_z.at[:, z], ((z + step) % 4) * 8 + spot) for step in (1, 3, 2)]
+    gathers_x = [gather(2 + step, rot_ref.at[pl.ds(2, 2)], rot_x.at[:, x], z * 8 + ((x + step) % 4) * 2 + y) for step in (1, 3, 2)]
+    gather_y = gather(6, rot_ref.at[pl.ds(0, 2)], rot_y.at[:, y], z * 8 + x * 2 + 1 - y)
+    for copy in gathers_z:
+        copy.start()
+
+    def piece_of(other, group):
+        at = pl.multiple_of(group * 2048 + other * 256, 256)
+        return rows_ref.at[:, pl.ds(at, 256)]
+
+    for step in range(1, 8):
+        other = (spot + step) % 8
+        for group in range(4):
+            remote(piece_of(other, group), start.at[spot, :, pl.ds(group * 256, 256)], send_0.at[step], recv_0.at[spot], z * 8 + other).start()
+    for group in range(4):
+        start[spot, :, group * 256:(group + 1) * 256] = rows_ref[:, pl.ds(pl.multiple_of(group * 2048 + spot * 256, 256), 256)]
     rot_z[:, z] = rot_ref[4:6]
     rot_x[:, x] = rot_ref[2:4]
     rot_y[:, y] = rot_ref[0:2]
-
-    for gather in gathers[:3]:
-        gather.wait_recv()
-    value = rows_ref[...]
+    for step in range(1, 8):
+        other = (spot + step) % 8
+        remote(start.at[spot], start.at[other], send_0.at[step], recv_0.at[other], me).wait_recv()
+    for copy in gathers_z:
+        copy.wait_recv()
+    for copy in gathers_x:
+        copy.start()
+    gather_y.start()
+    value = jnp.concatenate([start[other] for other in range(8)], axis=0)
     value = halves_dot(value, lambda k: rot_z[1, k // 2, k % 2], 3)
     value = halves_dot(value, lambda k: rot_z[0, k // 2, k % 2], 2)
     for piece in range(4):
         first[piece] = value[:, piece * 256:(piece + 1) * 256]
-    moves = [remote(first.at[piece], second.at[x], send_1.at[piece], recv_1.at[x], piece * 8 + z * 2 + y) for piece in range(4)]
-    for piece in range(4):
-        @pl.when(jnp.logical_or(z != piece, x != z))
+
+    over_z = [remote(first.at[(z + step) % 4], mid.at[z], send_1.at[step], recv_1.at[z], ((z + step) % 4) * 8 + spot) for step in (1, 3, 2)]
+    for copy in over_z:
+        copy.start()
+    mid[z] = first[z]
+
+    def onward(group):
+        return remote(mid.at[group], second.at[x], send_2.at[group], recv_2.at[x], z * 8 + group * 2 + y)
+
+    for step in (0, 3, 1, 2):
+        group = (z + step) % 4
+        if step != 0:
+            remote(first.at[0], mid.at[group], send_1.at[step], recv_1.at[group], me).wait_recv()
+
+        @pl.when(group != x)
         def _():
-            moves[piece].start()
-
-    @pl.when(x == z)
-    def _():
-        second[x] = first[z]
-
-    for piece in range(4):
-        @pl.when(jnp.logical_or(z != x, x != piece))
+            onward(group).start()
+
+        @pl.when(group == x)
         def _():
-            remote(first.at[0], second.at[piece], send_1.at[0], recv_1.at[piece], me).wait_recv()
-    for gather in gathers[3:6]:
-        gather.wait_recv()
+            second[x] = mid[group]
+
+    for step in (1, 3, 2):
+        source = (x + step) % 4
+        remote(mid.at[0], second.at[source], send_2.at[0], recv_2.at[source], me).wait_recv()
+    for copy in gathers_x:
+        copy.wait_recv()
     value = jnp.concatenate([second[piece] for piece in range(4)], axis=1)
     value = halves_dot(value, lambda k: rot_x[1, k // 2, k % 2], 3)
     value = halves_dot(value, lambda k: rot_x[0, k // 2, k % 2], 2)
     for piece in range(4):
         third[piece] = value[:, piece * 256:(piece + 1) * 256]
-    spreads = []
-    for other in range(8):
-        to_x, to_y = other // 2, other % 2
-        spreads.append(remote(third.at[to_x], landed.at[x * 2 + y], send_2.at[other], recv_2.at[x * 2 + y], z * 8 + other))
-    for other in range(8):
-        @pl.when(other != x * 2 + y)
-        def _():
-            spreads[other].start()
-    landed[x * 2 + y] = third[x]
-    gathers[6].wait_recv()
-    for group in range(4):
-        for side in range(2):
-            other = group * 2 + side
-
-            @pl.when(other != x * 2 + y)
-            def _():
-                remote(third.at[0], landed.at[other], send_2.at[0], recv_2.at[other], me).wait_recv()
-        value = jnp.concatenate([landed[group * 2], landed[group * 2 + 1]], axis=1)
+
+    over_x = [remote(third.at[(x + step) % 4], landed.at[y, x], send_3.at[step], recv_3.at[x], z * 8 + ((x + step) % 4) * 2 + y) for step in (1, 3, 2)]
+    for copy in over_x:
+        copy.start()
+    landed[y, x] = third[x]
+
+    def across(group):
+        return remote(landed.at[y, group], landed.at[y, group], send_4.at[group], recv_4.at[group], z * 8 + x * 2 + 1 - y)
+
+    for step in (0, 3, 1, 2):
+        group = (x + step) % 4
+        if step != 0:
+            remote(third.at[0], landed.at[y, group], send_3.at[step], recv_3.at[group], me).wait_recv()
+        across(group).start()
+    gather_y.wait_recv()
+    for step in (0, 3, 1, 2):
+        group = (x + step) % 4
+        remote(landed.at[y, group], landed.at[1 - y, group], send_4.at[group], recv_4.at[group], me).wait_recv()
+        value = jnp.concatenate([landed[0, group], landed[1, group]], axis=1)
         value = halves_dot(value, lambda k: rot_y[1, k // 2, k % 2], 2)
         value = halves_dot(value, lambda k: rot_y[0, k // 2, k % 2], 0)
         out_ref[group] = value
-    for gather in gathers:
-        gather.wait_send()
-    for piece in range(4):
-        @pl.when(jnp.logical_or(z != piece, x != z))
+    for copy in gathers_z + gathers_x + [gather_y] + over_z + over_x:
+        copy.wait_send()
+    for step in range(1, 8):
+        remote(start.at[spot], start.at[spot], send_0.at[step], recv_0.at[spot], me).wait_send()
+    for group in range(4):
+        across(group).wait_send()
+
+        @pl.when(group != x)
         def _():
-            moves[piece].wait_send()
-    for other in range(8):
-        @pl.when(other != x * 2 + y)
-        def _():
-            spreads[other].wait_send()
+            onward(group).wait_send()
 
 
 def turn_tokens(rows, rotations):
@@ -218,20 +249,35 @@
             pltpu.VMEM((2, 4, 2, BLK, BLK), bf),
             pltpu.VMEM((2, 4, 2, BLK, BLK), bf),
             pltpu.VMEM((2, 2, 2, BLK, BLK), bf),
+            pltpu.VMEM((8, 32, 1024), bf),
             pltpu.VMEM((4, 256, 256), bf),
             pltpu.VMEM((4, 256, 256), bf),
             pltpu.VMEM((4, 256, 256), bf),
-            pltpu.VMEM((8, 256, 256), bf),
-            pltpu.SemaphoreType.DMA((7,)),
-            pltpu.SemaphoreType.DMA((7,)),
-            pltpu.SemaphoreType.DMA((4,)),
-            pltpu.SemaphoreType.DMA((4,)),
-            pltpu.SemaphoreType.DMA((8,)),
-            pltpu.SemaphoreType.DMA((8,)),
-        ],
+            pltpu.VMEM((4, 256, 256), bf),
+            pltpu.VMEM((2, 4, 256, 256), bf),
+        ] + [pltpu.SemaphoreType.DMA((count,)) for count in (8, 8, 7, 7, 4, 4, 4, 4, 4, 4, 4, 4)],
         compiler_params=pltpu.CompilerParams(collective_id=1, has_side_effects=True),
         cost_estimate=pl.CostEstimate(flops=20 * 10**9, bytes_accessed=40 * 2**20, transcendentals=0),
     )(rows, rotations)
+
+
+def half_kernel(slab_ref, out_ref, done):
+    side = lax.axis_index("tensor") % 2
+    at = pl.multiple_of((1 - side) * 4096, 4096)
+    copy = pltpu.make_async_copy(slab_ref.at[:, pl.ds(at, 4096)], out_ref, done)
+    copy.start()
+    copy.wait()
+
+
+def partner_half(slab):
+    return pl.pallas_call(
+        half_kernel,
+        out_shape=jax.ShapeDtypeStruct((256, 4096), jnp.bfloat16),
+        in_specs=[pl.BlockSpec(memory_space=pl.ANY)],
+        out_specs=pl.BlockSpec(memory_space=pltpu.VMEM),
+        scratch_shapes=[pltpu.SemaphoreType.DMA],
+        cost_estimate=pl.CostEstimate(flops=0, bytes_accessed=4 * 2**20, transcendentals=0),
+    )(slab)
 
 
 def project_kernel(tok_ref, own_ref, other_ref, out_ref, slab, part, far, near, part2, far2, near2, last, swapped, send, recv, send_y, recv_y, load):
@@ -382,14 +428,9 @@
 
 
 def shards(weight_slab, token_rows, skew_params, pairing):
-    side = lax.axis_index("tensor") % 2
-    plane = [[z * 8 + c for c in range(8)] for z in range(4)]
-    outgoing = lax.dynamic_slice_in_dim(weight_slab, (1 - side) * 4096, 4096, 1)
-    received = lax.ppermute(outgoing, "tensor", [(d, d ^ 1) for d in range(32)])
-    local = token_rows.reshape(32, 4, 8, 256)
-    spread = lax.all_to_all(local, "tensor", split_axis=2, concat_axis=0, axis_index_groups=plane, tiled=True)
+    received = lax.ppermute(partner_half(weight_slab), "tensor", [(d, d ^ 1) for d in range(32)])
     rotations = cayley_blocks(skew_params, pairing)
-    tokens = turn_tokens(spread.reshape(256, 1024), rotations)
+    tokens = turn_tokens(token_rows, rotations)
     return project(tokens, weight_slab, received)
 
 

time: 155 us -> 151 us (0.974)
  Pallas kernels: 139 us -> 147 us
  local copies, waits for them, and re-layouts: 8.19 us -> 2.01 us
  starting transfers between devices: 7.04 us -> 1.36 us
    pallas_call x1, Pallas kernels: 50.2 us -> 65 us  [turn_tokens(): pl.pallas_call(token_kernel, out_shape=jax.ShapeDtypeStruct((4, 256, 512)...]
    pallas_call x1, Pallas kernels: 69 us -> 59.6 us  [project(): pl.pallas_call(project_kernel, out_shape=jax.ShapeDtypeStruct((32, 8192),...]
    all_to_all x1 -> x0, starting transfers between devices: 5.02 us -> none  [shards(): lax.all_to_all(local, 'tensor', split_axis=2, concat_axis=0, axis_index_g...]
    dynamic_slice x1 -> x0, local copies, waits for them, and re-layouts: 3.14 us -> none  [shards(): outgoing = lax.dynamic_slice_in_dim(weight_slab, (1 - side) * 4096, 4096, 1)]
    pallas_call x0 -> x1, Pallas kernels: none -> 2.94 us  [partner_half(): pl.pallas_call(half_kernel, out_shape=jax.ShapeDtypeStruct((256, 4096), j...]
    unnamed x5 -> x3, local copies, waits for them, and re-layouts: 4.06 us -> 2.01 us
  transfers between devices with their start and end apart: 2 -> 1, of which waited for: 0 -> 0; matrix products, arithmetic and copies ran while one was open for 3% -> 0% of each run, Pallas kernels for 45% -> 56%
where the time goes in v4:
time: 151 us
  Pallas kernels  147 us (97%)
  local copies, waits for them, and re-layouts  2.01 us (1%)
    pallas_call x1, Pallas kernels, turn_tokens(): pl.pallas_call(token_kernel, out_shape=jax.ShapeDtypeStruct((4, 256, 512)...  65 us
    pallas_call x1, Pallas kernels, project(): pl.pallas_call(project_kernel, out_shape=jax.ShapeDtypeStruct((32, 8192),...  59.6 us
    pallas_call x1, Pallas kernels, cayley_blocks(): pl.pallas_call(rotation_kernel, out_shape=jax.ShapeDtypeStruct((count, BL...  19.6 us
  transfers between devices with their start and end apart: 1, of which 0 were waited for; matrix products, arithmetic and copies ran while one was open for 0% of the time, Pallas kernels for 56%

profile of v4, /device:TPU:16, one launch (start us, length us, event | category | flops | bytes accessed | tf_op | source)
XLA Modules:
  0.0 150.5 jit_solution(3201054867792641017)
XLA Ops:
  0.0 2.9 %shard_map.48 = bf16[256,4096]{1,0:T(8,128)(2,1)} custom-call(bf16[256,8192]{1,0:T(8,128)(2,1)} %own_ref.1), custom_call_target="tpu_custom_call" | custom-call | bytes 4194304 | tf_op jit(solution)/shard_map/pallas_call | solution.py:273
  2.9 1.4 collective-permute-start
  4.3 19.6 %shard_map.46 = bf16[12,128,128]{2,1,0:T(8,128)(2,1)} custom-call(f32[12,128,128]{2,1,0:T(8,128)} %bitcast.2, s32[6,128]{1,0:T(8,128)} %pairing_ref.1), custom_call_target="tpu_custom_call" | custom-call | flops 503316480 | bytes 1179648 | tf_op jit(solution)/shard_map/pallas_call | solution.py:88
  23.9 65.0 %shard_map.47.tok_ref = bf16[4,256,512]{2,1,0:T(8,128)(2,1)} custom-call(bf16[32,8192]{1,0:T(8,128)(2,1)} %rows_ref.1, bf16[6,2,128,128]{3,2,1,0:T(8,128)(2,1)} %bitcast.3), custom_call_target="tpu_custom_call" | custom-call | flops 20000000000 | bytes 41943040 | tf_op jit(solution)/shard_map/pallas_call | solution.py:243
  88.9 0.0 collective-permute-done.other_ref
  88.9 0.0 copy-start
  88.9 1.2 copy-done
  90.1 59.6 %shard_map.49 = bf16[32,8192]{1,0:T(8,128)(2,1)S(1)} custom-call(bf16[4,256,512]{2,1,0:T(8,128)(2,1)S(1)} %copy-done, bf16[256,8192]{1,0:T(8,128)(2,1)} %own_ref.1, bf16[256,4096]{1,0:T(8,128)(2,1)S(1)} %collective-permute-done.other_ref), custom_call_target="tpu_custom_call" | custom-call | flops 4294967296 | bytes 10485760 | tf_op jit(solution)/shard_map/pallas_call | solution.py:400
  149.7 0.8 copy.6
Async XLA Ops:
  2.9 85.9 %collective-permute-start = (bf16[256,4096]{1,0:T(8,128)(2,1)}, bf16[256,4096]{1,0:T(8,128)(2,1)S(1)}, u32[]{:S(2)}, u32[]{:S(2)}) collective-permute-start(bf16[256,4096]{1,0:T(8,128)(2,1)} %shard_map.48), channel_id=1, source_target_pairs={{0,1},{1,0},{2,3},{3,2},{4,5},{5,4},{6,7},{7,6},{8,9},{9,8},{10,11... | collective-permute-start | bytes 6291464 | tf_op jit(solution)/shard_map/ppermute | solution.py:431
  88.9 1.2 copy-start

commit v5 on v4

--- a/solution.py
+++ b/solution.py
@@ -21,23 +21,28 @@
     return rows
 
 
-def split_dot(left, right):
-    left_hi = left.astype(jnp.bfloat16)
-    left_lo = (left - left_hi.astype(jnp.float32)).astype(jnp.bfloat16)
-    right_hi = right.astype(jnp.bfloat16)
-    right_lo = (right - right_hi.astype(jnp.float32)).astype(jnp.bfloat16)
-    return jnp.dot(
-        jnp.concatenate([left_hi, left_hi, left_lo], axis=1),
-        jnp.concatenate([right_hi, right_lo, right_hi], axis=0),
-        preferred_element_type=jnp.float32,
-    )
+def split(value):
+    high = value.astype(jnp.bfloat16)
+    return high, (value - high.astype(jnp.float32)).astype(jnp.bfloat16)
+
+
+def as_left(high, low):
+    return jnp.concatenate([high, high, low], axis=1)
+
+
+def as_right(high, low):
+    return jnp.concatenate([high, low, high], axis=0)
+
+
+def wide_dot(left, right):
+    return jnp.dot(left, right, preferred_element_type=jnp.float32)
 
 
 def full_dot(left, right):
     return jnp.dot(left, right, precision=lax.Precision.HIGHEST, preferred_element_type=jnp.float32)
 
 
-def rotation_kernel(skew_ref, pairing_ref, out_ref, gram, guess):
+def rotation_kernel(skew_ref, pairing_ref, out_ref, gram, gram_left, guess):
     count = gram.shape[0]
     rows = lax.broadcasted_iota(jnp.int32, (BLK, BLK), 0)
     lanes = lax.broadcasted_iota(jnp.int32, (BLK, BLK), 1)
@@ -47,7 +52,9 @@
         raw = skew_ref[block]
         skewed = raw - raw.T
         square = full_dot(skewed, skewed)
-        gram[block] = identity - square
+        shifted = identity - square
+        gram[block] = shifted
+        gram_left[block] = as_left(*split(shifted))
         rounded = square.astype(jnp.bfloat16)
         fourth = jnp.dot(rounded, rounded, preferred_element_type=jnp.float32)
         largest = jnp.maximum(largest, jnp.sum(jnp.sum(fourth * fourth, axis=0, keepdims=True), axis=1, keepdims=True))
@@ -63,23 +70,29 @@
         shrunk = spread * spread / (2.0 - spread * spread)
         scale = 2.0 / (2.0 - spread * spread)
         for block in range(count):
+            high, low = split(guess[block])
+            left = 2.0 * identity - wide_dot(gram_left[block], as_right(high, low))
+            guess[block] = scale * wide_dot(as_left(high, low), as_right(*split(left)))
+        return shrunk
+
+    lax.while_loop(more, improve, (top - 1.0) / (top + 1.0))
+    for section in range(count // 2):
+        turned = []
+        for block in (2 * section, 2 * section + 1):
+            raw = skew_ref[block]
+            raised = identity + raw - raw.T
             now = guess[block]
-            left = 2.0 * identity - split_dot(gram[block], now)
-            guess[block] = scale * split_dot(now, left)
-        return shrunk
-
-    lax.while_loop(more, improve, (top - 1.0) / (top + 1.0))
-    for block in range(count):
-        raw = skew_ref[block]
-        raised = identity + raw - raw.T
-        now = guess[block]
-        now = now + split_dot(now, identity - full_dot(gram[block], now))
-        rotation = (2.0 * split_dot(now, raised) - identity).astype(jnp.bfloat16)
-        order = pairing_ref[pl.ds(block // 2, 1), :]
-        chosen = (rows == order).astype(jnp.bfloat16)
-        inner = jnp.dot(chosen, rotation, preferred_element_type=jnp.float32).astype(jnp.bfloat16)
-        outer = lax.dot_general(inner, chosen, (((1,), (1,)), ((), ())), preferred_element_type=jnp.float32)
-        out_ref[block] = outer.astype(jnp.bfloat16)
+            miss = identity - full_dot(gram[block], now)
+            now = now + wide_dot(as_left(*split(now)), as_right(*split(miss)))
+            rotation = 2.0 * wide_dot(as_left(*split(now)), as_right(*split(raised))) - identity
+            turned.append(rotation.astype(jnp.bfloat16))
+        order = pairing_ref[pl.ds(section, 1), :]
+        chosen = (rows == order).astype(jnp.float32)
+        inner = wide_dot(chosen.astype(jnp.bfloat16), jnp.concatenate(turned, axis=1)).astype(jnp.bfloat16)
+        stacked = jnp.concatenate([inner[:, :BLK], inner[:, BLK:]], axis=0)
+        outer = wide_dot(stacked, chosen.T.astype(jnp.bfloat16)).astype(jnp.bfloat16)
+        out_ref[2 * section] = outer[:BLK]
+        out_ref[2 * section + 1] = outer[BLK:]
 
 
 def cayley_blocks(skew_params, pairing):
@@ -90,7 +103,11 @@
         out_shape=jax.ShapeDtypeStruct((count, BLK, BLK), jnp.bfloat16),
         in_specs=[pl.BlockSpec(memory_space=pltpu.VMEM)] * 2,
         out_specs=pl.BlockSpec(memory_space=pltpu.VMEM),
-        scratch_shapes=[pltpu.VMEM((count, BLK, BLK), jnp.float32)] * 2,
+        scratch_shapes=[
+            pltpu.VMEM((count, BLK, BLK), jnp.float32),
+            pltpu.VMEM((count, BLK, 3 * BLK), jnp.bfloat16),
+            pltpu.VMEM((count, BLK, BLK), jnp.float32),
+        ],
         cost_estimate=pl.CostEstimate(flops=count * BLK**3 * 20, bytes_accessed=count * BLK * BLK * 6, transcendentals=0),
     )(skew_params.reshape(count, BLK, BLK), pairing)
     return out.reshape(sections, owned, BLK, BLK)
@@ -125,17 +142,11 @@
     pl.semaphore_wait(barrier, len(peers))
 
 
-def token_kernel(rows_ref, rot_ref, out_ref, rot_z, rot_x, rot_y, start, first, mid, second, third, landed, send_0, recv_0, send_e, recv_e, send_1, recv_1, send_2, recv_2, send_3, recv_3, send_4, recv_4):
+def token_kernel(rows_ref, rot_ref, slab_ref, out_ref, late_ref, rot_z, rot_x, rot_y, start, first, mid, second, third, landed, send_0, recv_0, send_e, recv_e, send_1, recv_1, send_2, recv_2, send_3, recv_3, send_4, recv_4, send_w, recv_w):
     me, z, x, y = place()
     spot = x * 2 + y
-    barrier = pltpu.get_barrier_semaphore()
-
-    def signal(step, carry):
-        pl.semaphore_signal(barrier, inc=1, device_id={"tensor": (me + step) % 32}, device_id_type=pl.DeviceIdType.MESH)
-        return carry
-
-    lax.fori_loop(1, 32, signal, 0)
-    pl.semaphore_wait(barrier, 31)
+    partner = z * 8 + x * 2 + 1 - y
+    greet([((z + step) % 4) * 8 + spot for step in range(1, 4)] + [z * 8 + (spot + step) % 8 for step in range(1, 8)])
 
     def gather(slot, source, target, peer):
         return remote(source, target, send_e.at[slot], recv_e.at[slot], peer)
@@ -154,6 +165,10 @@
         other = (spot + step) % 8
         for group in range(4):
             remote(piece_of(other, group), start.at[spot, :, pl.ds(group * 256, 256)], send_0.at[step], recv_0.at[spot], z * 8 + other).start()
+    gather_y.start()
+    late = pl.multiple_of((1 - y) * 4096 + 2048, 2048)
+    rest = remote(slab_ref.at[:, pl.ds(late, 2048)], late_ref, send_w, recv_w, partner)
+    rest.start()
     for group in range(4):
         start[spot, :, group * 256:(group + 1) * 256] = rows_ref[:, pl.ds(pl.multiple_of(group * 2048 + spot * 256, 256), 256)]
     rot_z[:, z] = rot_ref[4:6]
@@ -166,7 +181,6 @@
         copy.wait_recv()
     for copy in gathers_x:
         copy.start()
-    gather_y.start()
     value = jnp.concatenate([start[other] for other in range(8)], axis=0)
     value = halves_dot(value, lambda k: rot_z[1, k // 2, k % 2], 3)
     value = halves_dot(value, lambda k: rot_z[0, k // 2, k % 2], 2)
@@ -226,7 +240,8 @@
         value = halves_dot(value, lambda k: rot_y[1, k // 2, k % 2], 2)
         value = halves_dot(value, lambda k: rot_y[0, k // 2, k % 2], 0)
         out_ref[group] = value
-    for copy in gathers_z + gathers_x + [gather_y] + over_z + over_x:
+    rest.wait_recv()
+    for copy in gathers_z + gathers_x + [gather_y, rest] + over_z + over_x:
         copy.wait_send()
     for step in range(1, 8):
         remote(start.at[spot], start.at[spot], send_0.at[step], recv_0.at[spot], me).wait_send()
@@ -238,13 +253,13 @@
             onward(group).wait_send()
 
 
-def turn_tokens(rows, rotations):
+def turn_tokens(rows, rotations, slab):
     bf = jnp.bfloat16
     return pl.pallas_call(
         token_kernel,
-        out_shape=jax.ShapeDtypeStruct((4, 256, 512), bf),
-        in_specs=[pl.BlockSpec(memory_space=pltpu.VMEM)] * 2,
-        out_specs=pl.BlockSpec(memory_space=pltpu.VMEM),
+        out_shape=(jax.ShapeDtypeStruct((4, 256, 512), bf), jax.ShapeDtypeStruct((256, 2048), bf)),
+        in_specs=[pl.BlockSpec(memory_space=pltpu.VMEM)] * 2 + [pl.BlockSpec(memory_space=pl.ANY)],
+        out_specs=(pl.BlockSpec(memory_space=pltpu.VMEM), pl.BlockSpec(memory_space=pl.ANY)),
         scratch_shapes=[
             pltpu.VMEM((2, 4, 2, BLK, BLK), bf),
             pltpu.VMEM((2, 4, 2, BLK, BLK), bf),
@@ -255,16 +270,16 @@
             pltpu.VMEM((4, 256, 256), bf),
             pltpu.VMEM((4, 256, 256), bf),
             pltpu.VMEM((2, 4, 256, 256), bf),
-        ] + [pltpu.SemaphoreType.DMA((count,)) for count in (8, 8, 7, 7, 4, 4, 4, 4, 4, 4, 4, 4)],
+        ] + [pltpu.SemaphoreType.DMA((count,)) for count in (8, 8, 7, 7, 4, 4, 4, 4, 4, 4, 4, 4)] + [pltpu.SemaphoreType.DMA] * 2,
         compiler_params=pltpu.CompilerParams(collective_id=1, has_side_effects=True),
         cost_estimate=pl.CostEstimate(flops=20 * 10**9, bytes_accessed=40 * 2**20, transcendentals=0),
-    )(rows, rotations)
+    )(rows, rotations, slab)
 
 
 def half_kernel(slab_ref, out_ref, done):
     side = lax.axis_index("tensor") % 2
     at = pl.multiple_of((1 - side) * 4096, 4096)
-    copy = pltpu.make_async_copy(slab_ref.at[:, pl.ds(at, 4096)], out_ref, done)
+    copy = pltpu.make_async_copy(slab_ref.at[:, pl.ds(at, 2048)], out_ref, done)
     copy.start()
     copy.wait()
 
@@ -272,7 +287,7 @@
 def partner_half(slab):
     return pl.pallas_call(
         half_kernel,
-        out_shape=jax.ShapeDtypeStruct((256, 4096), jnp.bfloat16),
+        out_shape=jax.ShapeDtypeStruct((256, 2048), jnp.bfloat16),
         in_specs=[pl.BlockSpec(memory_space=pl.ANY)],
         out_specs=pl.BlockSpec(memory_space=pltpu.VMEM),
         scratch_shapes=[pltpu.SemaphoreType.DMA],
@@ -280,7 +295,7 @@
     )(slab)
 
 
-def project_kernel(tok_ref, own_ref, other_ref, out_ref, slab, part, far, near, part2, far2, near2, last, swapped, send, recv, send_y, recv_y, load):
+def project_kernel(tok_hbm, own_ref, early_ref, late_ref, out_ref, slab, part, far, near, part2, far2, near2, last, swapped, tok_ref, send, recv, send_y, recv_y, load):
     me, z, x, y = place()
     coords = (z, x)
 
@@ -292,8 +307,10 @@
     partner = z * 8 + x * 2 + 1 - y
     loads = [
         pltpu.make_async_copy(own_ref.at[:, pl.ds(pl.multiple_of(y * 4096, 4096), 4096)], slab.at[pl.ds(pl.multiple_of(y * 256, 256), 256)], load.at[0]),
-        pltpu.make_async_copy(other_ref, slab.at[pl.ds(pl.multiple_of((1 - y) * 256, 256), 256)], load.at[1]),
+        pltpu.make_async_copy(early_ref, slab.at[pl.ds(pl.multiple_of((1 - y) * 256, 256), 256), pl.ds(0, 2048)], load.at[1]),
+        pltpu.make_async_copy(late_ref, slab.at[pl.ds(pl.multiple_of((1 - y) * 256, 256), 256), pl.ds(2048, 2048)], load.at[2]),
     ]
+    loads.append(pltpu.make_async_copy(tok_hbm, tok_ref, load.at[3]))
     for copy in loads:
         copy.start()
     greet([peer(0, 1), peer(0, 3), peer(1, 1), peer(1, 3), partner])
@@ -395,15 +412,16 @@
         copy.wait_send()
 
 
-def project(tokens, slab, received):
+def project(tokens, slab, early, late):
     bf = jnp.bfloat16
     return pl.pallas_call(
         project_kernel,
         out_shape=jax.ShapeDtypeStruct((32, 8192), bf),
         in_specs=[
-            pl.BlockSpec(memory_space=pltpu.VMEM),
+            pl.BlockSpec(memory_space=pltpu.HBM),
+            pl.BlockSpec(memory_space=pltpu.HBM),
             pl.BlockSpec(memory_space=pl.ANY),
-            pl.BlockSpec(memory_space=pl.ANY),
+            pl.BlockSpec(memory_space=pltpu.HBM),
         ],
         out_specs=pl.BlockSpec(memory_space=pltpu.VMEM),
         scratch_shapes=[
@@ -416,22 +434,23 @@
             pltpu.VMEM((2, 2, 4, 64, 512), bf),
             pltpu.VMEM((2, 32, 4096), bf),
             pltpu.VMEM((32, 4096), bf),
+            pltpu.VMEM((4, 256, 512), bf),
             pltpu.SemaphoreType.DMA((2, 2, 6)),
             pltpu.SemaphoreType.DMA((2, 2, 6)),
             pltpu.SemaphoreType.DMA,
             pltpu.SemaphoreType.DMA,
-            pltpu.SemaphoreType.DMA((2,)),
+            pltpu.SemaphoreType.DMA((4,)),
         ],
         compiler_params=pltpu.CompilerParams(collective_id=2, has_side_effects=True, vmem_limit_bytes=48 * 2**20),
         cost_estimate=pl.CostEstimate(flops=2 * 1024 * 512 * 4096, bytes_accessed=10 * 2**20, transcendentals=0),
-    )(tokens, slab, received)
+    )(tokens, slab, early, late)
 
 
 def shards(weight_slab, token_rows, skew_params, pairing):
-    received = lax.ppermute(partner_half(weight_slab), "tensor", [(d, d ^ 1) for d in range(32)])
+    early = lax.ppermute(partner_half(weight_slab), "tensor", [(d, d ^ 1) for d in range(32)])
     rotations = cayley_blocks(skew_params, pairing)
-    tokens = turn_tokens(token_rows, rotations)
-    return project(tokens, weight_slab, received)
+    tokens, late = turn_tokens(token_rows, rotations, weight_slab)
+    return project(tokens, weight_slab, early, late)
 
 
 def solution(mesh):

time: 151 us -> 134 us (0.89)
  Pallas kernels: 147 us -> 129 us
    pallas_call x2, Pallas kernels: 67.9 us -> 52.7 us  [the longest x1 50.5 us: turn_tokens(): pl.pallas_call(token_kernel, out_shape=(jax.ShapeDtypeStruct((4, 256, 512...]
    pallas_call x1, Pallas kernels: 19.6 us -> 17.6 us  [cayley_blocks(): pl.pallas_call(rotation_kernel, out_shape=jax.ShapeDtypeStruct((count, BL...]
    unnamed x3 -> x5, local copies, waits for them, and re-layouts: 2.01 us -> 3.24 us
  transfers between devices with their start and end apart: 1 -> 1, of which waited for: 0 -> 0; matrix products, arithmetic and copies ran while one was open for 0% -> 0% of each run, Pallas kernels for 56% -> 51%
where the time goes in v5:
time: 134 us
  Pallas kernels  129 us (96%)
  local copies, waits for them, and re-layouts  3.24 us (2%)
  starting transfers between devices  1.36 us (1%)
    pallas_call x1, Pallas kernels, project(): pl.pallas_call(project_kernel, out_shape=jax.ShapeDtypeStruct((32, 8192),...  58.9 us
    pallas_call x1, Pallas kernels, turn_tokens(): pl.pallas_call(token_kernel, out_shape=(jax.ShapeDtypeStruct((4, 256, 512...  50.5 us
    pallas_call x1, Pallas kernels, cayley_blocks(): pl.pallas_call(rotation_kernel, out_shape=jax.ShapeDtypeStruct((count, BL...  17.6 us
    unnamed x5, local copies, waits for them, and re-layouts  3.24 us
  transfers between devices with their start and end apart: 1, of which 0 were waited for; matrix products, arithmetic and copies ran while one was open for 0% of the time, Pallas kernels for 51%

profile of v5, /device:TPU:16, one launch (start us, length us, event | category | flops | bytes accessed | tf_op | source)
XLA Modules:
  0.0 133.8 jit_solution(18186352269940232888)
XLA Ops:
  0.0 2.2 %shard_map.48 = bf16[256,2048]{1,0:T(8,128)(2,1)} custom-call(bf16[256,8192]{1,0:T(8,128)(2,1)} %own_ref.1), custom_call_target="tpu_custom_call" | custom-call | bytes 4194304 | tf_op jit(solution)/shard_map/pallas_call | solution.py:288
  2.2 1.4 %collective-permute-start = (bf16[256,2048]{1,0:T(8,128)(2,1)}, bf16[256,2048]{1,0:T(8,128)(2,1)S(1)}, u32[]{:S(2)}, u32[]{:S(2)}) collective-permute-start(bf16[256,2048]{1,0:T(8,128)(2,1)} %shard_map.48), channel_id=1, source_target_pairs={{0,1},{1,0},{2,3},{3,2},{4,5},{5,4},{6,7},{7,6},{8,9},{9,8},{10,11... | collective-permute-start | bytes 3145736 | tf_op jit(solution)/shard_map/ppermute | solution.py:450
  3.6 17.6 %shard_map.46 = bf16[12,128,128]{2,1,0:T(8,128)(2,1)} custom-call(f32[12,128,128]{2,1,0:T(8,128)} %bitcast.2, s32[6,128]{1,0:T(8,128)} %pairing_ref.1), custom_call_target="tpu_custom_call" | custom-call | flops 503316480 | bytes 1179648 | tf_op jit(solution)/shard_map/pallas_call | solution.py:101
  21.2 50.5 %shard_map.47 = (bf16[4,256,512]{2,1,0:T(8,128)(2,1)}, bf16[256,2048]{1,0:T(8,128)(2,1)}) custom-call(bf16[32,8192]{1,0:T(8,128)(2,1)} %rows_ref.1, bf16[6,2,128,128]{3,2,1,0:T(8,128)(2,1)} %bitcast.3, bf16[256,8192]{1,0:T(8,128)(2,1)} %own_ref.1), custom_call_target="tpu_custom_call" | custom-call | flops 20000000000 | bytes 41943040 | tf_op jit(solution)/shard_map/pallas_call | solution.py:258
  71.7 0.0 collective-permute-done.early_ref
  71.7 0.0 copy-start
  71.7 1.2 copy-done
  72.9 0.0 copy-start.1
  72.9 1.2 copy-done.1
  74.1 58.9 %shard_map.49 = bf16[32,8192]{1,0:T(8,128)(2,1)S(1)} custom-call(bf16[4,256,512]{2,1,0:T(8,128)(2,1)S(1)} %copy-done, bf16[256,8192]{1,0:T(8,128)(2,1)} %own_ref.1, bf16[256,2048]{1,0:T(8,128)(2,1)S(1)} %collective-permute-done.early_ref, bf16[256,2048]{1,0:T(8,128)(2,1)S(1)} %copy-done.1), custom_call_target="tpu_custom_call" | custom-call | flops 4294967296 | bytes 10485760 | tf_op jit(solution)/shard_map/pallas_call | solution.py:417
  133.0 0.8 copy.6
Async XLA Ops:
  2.2 69.4 %collective-permute-start = (bf16[256,2048]{1,0:T(8,128)(2,1)}, bf16[256,2048]{1,0:T(8,128)(2,1)S(1)}, u32[]{:S(2)}, u32[]{:S(2)}) collective-permute-start(bf16[256,2048]{1,0:T(8,128)(2,1)} %shard_map.48), channel_id=1, source_target_pairs={{0,1},{1,0},{2,3},{3,2},{4,5},{5,4},{6,7},{7,6},{8,9},{9,8},{10,11... | collective-permute-start | bytes 3145736 | tf_op jit(solution)/shard_map/ppermute | solution.py:450
  71.7 1.2 copy-start
  72.9 1.2 copy-start.1

commit v6 on v5

v6 whole, which is shorter than its diff:
```python
import jax
import jax.numpy as jnp
import numpy as np
from jax import lax
from jax.experimental import pallas as pl
from jax.experimental.pallas import tpu as pltpu
from jax.sharding import PartitionSpec as P

HALF = 64
BLK = 128


def pair_table(distance, count):
    stride = 1 << distance
    rows = []
    for group in range(count // (2 * stride)):
        for offset in range(stride):
            low = group * 2 * stride + offset
            member = low if low >> 1 & 1 == 0 else low + stride
            rows.append((low, low + stride, (member >> 2) * 2 + (member & 1)))
    return rows


def split(value):
    high = value.astype(jnp.bfloat16)
    return high, (value - high.astype(jnp.float32)).astype(jnp.bfloat16)


def as_left(high, low):
    return jnp.concatenate([high, high, low], axis=1)


def as_right(high, low):
    return jnp.concatenate([high, low, high], axis=0)


def wide_dot(left, right):
    return jnp.dot(left, right, preferred_element_type=jnp.float32)


def full_dot(left, right):
    return jnp.dot(left, right, precision=lax.Precision.HIGHEST, preferred_element_type=jnp.float32)


def rotation_kernel(skew_ref, pairing_ref, out_ref, gram, gram_left, guess):
    count = gram.shape[0]
    rows = lax.broadcasted_iota(jnp.int32, (BLK, BLK), 0)
    lanes = lax.broadcasted_iota(jnp.int32, (BLK, BLK), 1)
    identity = (rows == lanes).astype(jnp.float32)
    largest = jnp.zeros((1, 1), jnp.float32)
    for block in range(count):
        raw = skew_ref[block]
        skewed = raw - raw.T
        square = full_dot(skewed, skewed)
        shifted = identity - square
        gram[block] = shifted
        gram_left[block] = as_left(*split(shifted))
        rounded = square.astype(jnp.bfloat16)
        fourth = jnp.dot(rounded, rounded, preferred_element_type=jnp.float32)
        largest = jnp.maximum(largest, jnp.sum(jnp.sum(fourth * fourth, axis=0, keepdims=True), axis=1, keepdims=True))
    top = 1.0 + 1.02 * jnp.sqrt(jnp.sqrt(0.5 * jnp.max(largest)))
    start = 2.0 / (1.0 + top)
    for block in range(count):
        guess[block] = identity * start

    def more(state):
        return state > 1e-2

    def improve(spread):
        shrunk = spread * spread / (2.0 - spread * spread)
        scale = 2.0 / (2.0 - spread * spread)
        for block in range(count):
            high, low = split(guess[block])
            left = 2.0 * identity - wide_dot(gram_left[block], as_right(high, low))
            guess[block] = scale * wide_dot(as_left(high, low), as_right(*split(left)))
        return shrunk

    lax.while_loop(more, improve, (top - 1.0) / (top + 1.0))
    for section in range(count // 2):
        turned = []
        for block in (2 * section, 2 * section + 1):
            raw = skew_ref[block]
            raised = identity + raw - raw.T
            now = guess[block]
            miss = identity - full_dot(gram[block], now)
            now = now + wide_dot(as_left(*split(now)), as_right(*split(miss)))
            rotation = 2.0 * wide_dot(as_left(*split(now)), as_right(*split(raised))) - identity
            turned.append(rotation.astype(jnp.bfloat16))
        order = pairing_ref[pl.ds(section, 1), :]
        chosen = (rows == order).astype(jnp.float32)
        inner = wide_dot(chosen.astype(jnp.bfloat16), jnp.concatenate(turned, axis=1)).astype(jnp.bfloat16)
        stacked = jnp.concatenate([inner[:, :BLK], inner[:, BLK:]], axis=0)
        outer = wide_dot(stacked, chosen.T.astype(jnp.bfloat16)).astype(jnp.bfloat16)
        out_ref[2 * section] = outer[:BLK]
        out_ref[2 * section + 1] = outer[BLK:]


def cayley_blocks(skew_params, pairing):
    sections, owned = skew_params.shape[:2]
    count = sections * owned
    out = pl.pallas_call(
        rotation_kernel,
        out_shape=jax.ShapeDtypeStruct((count, BLK, BLK), jnp.bfloat16),
        in_specs=[pl.BlockSpec(memory_space=pltpu.VMEM)] * 2,
        out_specs=pl.BlockSpec(memory_space=pltpu.VMEM),
        scratch_shapes=[
            pltpu.VMEM((count, BLK, BLK), jnp.float32),
            pltpu.VMEM((count, BLK, 3 * BLK), jnp.bfloat16),
            pltpu.VMEM((count, BLK, BLK), jnp.float32),
        ],
        cost_estimate=pl.CostEstimate(flops=count * BLK**3 * 20, bytes_accessed=count * BLK * BLK * 6, transcendentals=0),
    )(skew_params.reshape(count, BLK, BLK), pairing)
    return out.reshape(sections, owned, BLK, BLK)


def halves_dot(value, rotation_of, distance):
    halves = value.shape[1] // HALF
    parts = [None] * halves
    for low, high, owner in pair_table(distance, halves):
        joined = jnp.concatenate([value[:, low * HALF:(low + 1) * HALF], value[:, high * HALF:(high + 1) * HALF]], axis=1)
        turned = jnp.dot(joined, rotation_of(owner), preferred_element_type=jnp.float32).astype(jnp.bfloat16)
        parts[low], parts[high] = turned[:, :HALF], turned[:, HALF:]
    return jnp.concatenate(parts, axis=1)


def place():
    me = lax.axis_index("tensor")
    return me, me // 8, (me // 2) % 4, me % 2


def remote(src, dst, send, recv, peer):
    return pltpu.make_async_remote_copy(
        src_ref=src, dst_ref=dst, send_sem=send, recv_sem=recv,
        device_id={"tensor": peer}, device_id_type=pl.DeviceIdType.MESH,
    )


def greet(peers):
    barrier = pltpu.get_barrier_semaphore()
    for peer in peers:
        pl.semaphore_signal(barrier, inc=1, device_id={"tensor": peer}, device_id_type=pl.DeviceIdType.MESH)
    pl.semaphore_wait(barrier, len(peers))


def main_kernel(rows_ref, rot_ref, slab_ref, out_ref, rot_z, rot_x, rot_y, start, first, mid, second, third, landed, send_0, recv_0, send_e, recv_e, send_1, recv_1, send_2, recv_2, send_3, recv_3, send_4, recv_4, send_w, recv_w, own_w, tokens, slab, part, far, near, part2, far2, near2, last, swapped, send, recv, send_y, recv_y):
    me, z, x, y = place()
    spot = x * 2 + y
    own = pltpu.make_async_copy(slab_ref.at[:, pl.ds(pl.multiple_of(y * 4096, 4096), 4096)], slab.at[pl.ds(pl.multiple_of(y * 256, 256), 256)], own_w)
    own.start()
    partner = z * 8 + x * 2 + 1 - y
    greet([((z + step) % 4) * 8 + spot for step in range(1, 4)] + [z * 8 + (spot + step) % 8 for step in range(1, 8)])

    def gather(slot, source, target, peer):
        return remote(source, target, send_e.at[slot], recv_e.at[slot], peer)

    gathers_z = [gather(step - 1, rot_ref.at[pl.ds(4, 2)], rot_z.at[:, z], ((z + step) % 4) * 8 + spot) for step in (1, 3, 2)]
    gathers_x = [gather(2 + step, rot_ref.at[pl.ds(2, 2)], rot_x.at[:, x], z * 8 + ((x + step) % 4) * 2 + y) for step in (1, 3, 2)]
    gather_y = gather(6, rot_ref.at[pl.ds(0, 2)], rot_y.at[:, y], z * 8 + x * 2 + 1 - y)
    for copy in gathers_z:
        copy.start()

    def piece_of(other, group):
        at = pl.multiple_of(group * 2048 + other * 256, 256)
        return rows_ref.at[:, pl.ds(at, 256)]

    for step in range(1, 8):
        other = (spot + step) % 8
        for group in range(4):
            remote(piece_of(other, group), start.at[spot, :, pl.ds(group * 256, 256)], send_0.at[step], recv_0.at[spot], z * 8 + other).start()
    gather_y.start()

    columns = [(0, 1024), (2048, 512), (2560, 512), (1024, 1024), (3072, 1024)]
    rest = []
    for slot, (first_col, width) in enumerate(columns):
        source = slab_ref.at[:, pl.ds(pl.multiple_of((1 - y) * 4096 + first_col, 512), width)]
        target = slab.at[pl.ds(pl.multiple_of(y * 256, 256), 256), pl.ds(first_col, width)]
        rest.append(remote(source, target, send_w.at[slot], recv_w.at[slot], partner))
    rest[0].start()
    rest[1].start()
    for group in range(4):
        start[spot, :, group * 256:(group + 1) * 256] = rows_ref[:, pl.ds(pl.multiple_of(group * 2048 + spot * 256, 256), 256)]
    rot_z[:, z] = rot_ref[4:6]
    rot_x[:, x] = rot_ref[2:4]
    rot_y[:, y] = rot_ref[0:2]
    for step in range(1, 8):
        other = (spot + step) % 8
        remote(start.at[spot], start.at[other], send_0.at[step], recv_0.at[other], me).wait_recv()
    for copy in gathers_z:
        copy.wait_recv()
    for copy in gathers_x:
        copy.start()
    value = jnp.concatenate([start[other] for other in range(8)], axis=0)
    value = halves_dot(value, lambda k: rot_z[1, k // 2, k % 2], 3)
    value = halves_dot(value, lambda k: rot_z[0, k // 2, k % 2], 2)
    for piece in range(4):
        first[piece] = value[:, piece * 256:(piece + 1) * 256]

    over_z = [remote(first.at[(z + step) % 4], mid.at[z], send_1.at[step], recv_1.at[z], ((z + step) % 4) * 8 + spot) for step in (1, 3, 2)]
    for copy in over_z:
        copy.start()
    mid[z] = first[z]

    def onward(group):
        return remote(mid.at[group], second.at[x], send_2.at[group], recv_2.at[x], z * 8 + group * 2 + y)

    for step in (0, 3, 1, 2):
        group = (z + step) % 4
        if step != 0:
            remote(first.at[0], mid.at[group], send_1.at[step], recv_1.at[group], me).wait_recv()

        @pl.when(group != x)
        def _():
            onward(group).start()

        @pl.when(group == x)
        def _():
            second[x] = mid[group]

    for step in (1, 3, 2):
        source = (x + step) % 4
        remote(mid.at[0], second.at[source], send_2.at[0], recv_2.at[source], me).wait_recv()
    for copy in gathers_x:
        copy.wait_recv()
    value = jnp.concatenate([second[piece] for piece in range(4)], axis=1)
    value = halves_dot(value, lambda k: rot_x[1, k // 2, k % 2], 3)
    value = halves_dot(value, lambda k: rot_x[0, k // 2, k % 2], 2)
    for piece in range(4):
        third[piece] = value[:, piece * 256:(piece + 1) * 256]

    over_x = [remote(third.at[(x + step) % 4], landed.at[y, x], send_3.at[step], recv_3.at[x], z * 8 + ((x + step) % 4) * 2 + y) for step in (1, 3, 2)]
    for copy in over_x:
        copy.start()
    landed[y, x] = third[x]

    def across(group):
        return remote(landed.at[y, group], landed.at[y, group], send_4.at[group], recv_4.at[group], z * 8 + x * 2 + 1 - y)

    for step in (0, 3, 1, 2):
        group = (x + step) % 4
        if step != 0:
            remote(third.at[0], landed.at[y, group], send_3.at[step], recv_3.at[group], me).wait_recv()
        across(group).start()
    for copy in rest[2:]:
        copy.start()
    gather_y.wait_recv()
    for step in (0, 3, 1, 2):
        group = (x + step) % 4
        remote(landed.at[y, group], landed.at[1 - y, group], send_4.at[group], recv_4.at[group], me).wait_recv()
        value = jnp.concatenate([landed[0, group], landed[1, group]], axis=1)
        value = halves_dot(value, lambda k: rot_y[1, k // 2, k % 2], 2)
        value = halves_dot(value, lambda k: rot_y[0, k // 2, k % 2], 0)
        tokens[group] = value
    own.wait()

    coords = (z, x)

    def peer(axis, step):
        if axis == 0:
            return ((z + step) % 4) * 8 + spot
        return z * 8 + ((x + step) % 4) * 2 + y

    def compute(color, sub, role):
        block = (coords[color] + role) % 4
        if color == 0:
            left = tokens[block]
        else:
            left = jnp.concatenate([tokens[group, pl.ds(pl.multiple_of(block * 64, 64), 64), :] for group in range(4)], axis=0)

        def tile(half, carry):
            at = pl.multiple_of(color * 2048 + sub * 1024 + half * 512, 512)
            part[color, sub, role, half] = jnp.dot(left, slab[:, pl.ds(at, 512)], preferred_element_type=jnp.float32).astype(jnp.bfloat16)
            return carry

        lax.fori_loop(0, 2, tile, 0)

    pending = []

    def ship(stage, color, sub, slot, source, target, step):
        axis = color if stage == 0 else 1 - color
        copy = remote(source, target, send.at[stage, color, sub, slot], recv.at[stage, color, sub, slot], peer(axis, step))
        copy.start()
        pending.append(copy)
        return copy

    stages = ((part, far, near), (part2, far2, near2))
    fars, nears = {}, {}

    def start_far(stage, color, sub):
        block, far_buf, _ = stages[stage]
        fars[stage, color, sub] = (
            ship(stage, color, sub, 0, block.at[color, sub, 2, 0], far_buf.at[color, sub, 0], 1),
            ship(stage, color, sub, 1, block.at[color, sub, 2, 1], far_buf.at[color, sub, 1], 3),
        )

    def start_plain(stage, color, sub):
        block, _, near_buf = stages[stage]
        nears[stage, color, sub] = [
            ship(stage, color, sub, 2, block.at[color, sub, 1, 1], near_buf.at[color, sub, 0, 1], 1),
            ship(stage, color, sub, 3, block.at[color, sub, 3, 0], near_buf.at[color, sub, 1, 0], 3),
        ]

    def add(a, b):
        return (a.astype(jnp.float32) + b.astype(jnp.float32)).astype(jnp.bfloat16)

    def relay(stage, color, sub):
        block, far_buf, near_buf = stages[stage]
        fars[stage, color, sub][0].wait_recv()
        block[color, sub, 1, 0] = add(block[color, sub, 1, 0], far_buf[color, sub, 0])
        up = ship(stage, color, sub, 4, block.at[color, sub, 1, 0], near_buf.at[color, sub, 0, 0], 1)
        fars[stage, color, sub][1].wait_recv()
        block[color, sub, 3, 1] = add(block[color, sub, 3, 1], far_buf[color, sub, 1])
        down = ship(stage, color, sub, 5, block.at[color, sub, 3, 1], near_buf.at[color, sub, 1, 1], 3)
        nears[stage, color, sub] += [up, down]

    def second_stage(color, sub):
        for copy in nears[0, color, sub]:
            copy.wait_recv()
        for role in (2, 1, 3, 0):
            at = pl.ds(pl.multiple_of((coords[1 - color] + role) % 4 * 64, 64), 64)
            for half in range(2):
                total = part[color, sub, 0, half, at, :].astype(jnp.float32)
                total = total + near[color, sub, 0, half, at, :].astype(jnp.float32) + near[color, sub, 1, half, at, :].astype(jnp.float32)
                part2[color, sub, role, half] = total.astype(jnp.bfloat16)
            if role == 2:
                start_far(1, color, sub)
        start_plain(1, color, sub)

    def finish(color, sub):
        for copy in nears[1, color, sub]:
            copy.wait_recv()
        for half in range(2):
            total = part2[color, sub, 0, half].astype(jnp.float32)
            total = total + near2[color, sub, 0, half].astype(jnp.float32) + near2[color, sub, 1, half].astype(jnp.float32)
            total = total.astype(jnp.bfloat16)
            last[sub, 0, color, :, half * 512:half * 512 + 512] = total[:32]
            last[sub, 1, color, :, half * 512:half * 512 + 512] = total[32:]

    def first_stage(sub):
        for color in range(2):
            for slot in ((0,), (1, 2))[color] if sub == 0 else ((3,), (4,))[color]:
                width = columns[slot][1]
                there = slab.at[pl.ds(pl.multiple_of((1 - y) * 256, 256), 256), pl.ds(columns[slot][0], width)]
                remote(there, there, send_w.at[slot], recv_w.at[slot], me).wait_recv()
            compute(color, sub, 2)
            start_far(0, color, sub)
        for color in range(2):
            compute(color, sub, 1)
            compute(color, sub, 3)
            start_plain(0, color, sub)
        for color in range(2):
            compute(color, sub, 0)

    swaps = [remote(last.at[sub, 1 - y], swapped.at[sub], send_y.at[sub], recv_y.at[sub], partner) for sub in range(2)]

    def swap_out(sub):
        swaps[sub].start()
        for color in range(2):
            at = pl.multiple_of(y * 4096 + color * 2048 + sub * 1024, 1024)
            out_ref[:, pl.ds(at, 1024)] = last[sub, y, color]

    def swap_in(sub):
        swaps[sub].wait_recv()
        for color in range(2):
            at = pl.multiple_of((1 - y) * 4096 + color * 2048 + sub * 1024, 1024)
            out_ref[:, pl.ds(at, 1024)] = swapped[sub, color]

    first_stage(0)
    for color in range(2):
        relay(0, color, 0)
    first_stage(1)
    for color in range(2):
        second_stage(color, 0)
    for color in range(2):
        relay(0, color, 1)
    for color in range(2):
        relay(1, color, 0)
    for color in range(2):
        finish(color, 0)
    swap_out(0)
    for color in range(2):
        second_stage(color, 1)
    for color in range(2):
        relay(1, color, 1)
    for color in range(2):
        finish(color, 1)
    swap_out(1)
    swap_in(0)
    swap_in(1)
    for copy in swaps + pending:
        copy.wait_send()
    for copy in gathers_z + gathers_x + [gather_y] + rest + over_z + over_x:
        copy.wait_send()
    for step in range(1, 8):
        remote(start.at[spot], start.at[spot], send_0.at[step], recv_0.at[spot], me).wait_send()
    for group in range(4):
        across(group).wait_send()

        @pl.when(group != x)
        def _():
            onward(group).wait_send()


def rotate_and_project(rows, rotations, slab):
    bf = jnp.bfloat16
    dma = pltpu.SemaphoreType.DMA
    return pl.pallas_call(
        main_kernel,
        out_shape=jax.ShapeDtypeStruct((32, 8192), bf),
        in_specs=[pl.BlockSpec(memory_space=pltpu.VMEM)] * 2 + [pl.BlockSpec(memory_space=pl.ANY)],
        out_specs=pl.BlockSpec(memory_space=pltpu.VMEM),
        scratch_shapes=[
            pltpu.VMEM((2, 4, 2, BLK, BLK), bf),
            pltpu.VMEM((2, 4, 2, BLK, BLK), bf),
            pltpu.VMEM((2, 2, 2, BLK, BLK), bf),
            pltpu.VMEM((8, 32, 1024), bf),
            pltpu.VMEM((4, 256, 256), bf),
            pltpu.VMEM((4, 256, 256), bf),
            pltpu.VMEM((4, 256, 256), bf),
            pltpu.VMEM((4, 256, 256), bf),
            pltpu.VMEM((2, 4, 256, 256), bf),
        ]
        + [dma((count,)) for count in (8, 8, 7, 7, 4, 4, 4, 4, 4, 4, 4, 4, 5, 5)]
        + [
            dma,
            pltpu.VMEM((4, 256, 512), bf),
            pltpu.VMEM((512, 4096), bf),
            pltpu.VMEM((2, 2, 4, 2, 256, 512), bf),
            pltpu.VMEM((2, 2, 2, 256, 512), bf),
            pltpu.VMEM((2, 2, 2, 2, 256, 512), bf),
            pltpu.VMEM((2, 2, 4, 2, 64, 512), bf),
            pltpu.VMEM((2, 2, 2, 64, 512), bf),
            pltpu.VMEM((2, 2, 2, 2, 64, 512), bf),
            pltpu.VMEM((2, 2, 2, 32, 1024), bf),
            pltpu.VMEM((2, 2, 32, 1024), bf),
            dma((2, 2, 2, 6)),
            dma((2, 2, 2, 6)),
            dma((2,)),
            dma((2,)),
        ],
        compiler_params=pltpu.CompilerParams(collective_id=1, has_side_effects=True, vmem_limit_bytes=60 * 2**20),
        cost_estimate=pl.CostEstimate(flops=2 * 1024 * 512 * 4096, bytes_accessed=10 * 2**20, transcendentals=0),
    )(rows, rotations, slab)


def shards(weight_slab, token_rows, skew_params, pairing):
    return rotate_and_project(token_rows, cayley_blocks(skew_params, pairing), weight_slab)


def solution(mesh):
    in_specs = (
        P(("layer", "tensor"), None),
        P(("layer", "tensor"), None),
        P("layer", "tensor", None, None),
        P("layer", None),
    )
    out_specs = P(("layer", "tensor"), None)
    return jax.shard_map(shards, mesh=mesh, in_specs=in_specs, out_specs=out_specs, check_vma=False)
```

time: 134 us -> 134 us (level)
  Pallas kernels: 129 us -> 132 us
  local copies, waits for them, and re-layouts: 3.24 us -> 1.87 us
  starting transfers between devices: 1.36 us -> 0 us
    pallas_call x3 -> x1, Pallas kernels: 112 us -> 117 us  [rotate_and_project(): pl.pallas_call(main_kernel, out_shape=jax.ShapeDtypeStruct((32, 8192), bf...]
    pallas_call x1, Pallas kernels: 17.6 us -> 15.1 us  [cayley_blocks(): pl.pallas_call(rotation_kernel, out_shape=jax.ShapeDtypeStruct((count, BL...]
    unnamed x5 -> x1, local copies, waits for them, and re-layouts: 3.24 us -> 1.87 us
    ppermute x1 -> x0, starting transfers between devices: 1.36 us -> none  [shards(): lax.ppermute(partner_half(weight_slab), 'tensor', [(d, d ^ 1) for d in ra...]
  transfers between devices with their start and end apart: 1 -> 0, of which waited for: 0 -> 0; matrix products, arithmetic and copies ran while one was open for 0% -> 0% of each run, Pallas kernels for 51% -> 0%
where the time goes in v6:
time: 134 us
  Pallas kernels  132 us (99%)
  local copies, waits for them, and re-layouts  1.87 us (1%)
    pallas_call x1, Pallas kernels, rotate_and_project(): pl.pallas_call(main_kernel, out_shape=jax.ShapeDtypeStruct((32, 8192), bf...  117 us
    pallas_call x1, Pallas kernels, cayley_blocks(): pl.pallas_call(rotation_kernel, out_shape=jax.ShapeDtypeStruct((count, BL...  15.1 us

profile of v6, /device:TPU:16, one launch (start us, length us, event | category | flops | bytes accessed | tf_op | source)
XLA Modules:
  0.0 134.2 jit_solution(340767812274655774)
XLA Ops:
  0.0 15.1 %shard_map.46 = bf16[12,128,128]{2,1,0:T(8,128)(2,1)} custom-call(f32[12,128,128]{2,1,0:T(8,128)} %bitcast.2, s32[6,128]{1,0:T(8,128)} %pairing_ref.1), custom_call_target="tpu_custom_call" | custom-call | flops 503316480 | bytes 1179648 | tf_op jit(solution)/shard_map/pallas_call | solution.py:101
  15.1 117.2 %shard_map.47 = bf16[32,8192]{1,0:T(8,128)(2,1)} custom-call(bf16[32,8192]{1,0:T(8,128)(2,1)} %rows_ref.1, bf16[6,2,128,128]{3,2,1,0:T(8,128)(2,1)} %bitcast.3, bf16[256,8192]{1,0:T(8,128)(2,1)} %slab_ref.1), custom_call_target="tpu_custom_call" | custom-call | flops 4294967296 | bytes 10485760 | tf_op jit(solution)/shard_map/pallas_call | solution.py:406
  132.3 1.9 %copy.6 = bf16[32,8192]{1,0:T(8,128)(2,1)} copy(bf16[32,8192]{1,0:T(8,128)(2,1)} %shard_map.47) | data formatting | bytes 1048576

commit v7 on v6

--- a/solution.py
+++ b/solution.py
@@ -142,13 +142,15 @@
     pl.semaphore_wait(barrier, len(peers))
 
 
-def main_kernel(rows_ref, rot_ref, slab_ref, out_ref, rot_z, rot_x, rot_y, start, first, mid, second, third, landed, send_0, recv_0, send_e, recv_e, send_1, recv_1, send_2, recv_2, send_3, recv_3, send_4, recv_4, send_w, recv_w, own_w, tokens, slab, part, far, near, part2, far2, near2, last, swapped, send, recv, send_y, recv_y):
+def main_kernel(rows_ref, rot_ref, slab_ref, early_ref, out_ref, rot_z, rot_x, rot_y, start, first, mid, second, third, landed, send_0, recv_0, send_e, recv_e, send_1, recv_1, send_2, recv_2, send_3, recv_3, send_4, recv_4, send_w, recv_w, own_w, tokens, slab, part, far, near, merged, final, send, recv, send_f, recv_f, early_w):
     me, z, x, y = place()
     spot = x * 2 + y
     own = pltpu.make_async_copy(slab_ref.at[:, pl.ds(pl.multiple_of(y * 4096, 4096), 4096)], slab.at[pl.ds(pl.multiple_of(y * 256, 256), 256)], own_w)
     own.start()
+    early = pltpu.make_async_copy(early_ref, slab.at[pl.ds(pl.multiple_of((1 - y) * 256, 256), 256), pl.ds(0, 1024)], early_w)
+    early.start()
     partner = z * 8 + x * 2 + 1 - y
-    greet([((z + step) % 4) * 8 + spot for step in range(1, 4)] + [z * 8 + (spot + step) % 8 for step in range(1, 8)])
+    greet([((z + step) % 4) * 8 + spot for step in range(1, 4)] + [z * 8 + (spot + step) % 8 for step in range(1, 8)] + [((z + step) % 4) * 8 + x * 2 + 1 - y for step in range(1, 4)])
 
     def gather(slot, source, target, peer):
         return remote(source, target, send_e.at[slot], recv_e.at[slot], peer)
@@ -169,14 +171,13 @@
             remote(piece_of(other, group), start.at[spot, :, pl.ds(group * 256, 256)], send_0.at[step], recv_0.at[spot], z * 8 + other).start()
     gather_y.start()
 
-    columns = [(0, 1024), (2048, 512), (2560, 512), (1024, 1024), (3072, 1024)]
+    columns = [(1024, 1024), (2048, 1024), (3072, 1024)]
     rest = []
     for slot, (first_col, width) in enumerate(columns):
         source = slab_ref.at[:, pl.ds(pl.multiple_of((1 - y) * 4096 + first_col, 512), width)]
         target = slab.at[pl.ds(pl.multiple_of(y * 256, 256), 256), pl.ds(first_col, width)]
         rest.append(remote(source, target, send_w.at[slot], recv_w.at[slot], partner))
     rest[0].start()
-    rest[1].start()
     for group in range(4):
         start[spot, :, group * 256:(group + 1) * 256] = rows_ref[:, pl.ds(pl.multiple_of(group * 2048 + spot * 256, 256), 256)]
     rot_z[:, z] = rot_ref[4:6]
@@ -240,7 +241,7 @@
         if step != 0:
             remote(third.at[0], landed.at[y, group], send_3.at[step], recv_3.at[group], me).wait_recv()
         across(group).start()
-    for copy in rest[2:]:
+    for copy in rest[1:]:
         copy.start()
     gather_y.wait_recv()
     for step in (0, 3, 1, 2):
@@ -251,6 +252,7 @@
         value = halves_dot(value, lambda k: rot_y[0, k // 2, k % 2], 0)
         tokens[group] = value
     own.wait()
+    early.wait()
 
     coords = (z, x)
 
@@ -267,7 +269,7 @@
             left = jnp.concatenate([tokens[group, pl.ds(pl.multiple_of(block * 64, 64), 64), :] for group in range(4)], axis=0)
 
         def tile(half, carry):
-            at = pl.multiple_of(color * 2048 + sub * 1024 + half * 512, 512)
+            at = pl.multiple_of(sub * 2048 + color * 1024 + half * 512, 512)
             part[color, sub, role, half] = jnp.dot(left, slab[:, pl.ds(at, 512)], preferred_element_type=jnp.float32).astype(jnp.bfloat16)
             return carry
 
@@ -275,118 +277,122 @@
 
     pending = []
 
-    def ship(stage, color, sub, slot, source, target, step):
-        axis = color if stage == 0 else 1 - color
-        copy = remote(source, target, send.at[stage, color, sub, slot], recv.at[stage, color, sub, slot], peer(axis, step))
+    def ship(color, sub, slot, source, target, step):
+        copy = remote(source, target, send.at[color, sub, slot], recv.at[color, sub, slot], peer(color, step))
         copy.start()
         pending.append(copy)
         return copy
 
-    stages = ((part, far, near), (part2, far2, near2))
     fars, nears = {}, {}
 
-    def start_far(stage, color, sub):
-        block, far_buf, _ = stages[stage]
-        fars[stage, color, sub] = (
-            ship(stage, color, sub, 0, block.at[color, sub, 2, 0], far_buf.at[color, sub, 0], 1),
-            ship(stage, color, sub, 1, block.at[color, sub, 2, 1], far_buf.at[color, sub, 1], 3),
+    def start_far(color, sub):
+        fars[color, sub] = (
+            ship(color, sub, 0, part.at[color, sub, 2, 0], far.at[color, sub, 0], 1),
+            ship(color, sub, 1, part.at[color, sub, 2, 1], far.at[color, sub, 1], 3),
         )
 
-    def start_plain(stage, color, sub):
-        block, _, near_buf = stages[stage]
-        nears[stage, color, sub] = [
-            ship(stage, color, sub, 2, block.at[color, sub, 1, 1], near_buf.at[color, sub, 0, 1], 1),
-            ship(stage, color, sub, 3, block.at[color, sub, 3, 0], near_buf.at[color, sub, 1, 0], 3),
+    def start_plain(color, sub):
+        nears[color, sub] = [
+            ship(color, sub, 2, part.at[color, sub, 1, 1], near.at[color, sub, 0, 1], 1),
+            ship(color, sub, 3, part.at[color, sub, 3, 0], near.at[color, sub, 1, 0], 3),
         ]
 
     def add(a, b):
         return (a.astype(jnp.float32) + b.astype(jnp.float32)).astype(jnp.bfloat16)
 
-    def relay(stage, color, sub):
-        block, far_buf, near_buf = stages[stage]
-        fars[stage, color, sub][0].wait_recv()
-        block[color, sub, 1, 0] = add(block[color, sub, 1, 0], far_buf[color, sub, 0])
-        up = ship(stage, color, sub, 4, block.at[color, sub, 1, 0], near_buf.at[color, sub, 0, 0], 1)
-        fars[stage, color, sub][1].wait_recv()
-        block[color, sub, 3, 1] = add(block[color, sub, 3, 1], far_buf[color, sub, 1])
-        down = ship(stage, color, sub, 5, block.at[color, sub, 3, 1], near_buf.at[color, sub, 1, 1], 3)
-        nears[stage, color, sub] += [up, down]
+    def relay(color, sub):
+        fars[color, sub][0].wait_recv()
+        part[color, sub, 1, 0] = add(part[color, sub, 1, 0], far[color, sub, 0])
+        up = ship(color, sub, 4, part.at[color, sub, 1, 0], near.at[color, sub, 0, 0], 1)
+        fars[color, sub][1].wait_recv()
+        part[color, sub, 3, 1] = add(part[color, sub, 3, 1], far[color, sub, 1])
+        down = ship(color, sub, 5, part.at[color, sub, 3, 1], near.at[color, sub, 1, 1], 3)
+        nears[color, sub] += [up, down]
+
+    def owner(color, step, cross):
+        side = 1 - y if cross else y
+        if color == 0:
+            return z * 8 + ((x + step) % 4) * 2 + side
+        return ((z + step) % 4) * 8 + x * 2 + side
 
     def second_stage(color, sub):
-        for copy in nears[0, color, sub]:
+        for copy in nears[color, sub]:
             copy.wait_recv()
-        for role in (2, 1, 3, 0):
-            at = pl.ds(pl.multiple_of((coords[1 - color] + role) % 4 * 64, 64), 64)
+        here = coords[1 - color]
+        for step in (2, 1, 3, 0):
+            there = (here + step) % 4
+            at = pl.ds(pl.multiple_of(there * 64, 64), 64)
             for half in range(2):
                 total = part[color, sub, 0, half, at, :].astype(jnp.float32)
                 total = total + near[color, sub, 0, half, at, :].astype(jnp.float32) + near[color, sub, 1, half, at, :].astype(jnp.float32)
-                part2[color, sub, role, half] = total.astype(jnp.bfloat16)
-            if role == 2:
-                start_far(1, color, sub)
-        start_plain(1, color, sub)
+                total = total.astype(jnp.bfloat16)
+                merged[color, sub, step, 0, :, half * 512:half * 512 + 512] = total[:32]
+                merged[color, sub, step, 1, :, half * 512:half * 512 + 512] = total[32:]
+            for cross in (1, 0):
+                if step != 0 or cross == 1:
+                    side = 1 - y if cross else y
+                    slot = step * 2 + cross
+                    copy = remote(merged.at[color, sub, step, side], final.at[color, sub, slot], send_f.at[color, sub, slot], recv_f.at[color, sub, slot], owner(color, step, cross))
+                    copy.start()
+                    pending.append(copy)
 
     def finish(color, sub):
-        for copy in nears[1, color, sub]:
-            copy.wait_recv()
-        for half in range(2):
-            total = part2[color, sub, 0, half].astype(jnp.float32)
-            total = total + near2[color, sub, 0, half].astype(jnp.float32) + near2[color, sub, 1, half].astype(jnp.float32)
-            total = total.astype(jnp.bfloat16)
-            last[sub, 0, color, :, half * 512:half * 512 + 512] = total[:32]
-            last[sub, 1, color, :, half * 512:half * 512 + 512] = total[32:]
-
-    def first_stage(sub):
-        for color in range(2):
-            for slot in ((0,), (1, 2))[color] if sub == 0 else ((3,), (4,))[color]:
-                width = columns[slot][1]
-                there = slab.at[pl.ds(pl.multiple_of((1 - y) * 256, 256), 256), pl.ds(columns[slot][0], width)]
-                remote(there, there, send_w.at[slot], recv_w.at[slot], me).wait_recv()
-            compute(color, sub, 2)
-            start_far(0, color, sub)
-        for color in range(2):
-            compute(color, sub, 1)
-            compute(color, sub, 3)
-            start_plain(0, color, sub)
-        for color in range(2):
-            compute(color, sub, 0)
-
-    swaps = [remote(last.at[sub, 1 - y], swapped.at[sub], send_y.at[sub], recv_y.at[sub], partner) for sub in range(2)]
-
-    def swap_out(sub):
-        swaps[sub].start()
-        for color in range(2):
-            at = pl.multiple_of(y * 4096 + color * 2048 + sub * 1024, 1024)
-            out_ref[:, pl.ds(at, 1024)] = last[sub, y, color]
-
-    def swap_in(sub):
-        swaps[sub].wait_recv()
-        for color in range(2):
-            at = pl.multiple_of((1 - y) * 4096 + color * 2048 + sub * 1024, 1024)
-            out_ref[:, pl.ds(at, 1024)] = swapped[sub, color]
-
-    first_stage(0)
-    for color in range(2):
-        relay(0, color, 0)
-    first_stage(1)
+        for cross in (0, 1):
+            total = jnp.zeros((32, 1024), jnp.float32)
+            if cross == 0:
+                total = merged[color, sub, 0, y].astype(jnp.float32)
+            for step in (0, 1, 3, 2):
+                slot = step * 2 + cross
+                if slot != 0:
+                    landing = final.at[color, sub, slot]
+                    remote(landing, landing, send_f.at[color, sub, slot], recv_f.at[color, sub, slot], me).wait_recv()
+                    total = total + final[color, sub, slot].astype(jnp.float32)
+            side = 1 - y if cross else y
+            at = pl.multiple_of(side * 4096 + sub * 2048 + color * 1024, 1024)
+            out_ref[:, pl.ds(at, 1024)] = total.astype(jnp.bfloat16)
+
+    def arrived(slot):
+        there = slab.at[pl.ds(pl.multiple_of((1 - y) * 256, 256), 256), pl.ds(columns[slot][0], columns[slot][1])]
+        remote(there, there, send_w.at[slot], recv_w.at[slot], me).wait_recv()
+
+    compute(0, 0, 2)
+    start_far(0, 0)
+    arrived(0)
+    compute(1, 0, 2)
+    start_far(1, 0)
+    for color in range(2):
+        compute(color, 0, 1)
+        compute(color, 0, 3)
+        start_plain(color, 0)
+    for color in range(2):
+        compute(color, 0, 0)
+    for color in range(2):
+        relay(color, 0)
+    arrived(1)
+    compute(0, 1, 2)
+    start_far(0, 1)
+    compute(0, 1, 1)
+    compute(0, 1, 3)
+    start_plain(0, 1)
+    compute(0, 1, 0)
+    arrived(2)
+    compute(1, 1, 2)
+    start_far(1, 1)
+    compute(1, 1, 1)
+    compute(1, 1, 3)
+    start_plain(1, 1)
+    compute(1, 1, 0)
     for color in range(2):
         second_stage(color, 0)
     for color in range(2):
-        relay(0, color, 1)
-    for color in range(2):
-        relay(1, color, 0)
+        relay(color, 1)
     for color in range(2):
         finish(color, 0)
-    swap_out(0)
     for color in range(2):
         second_stage(color, 1)
     for color in range(2):
-        relay(1, color, 1)
-    for color in range(2):
         finish(color, 1)
-    swap_out(1)
-    swap_in(0)
-    swap_in(1)
-    for copy in swaps + pending:
+    for copy in pending:
         copy.wait_send()
     for copy in gathers_z + gathers_x + [gather_y] + rest + over_z + over_x:
         copy.wait_send()
@@ -400,13 +406,13 @@
             onward(group).wait_send()
 
 
-def rotate_and_project(rows, rotations, slab):
+def rotate_and_project(rows, rotations, slab, early):
     bf = jnp.bfloat16
     dma = pltpu.SemaphoreType.DMA
     return pl.pallas_call(
         main_kernel,
         out_shape=jax.ShapeDtypeStruct((32, 8192), bf),
-        in_specs=[pl.BlockSpec(memory_space=pltpu.VMEM)] * 2 + [pl.BlockSpec(memory_space=pl.ANY)],
+        in_specs=[pl.BlockSpec(memory_space=pltpu.VMEM)] * 2 + [pl.BlockSpec(memory_space=pl.ANY)] * 2,
         out_specs=pl.BlockSpec(memory_space=pltpu.VMEM),
         scratch_shapes=[
             pltpu.VMEM((2, 4, 2, BLK, BLK), bf),
@@ -419,7 +425,7 @@
             pltpu.VMEM((4, 256, 256), bf),
             pltpu.VMEM((2, 4, 256, 256), bf),
         ]
-        + [dma((count,)) for count in (8, 8, 7, 7, 4, 4, 4, 4, 4, 4, 4, 4, 5, 5)]
+        + [dma((count,)) for count in (8, 8, 7, 7, 4, 4, 4, 4, 4, 4, 4, 4, 3, 3)]
         + [
             dma,
             pltpu.VMEM((4, 256, 512), bf),
@@ -427,23 +433,41 @@
             pltpu.VMEM((2, 2, 4, 2, 256, 512), bf),
             pltpu.VMEM((2, 2, 2, 256, 512), bf),
             pltpu.VMEM((2, 2, 2, 2, 256, 512), bf),
-            pltpu.VMEM((2, 2, 4, 2, 64, 512), bf),
-            pltpu.VMEM((2, 2, 2, 64, 512), bf),
-            pltpu.VMEM((2, 2, 2, 2, 64, 512), bf),
-            pltpu.VMEM((2, 2, 2, 32, 1024), bf),
-            pltpu.VMEM((2, 2, 32, 1024), bf),
-            dma((2, 2, 2, 6)),
-            dma((2, 2, 2, 6)),
-            dma((2,)),
-            dma((2,)),
+            pltpu.VMEM((2, 2, 4, 2, 32, 1024), bf),
+            pltpu.VMEM((2, 2, 8, 32, 1024), bf),
+            dma((2, 2, 6)),
+            dma((2, 2, 6)),
+            dma((2, 2, 8)),
+            dma((2, 2, 8)),
+            dma,
         ],
-        compiler_params=pltpu.CompilerParams(collective_id=1, has_side_effects=True, vmem_limit_bytes=60 * 2**20),
+        compiler_params=pltpu.CompilerParams(collective_id=1, has_side_effects=True, vmem_limit_bytes=52 * 2**20),
         cost_estimate=pl.CostEstimate(flops=2 * 1024 * 512 * 4096, bytes_accessed=10 * 2**20, transcendentals=0),
-    )(rows, rotations, slab)
+    )(rows, rotations, slab, early)
+
+
+def half_kernel(slab_ref, out_ref, done):
+    side = lax.axis_index("tensor") % 2
+    at = pl.multiple_of((1 - side) * 4096, 4096)
+    copy = pltpu.make_async_copy(slab_ref.at[:, pl.ds(at, 1024)], out_ref, done)
+    copy.start()
+    copy.wait()
+
+
+def partner_columns(slab):
+    return pl.pallas_call(
+        half_kernel,
+        out_shape=jax.ShapeDtypeStruct((256, 1024), jnp.bfloat16),
+        in_specs=[pl.BlockSpec(memory_space=pl.ANY)],
+        out_specs=pl.BlockSpec(memory_space=pltpu.VMEM),
+        scratch_shapes=[pltpu.SemaphoreType.DMA],
+        cost_estimate=pl.CostEstimate(flops=0, bytes_accessed=4 * 2**20, transcendentals=0),
+    )(slab)
 
 
 def shards(weight_slab, token_rows, skew_params, pairing):
-    return rotate_and_project(token_rows, cayley_blocks(skew_params, pairing), weight_slab)
+    early = lax.ppermute(partner_columns(weight_slab), "tensor", [(d, d ^ 1) for d in range(32)])
+    return rotate_and_project(token_rows, cayley_blocks(skew_params, pairing), weight_slab, early)
 
 
 def solution(mesh):

time: 134 us -> 125 us (0.933)
  Pallas kernels: 132 us -> 121 us
  starting transfers between devices: 0 us -> 1.36 us
    pallas_call x1, Pallas kernels: 117 us -> 102 us  [rotate_and_project(): pl.pallas_call(main_kernel, out_shape=jax.ShapeDtypeStruct((32, 8192), bf...]
    pallas_call x1, Pallas kernels: 15.1 us -> 17.6 us  [cayley_blocks(): pl.pallas_call(rotation_kernel, out_shape=jax.ShapeDtypeStruct((count, BL...]
    pallas_call x0 -> x1, Pallas kernels: none -> 1.9 us  [partner_columns(): pl.pallas_call(half_kernel, out_shape=jax.ShapeDtypeStruct((256, 1024), j...]
    ppermute x0 -> x1, starting transfers between devices: none -> 1.36 us  [shards(): lax.ppermute(partner_columns(weight_slab), 'tensor', [(d, d ^ 1) for d in...]
  transfers between devices with their start and end apart: 0 -> 1, of which waited for: 0 -> 0; matrix products, arithmetic and copies ran while one was open for 0% -> 0% of each run, Pallas kernels for 0% -> 14%
where the time goes in v7:
time: 125 us; the launch traced here: 124 us
  Pallas kernels  121 us (97%)
  local copies, waits for them, and re-layouts  1.79 us (1%)
  starting transfers between devices  1.36 us (1%)
    pallas_call x1, Pallas kernels, rotate_and_project(): pl.pallas_call(main_kernel, out_shape=jax.ShapeDtypeStruct((32, 8192), bf...  102 us
    pallas_call x1, Pallas kernels, cayley_blocks(): pl.pallas_call(rotation_kernel, out_shape=jax.ShapeDtypeStruct((count, BL...  17.6 us
  transfers between devices with their start and end apart: 1, of which 0 were waited for; matrix products, arithmetic and copies ran while one was open for 0% of the time, Pallas kernels for 14%

profile of v7, /device:TPU:16, one launch (start us, length us, event | category | flops | bytes accessed | tf_op | source)
XLA Modules:
  0.0 124.3 jit_solution(120348166247226317)
XLA Ops:
  0.0 0.0 copy-start
  0.0 1.9 %shard_map.47 = bf16[256,1024]{1,0:T(8,128)(2,1)} custom-call(bf16[256,8192]{1,0:T(8,128)(2,1)} %slab_ref.3), custom_call_target="tpu_custom_call" | custom-call | bytes 4194304 | tf_op jit(solution)/shard_map/pallas_call | solution.py:458
  1.9 1.4 %collective-permute-start = (bf16[256,1024]{1,0:T(8,128)(2,1)}, bf16[256,1024]{1,0:T(8,128)(2,1)S(1)}, u32[]{:S(2)}, u32[]{:S(2)}) collective-permute-start(bf16[256,1024]{1,0:T(8,128)(2,1)} %shard_map.47), channel_id=1, source_target_pairs={{0,1},{1,0},{2,3},{3,2},{4,5},{5,4},{6,7},{7,6},{8,9},{9,8},{10,11... | collective-permute-start | bytes 1572872 | tf_op jit(solution)/shard_map/ppermute | solution.py:469
  3.3 17.6 %shard_map.46 = bf16[12,128,128]{2,1,0:T(8,128)(2,1)} custom-call(f32[12,128,128]{2,1,0:T(8,128)} %bitcast.3, s32[6,128]{1,0:T(8,128)} %pairing_ref.1), custom_call_target="tpu_custom_call" | custom-call | flops 503316480 | bytes 1179648 | tf_op jit(solution)/shard_map/pallas_call | solution.py:101
  20.9 0.0 collective-permute-done.early_ref
  20.9 0.0 copy-done
  20.9 0.0 copy-start.1
  20.9 1.0 copy-done.1
  21.9 101.6 %shard_map.48 = bf16[32,8192]{1,0:T(8,128)(2,1)S(1)} custom-call(bf16[32,8192]{1,0:T(8,128)(2,1)S(1)} %copy-done, bf16[6,2,128,128]{3,2,1,0:T(8,128)(2,1)S(1)} %bitcast.2, bf16[256,8192]{1,0:T(8,128)(2,1)} %slab_ref.3, bf16[256,1024]{1,0:T(8,128)(2,1)S(1)} %collective-permute-done.early_ref), custom_call_target="tpu_custom_call" | custom-call | flops 4294967296 | bytes 10485760 | tf_op jit(solution)/shard_map/pallas_call | solution.py:412
  123.5 0.8 copy.6
Async XLA Ops:
  0.0 20.9 %copy-start = (bf16[32,8192]{1,0:T(8,128)(2,1)S(1)}, bf16[32,8192]{1,0:T(8,128)(2,1)}, u32[]{:S(2)}) copy-start(bf16[32,8192]{1,0:T(8,128)(2,1)} %rows_ref.1) | copy-start | bytes 1572868
  1.9 19.0 %collective-permute-start = (bf16[256,1024]{1,0:T(8,128)(2,1)}, bf16[256,1024]{1,0:T(8,128)(2,1)S(1)}, u32[]{:S(2)}, u32[]{:S(2)}) collective-permute-start(bf16[256,1024]{1,0:T(8,128)(2,1)} %shard_map.47), channel_id=1, source_target_pairs={{0,1},{1,0},{2,3},{3,2},{4,5},{5,4},{6,7},{7,6},{8,9},{9,8},{10,11... | collective-permute-start | bytes 1572872 | tf_op jit(solution)/shard_map/ppermute | solution.py:469
  20.9 1.0 copy-start.1

commit v8 on v7

--- a/solution.py
+++ b/solution.py
@@ -27,19 +27,35 @@
 
 
 def as_left(high, low):
-    return jnp.concatenate([high, high, low], axis=1)
+    return jnp.concatenate([high, low], axis=1)
 
 
 def as_right(high, low):
-    return jnp.concatenate([high, low, high], axis=0)
+    row = jnp.concatenate([high, low], axis=1)
+    return jnp.concatenate([row, row], axis=0)
 
 
 def wide_dot(left, right):
     return jnp.dot(left, right, preferred_element_type=jnp.float32)
 
 
+def folded_dot(left, right):
+    both = wide_dot(left, right)
+    return both[:, :BLK] + both[:, BLK:]
+
+
+def split_three(value):
+    high = value.astype(jnp.bfloat16)
+    left_over = value - high.astype(jnp.float32)
+    middle = left_over.astype(jnp.bfloat16)
+    return high, middle, (left_over - middle.astype(jnp.float32)).astype(jnp.bfloat16)
+
+
 def full_dot(left, right):
-    return jnp.dot(left, right, precision=lax.Precision.HIGHEST, preferred_element_type=jnp.float32)
+    left_hi, left_mid, left_lo = split_three(left)
+    right_hi, right_mid, right_lo = split_three(right)
+    small = wide_dot(as_left(left_hi, left_lo), jnp.concatenate([right_lo, right_hi], axis=0))
+    return folded_dot(as_left(left_hi, left_mid), as_right(right_hi, right_mid)) + small
 
 
 def rotation_kernel(skew_ref, pairing_ref, out_ref, gram, gram_left, guess):
@@ -71,8 +87,8 @@
         scale = 2.0 / (2.0 - spread * spread)
         for block in range(count):
             high, low = split(guess[block])
-            left = 2.0 * identity - wide_dot(gram_left[block], as_right(high, low))
-            guess[block] = scale * wide_dot(as_left(high, low), as_right(*split(left)))
+            left = 2.0 * identity - folded_dot(gram_left[block], as_right(high, low))
+            guess[block] = scale * folded_dot(as_left(high, low), as_right(*split(left)))
         return shrunk
 
     lax.while_loop(more, improve, (top - 1.0) / (top + 1.0))
@@ -83,8 +99,8 @@
             raised = identity + raw - raw.T
             now = guess[block]
             miss = identity - full_dot(gram[block], now)
-            now = now + wide_dot(as_left(*split(now)), as_right(*split(miss)))
-            rotation = 2.0 * wide_dot(as_left(*split(now)), as_right(*split(raised))) - identity
+            now = now + folded_dot(as_left(*split(now)), as_right(*split(miss)))
+            rotation = 2.0 * folded_dot(as_left(*split(now)), as_right(*split(raised))) - identity
             turned.append(rotation.astype(jnp.bfloat16))
         order = pairing_ref[pl.ds(section, 1), :]
         chosen = (rows == order).astype(jnp.float32)
@@ -105,9 +121,10 @@
         out_specs=pl.BlockSpec(memory_space=pltpu.VMEM),
         scratch_shapes=[
             pltpu.VMEM((count, BLK, BLK), jnp.float32),
-            pltpu.VMEM((count, BLK, 3 * BLK), jnp.bfloat16),
+            pltpu.VMEM((count, BLK, 2 * BLK), jnp.bfloat16),
             pltpu.VMEM((count, BLK, BLK), jnp.float32),
         ],
+        compiler_params=pltpu.CompilerParams(vmem_limit_bytes=16 * 2**20),
         cost_estimate=pl.CostEstimate(flops=count * BLK**3 * 20, bytes_accessed=count * BLK * BLK * 6, transcendentals=0),
     )(skew_params.reshape(count, BLK, BLK), pairing)
     return out.reshape(sections, owned, BLK, BLK)
@@ -147,7 +164,7 @@
     spot = x * 2 + y
     own = pltpu.make_async_copy(slab_ref.at[:, pl.ds(pl.multiple_of(y * 4096, 4096), 4096)], slab.at[pl.ds(pl.multiple_of(y * 256, 256), 256)], own_w)
     own.start()
-    early = pltpu.make_async_copy(early_ref, slab.at[pl.ds(pl.multiple_of((1 - y) * 256, 256), 256), pl.ds(0, 1024)], early_w)
+    early = pltpu.make_async_copy(early_ref, slab.at[pl.ds(pl.multiple_of((1 - y) * 256, 256), 256), pl.ds(0, 768)], early_w)
     early.start()
     partner = z * 8 + x * 2 + 1 - y
     greet([((z + step) % 4) * 8 + spot for step in range(1, 4)] + [z * 8 + (spot + step) % 8 for step in range(1, 8)] + [((z + step) % 4) * 8 + x * 2 + 1 - y for step in range(1, 4)])
@@ -171,10 +188,10 @@
             remote(piece_of(other, group), start.at[spot, :, pl.ds(group * 256, 256)], send_0.at[step], recv_0.at[spot], z * 8 + other).start()
     gather_y.start()
 
-    columns = [(1024, 1024), (2048, 1024), (3072, 1024)]
+    columns = [(768, 1280), (2048, 1024), (3072, 1024)]
     rest = []
     for slot, (first_col, width) in enumerate(columns):
-        source = slab_ref.at[:, pl.ds(pl.multiple_of((1 - y) * 4096 + first_col, 512), width)]
+        source = slab_ref.at[:, pl.ds(pl.multiple_of((1 - y) * 4096 + first_col, 256), width)]
         target = slab.at[pl.ds(pl.multiple_of(y * 256, 256), 256), pl.ds(first_col, width)]
         rest.append(remote(source, target, send_w.at[slot], recv_w.at[slot], partner))
     rest[0].start()
@@ -355,9 +372,9 @@
         there = slab.at[pl.ds(pl.multiple_of((1 - y) * 256, 256), 256), pl.ds(columns[slot][0], columns[slot][1])]
         remote(there, there, send_w.at[slot], recv_w.at[slot], me).wait_recv()
 
+    arrived(0)
     compute(0, 0, 2)
     start_far(0, 0)
-    arrived(0)
     compute(1, 0, 2)
     start_far(1, 0)
     for color in range(2):
@@ -446,27 +463,10 @@
     )(rows, rotations, slab, early)
 
 
-def half_kernel(slab_ref, out_ref, done):
+def shards(weight_slab, token_rows, skew_params, pairing):
     side = lax.axis_index("tensor") % 2
-    at = pl.multiple_of((1 - side) * 4096, 4096)
-    copy = pltpu.make_async_copy(slab_ref.at[:, pl.ds(at, 1024)], out_ref, done)
-    copy.start()
-    copy.wait()
-
-
-def partner_columns(slab):
-    return pl.pallas_call(
-        half_kernel,
-        out_shape=jax.ShapeDtypeStruct((256, 1024), jnp.bfloat16),
-        in_specs=[pl.BlockSpec(memory_space=pl.ANY)],
-        out_specs=pl.BlockSpec(memory_space=pltpu.VMEM),
-        scratch_shapes=[pltpu.SemaphoreType.DMA],
-        cost_estimate=pl.CostEstimate(flops=0, bytes_accessed=4 * 2**20, transcendentals=0),
-    )(slab)
-
-
-def shards(weight_slab, token_rows, skew_params, pairing):
-    early = lax.ppermute(partner_columns(weight_slab), "tensor", [(d, d ^ 1) for d in range(32)])
+    outgoing = lax.dynamic_slice_in_dim(weight_slab, (1 - side) * 4096, 768, 1)
+    early = lax.ppermute(outgoing, "tensor", [(d, d ^ 1) for d in range(32)])
     return rotate_and_project(token_rows, cayley_blocks(skew_params, pairing), weight_slab, early)
 
 

time: 125 us -> 119 us (0.952)
  the two profiles are of different devices: /device:TPU:16 before, /device:TPU:6 now
where the time goes in v8:
time: 119 us; the launch traced here: 118 us
  Pallas kernels  112 us (94%)
  local copies, waits for them, and re-layouts  4.67 us (4%)
  starting transfers between devices  1.66 us (1%)
    pallas_call x1, Pallas kernels, rotate_and_project(): pl.pallas_call(main_kernel, out_shape=jax.ShapeDtypeStruct((32, 8192), bf...  101 us
    pallas_call x1, Pallas kernels, cayley_blocks(): pl.pallas_call(rotation_kernel, out_shape=jax.ShapeDtypeStruct((count, BL...  10.8 us
    unnamed x7, local copies, waits for them, and re-layouts  3.65 us
  transfers between devices with their start and end apart: 1, of which 0 were waited for; matrix products, arithmetic and copies ran while one was open for 0% of the time, Pallas kernels for 9%

profile of v8, /device:TPU:6, one launch (start us, length us, event | category | flops | bytes accessed | tf_op | source)
XLA Modules:
  0.0 118.3 jit_solution(7991833181544243947)
XLA Ops:
  0.0 1.0 constant_dynamic-slice_fusion
  1.0 1.7 %collective-permute-start = (bf16[256,768]{1,0:T(8,128)(2,1)S(1)}, bf16[256,768]{1,0:T(8,128)(2,1)S(1)}, u32[]{:S(2)}, u32[]{:S(2)}) collective-permute-start(bf16[256,768]{1,0:T(8,128)(2,1)S(1)} %constant_dynamic-slice_fusion), channel_id=1, source_target_pairs={{0,1},{1,0},{2,3},{3,2},{4,5},{5,4},{6,7},{7,6},{8,9},{9,8},{10,11... | collective-permute-start | bytes 1179656 | tf_op jit(solution)/shard_map/ppermute | solution.py:469
  2.7 0.0 copy-start
  2.7 1.1 copy-done
  3.8 0.0 copy-start.2
  3.8 0.7 copy-done.2
  4.5 10.8 %shard_map.46 = bf16[12,128,128]{2,1,0:T(8,128)(2,1)S(1)} custom-call(f32[12,128,128]{2,1,0:T(8,128)S(1)} %bitcast.2, s32[6,128]{1,0:T(8,128)S(1)} %copy-done.2), custom_call_target="tpu_custom_call" | custom-call | flops 503316480 | bytes 1179648 | tf_op jit(solution)/shard_map/pallas_call | solution.py:117
  15.3 0.0 collective-permute-done.early_ref
  15.3 0.0 copy-start.1
  15.3 1.0 copy-done.1
  16.3 101.2 %shard_map.47 = bf16[32,8192]{1,0:T(8,128)(2,1)S(1)} custom-call(bf16[32,8192]{1,0:T(8,128)(2,1)S(1)} %copy-done.1, bf16[6,2,128,128]{3,2,1,0:T(8,128)(2,1)S(1)} %bitcast.3, bf16[256,8192]{1,0:T(8,128)(2,1)} %slab_ref.1, bf16[256,768]{1,0:T(8,128)(2,1)S(1)} %collective-permute-done.early_ref), custom_call_target="tpu_custom_call" | custom-call | flops 4294967296 | bytes 10485760 | tf_op jit(solution)/shard_map/pallas_call | solution.py:429
  117.5 0.8 copy.6
Async XLA Ops:
  1.0 14.2 %collective-permute-start = (bf16[256,768]{1,0:T(8,128)(2,1)S(1)}, bf16[256,768]{1,0:T(8,128)(2,1)S(1)}, u32[]{:S(2)}, u32[]{:S(2)}) collective-permute-start(bf16[256,768]{1,0:T(8,128)(2,1)S(1)} %constant_dynamic-slice_fusion), channel_id=1, source_target_pairs={{0,1},{1,0},{2,3},{3,2},{4,5},{5,4},{6,7},{7,6},{8,9},{9,8},{10,11... | collective-permute-start | bytes 1179656 | tf_op jit(solution)/shard_map/ppermute | solution.py:469
  2.7 1.1 copy-start
  3.8 0.7 copy-start.2
  15.3 1.0 copy-start.1

commit v9 on v8

--- a/solution.py
+++ b/solution.py
@@ -164,7 +164,7 @@
     spot = x * 2 + y
     own = pltpu.make_async_copy(slab_ref.at[:, pl.ds(pl.multiple_of(y * 4096, 4096), 4096)], slab.at[pl.ds(pl.multiple_of(y * 256, 256), 256)], own_w)
     own.start()
-    early = pltpu.make_async_copy(early_ref, slab.at[pl.ds(pl.multiple_of((1 - y) * 256, 256), 256), pl.ds(0, 768)], early_w)
+    early = pltpu.make_async_copy(early_ref, slab.at[pl.ds(pl.multiple_of((1 - y) * 256, 256), 256), pl.ds(0, 1024)], early_w)
     early.start()
     partner = z * 8 + x * 2 + 1 - y
     greet([((z + step) % 4) * 8 + spot for step in range(1, 4)] + [z * 8 + (spot + step) % 8 for step in range(1, 8)] + [((z + step) % 4) * 8 + x * 2 + 1 - y for step in range(1, 4)])
@@ -188,7 +188,7 @@
             remote(piece_of(other, group), start.at[spot, :, pl.ds(group * 256, 256)], send_0.at[step], recv_0.at[spot], z * 8 + other).start()
     gather_y.start()
 
-    columns = [(768, 1280), (2048, 1024), (3072, 1024)]
+    columns = [(1024, 1024), (2048, 1024), (3072, 1024)]
     rest = []
     for slot, (first_col, width) in enumerate(columns):
         source = slab_ref.at[:, pl.ds(pl.multiple_of((1 - y) * 4096 + first_col, 256), width)]
@@ -372,9 +372,9 @@
         there = slab.at[pl.ds(pl.multiple_of((1 - y) * 256, 256), 256), pl.ds(columns[slot][0], columns[slot][1])]
         remote(there, there, send_w.at[slot], recv_w.at[slot], me).wait_recv()
 
-    arrived(0)
     compute(0, 0, 2)
     start_far(0, 0)
+    arrived(0)
     compute(1, 0, 2)
     start_far(1, 0)
     for color in range(2):
@@ -400,15 +400,13 @@
     start_plain(1, 1)
     compute(1, 1, 0)
     for color in range(2):
-        second_stage(color, 0)
-    for color in range(2):
         relay(color, 1)
-    for color in range(2):
-        finish(color, 0)
-    for color in range(2):
-        second_stage(color, 1)
-    for color in range(2):
-        finish(color, 1)
+    for sub in range(2):
+        for color in range(2):
+            second_stage(color, sub)
+    for sub in range(2):
+        for color in range(2):
+            finish(color, sub)
     for copy in pending:
         copy.wait_send()
     for copy in gathers_z + gathers_x + [gather_y] + rest + over_z + over_x:
@@ -465,7 +463,7 @@
 
 def shards(weight_slab, token_rows, skew_params, pairing):
     side = lax.axis_index("tensor") % 2
-    outgoing = lax.dynamic_slice_in_dim(weight_slab, (1 - side) * 4096, 768, 1)
+    outgoing = lax.dynamic_slice_in_dim(weight_slab, (1 - side) * 4096, 1024, 1)
     early = lax.ppermute(outgoing, "tensor", [(d, d ^ 1) for d in range(32)])
     return rotate_and_project(token_rows, cayley_blocks(skew_params, pairing), weight_slab, early)
 

time: 119 us -> 117 us (0.983)
  the two profiles are of different devices: /device:TPU:6 before, /device:TPU:16 now
where the time goes in v9:
time: 117 us
  Pallas kernels  111 us (95%)
  local copies, waits for them, and re-layouts  4.73 us (4%)
  starting transfers between devices  1.36 us (1%)
    pallas_call x1, Pallas kernels, rotate_and_project(): pl.pallas_call(main_kernel, out_shape=jax.ShapeDtypeStruct((32, 8192), bf...  100 us
    pallas_call x1, Pallas kernels, cayley_blocks(): pl.pallas_call(rotation_kernel, out_shape=jax.ShapeDtypeStruct((count, BL...  10.8 us
    unnamed x7, local copies, waits for them, and re-layouts  3.65 us
  transfers between devices with their start and end apart: 1, of which 0 were waited for; matrix products, arithmetic and copies ran while one was open for 0% of the time, Pallas kernels for 9%

profile of v9, /device:TPU:16, one launch (start us, length us, event | category | flops | bytes accessed | tf_op | source)
XLA Modules:
  0.0 116.8 jit_solution(13447999083892701080)
XLA Ops:
  0.0 1.1 constant_dynamic-slice_fusion
  1.1 1.4 %collective-permute-start = (bf16[256,1024]{1,0:T(8,128)(2,1)S(1)}, bf16[256,1024]{1,0:T(8,128)(2,1)S(1)}, u32[]{:S(2)}, u32[]{:S(2)}) collective-permute-start(bf16[256,1024]{1,0:T(8,128)(2,1)S(1)} %constant_dynamic-slice_fusion), channel_id=1, source_target_pairs={{0,1},{1,0},{2,3},{3,2},{4,5},{5,4},{6,7},{7,6},{8,9},{9,8},{10,11... | collective-permute-start | bytes 1572872 | tf_op jit(solution)/shard_map/ppermute | solution.py:467
  2.4 0.0 copy-start
  2.4 1.1 copy-done
  3.6 0.0 copy-start.2
  3.6 0.7 copy-done.2
  4.3 10.8 %shard_map.46 = bf16[12,128,128]{2,1,0:T(8,128)(2,1)S(1)} custom-call(f32[12,128,128]{2,1,0:T(8,128)S(1)} %bitcast.2, s32[6,128]{1,0:T(8,128)S(1)} %copy-done.2), custom_call_target="tpu_custom_call" | custom-call | flops 503316480 | bytes 1179648 | tf_op jit(solution)/shard_map/pallas_call | solution.py:117
  15.0 0.0 collective-permute-done.early_ref
  15.0 0.0 copy-start.1
  15.0 1.0 copy-done.1
  16.1 100.0 %shard_map.47 = bf16[32,8192]{1,0:T(8,128)(2,1)S(1)} custom-call(bf16[32,8192]{1,0:T(8,128)(2,1)S(1)} %copy-done.1, bf16[6,2,128,128]{3,2,1,0:T(8,128)(2,1)S(1)} %bitcast.3, bf16[256,8192]{1,0:T(8,128)(2,1)} %slab_ref.1, bf16[256,1024]{1,0:T(8,128)(2,1)S(1)} %collective-permute-done.early_ref), custom_call_target="tpu_custom_call" | custom-call | flops 4294967296 | bytes 10485760 | tf_op jit(solution)/shard_map/pallas_call | solution.py:427
  116.0 0.8 copy.6
Async XLA Ops:
  1.1 13.9 %collective-permute-start = (bf16[256,1024]{1,0:T(8,128)(2,1)S(1)}, bf16[256,1024]{1,0:T(8,128)(2,1)S(1)}, u32[]{:S(2)}, u32[]{:S(2)}) collective-permute-start(bf16[256,1024]{1,0:T(8,128)(2,1)S(1)} %constant_dynamic-slice_fusion), channel_id=1, source_target_pairs={{0,1},{1,0},{2,3},{3,2},{4,5},{5,4},{6,7},{7,6},{8,9},{9,8},{10,11... | collective-permute-start | bytes 1572872 | tf_op jit(solution)/shard_map/ppermute | solution.py:467
  2.4 1.1 copy-start
  3.6 0.7 copy-start.2
  15.0 1.0 copy-start.1

commit v10 on v9

--- a/solution.py
+++ b/solution.py
@@ -186,7 +186,8 @@
         other = (spot + step) % 8
         for group in range(4):
             remote(piece_of(other, group), start.at[spot, :, pl.ds(group * 256, 256)], send_0.at[step], recv_0.at[spot], z * 8 + other).start()
-    gather_y.start()
+    for copy in gathers_x + [gather_y]:
+        copy.start()
 
     columns = [(1024, 1024), (2048, 1024), (3072, 1024)]
     rest = []
@@ -205,8 +206,6 @@
         remote(start.at[spot], start.at[other], send_0.at[step], recv_0.at[other], me).wait_recv()
     for copy in gathers_z:
         copy.wait_recv()
-    for copy in gathers_x:
-        copy.start()
     value = jnp.concatenate([start[other] for other in range(8)], axis=0)
     value = halves_dot(value, lambda k: rot_z[1, k // 2, k % 2], 3)
     value = halves_dot(value, lambda k: rot_z[0, k // 2, k % 2], 2)

time: 117 us -> 116 us (level); the launches traced: 117 us -> 114 us
  Pallas kernels: 111 us -> 108 us
    pallas_call x1, Pallas kernels: 100 us -> 97.6 us  [rotate_and_project(): pl.pallas_call(main_kernel, out_shape=jax.ShapeDtypeStruct((32, 8192), bf...]
  transfers between devices with their start and end apart: 1 -> 1, of which waited for: 0 -> 1; matrix products, arithmetic and copies ran while one was open for 0% -> 0% of each run, Pallas kernels for 9% -> 9%
where the time goes in v10:
time: 116 us; the launch traced here: 114 us
  Pallas kernels  108 us (93%)
  local copies, waits for them, and re-layouts  4.73 us (4%)
  starting transfers between devices  1.36 us (1%)
    pallas_call x1, Pallas kernels, rotate_and_project(): pl.pallas_call(main_kernel, out_shape=jax.ShapeDtypeStruct((32, 8192), bf...  97.6 us
    pallas_call x1, Pallas kernels, cayley_blocks(): pl.pallas_call(rotation_kernel, out_shape=jax.ShapeDtypeStruct((count, BL...  10 us
    unnamed x7, local copies, waits for them, and re-layouts  3.66 us
  transfers between devices with their start and end apart: 1, of which 1 were waited for; matrix products, arithmetic and copies ran while one was open for 0% of the time, Pallas kernels for 9%

profile of v10, /device:TPU:16, one launch (start us, length us, event | category | flops | bytes accessed | tf_op | source)
XLA Modules:
  0.0 114.3 jit_solution(6171340841497694020)
XLA Ops:
  0.0 1.1 constant_dynamic-slice_fusion
  1.1 1.4 %collective-permute-start = (bf16[256,1024]{1,0:T(8,128)(2,1)S(1)}, bf16[256,1024]{1,0:T(8,128)(2,1)S(1)}, u32[]{:S(2)}, u32[]{:S(2)}) collective-permute-start(bf16[256,1024]{1,0:T(8,128)(2,1)S(1)} %constant_dynamic-slice_fusion), channel_id=1, source_target_pairs={{0,1},{1,0},{2,3},{3,2},{4,5},{5,4},{6,7},{7,6},{8,9},{9,8},{10,11... | collective-permute-start | bytes 1572872 | tf_op jit(solution)/shard_map/ppermute | solution.py:466
  2.4 0.0 copy-start
  2.4 1.1 copy-done
  3.6 0.0 copy-start.2
  3.6 0.7 copy-done.2
  4.3 10.0 %shard_map.46 = bf16[12,128,128]{2,1,0:T(8,128)(2,1)S(1)} custom-call(f32[12,128,128]{2,1,0:T(8,128)S(1)} %bitcast.2, s32[6,128]{1,0:T(8,128)S(1)} %copy-done.2), custom_call_target="tpu_custom_call" | custom-call | flops 503316480 | bytes 1179648 | tf_op jit(solution)/shard_map/pallas_call | solution.py:117
  14.3 0.5 collective-permute-done.early_ref
  14.8 0.0 copy-start.1
  14.8 1.0 copy-done.1
  15.9 97.6 %shard_map.47 = bf16[32,8192]{1,0:T(8,128)(2,1)S(1)} custom-call(bf16[32,8192]{1,0:T(8,128)(2,1)S(1)} %copy-done.1, bf16[6,2,128,128]{3,2,1,0:T(8,128)(2,1)S(1)} %bitcast.3, bf16[256,8192]{1,0:T(8,128)(2,1)} %slab_ref.1, bf16[256,1024]{1,0:T(8,128)(2,1)S(1)} %collective-permute-done.early_ref), custom_call_target="tpu_custom_call" | custom-call | flops 4294967296 | bytes 10485760 | tf_op jit(solution)/shard_map/pallas_call | solution.py:426
  113.5 0.8 copy.6
Async XLA Ops:
  1.1 13.7 %collective-permute-start = (bf16[256,1024]{1,0:T(8,128)(2,1)S(1)}, bf16[256,1024]{1,0:T(8,128)(2,1)S(1)}, u32[]{:S(2)}, u32[]{:S(2)}) collective-permute-start(bf16[256,1024]{1,0:T(8,128)(2,1)S(1)} %constant_dynamic-slice_fusion), channel_id=1, source_target_pairs={{0,1},{1,0},{2,3},{3,2},{4,5},{5,4},{6,7},{7,6},{8,9},{9,8},{10,11... | collective-permute-start | bytes 1572872 | tf_op jit(solution)/shard_map/ppermute | solution.py:466
  2.4 1.1 copy-start
  3.6 0.7 copy-start.2
  14.8 1.0 copy-start.1
